TPU v7x, 32 devices: a whole 2x2x4 slice. The times are simulated.
32 devices in a mesh: node: 4 (over y, x), rows: 8 (over z, core).
Axes of the slice: x: 2, y: 2, z: 4, core: 2. Of those that a mesh axis runs over, the one named last changes fastest.
Arguments:
- subspace: bfloat16 [6144, 256], P('rows'), may hold values from -6 to 6
- inverse: bfloat16 [4, 2, 6144, 768], P('node', None, 'rows')
- weights: float32 [4, 2], P('node'), may hold values from 0.25 to 1
- diag_tiles: float32 [6144, 128], P('rows'), may hold values from -0.5 to 0.5
- upper_tiles: float32 [6144, 128], P('rows'), may hold values from -0.5 to 0.5
Outputs:
- subspace_out: float32 [6144, 256], P('rows')
- projected: float32 [2, 256, 256], replicated
All inputs are finite; a program needn't handle non-finite values.
Results may differ from a plain program's by a relative error of at most 0.0025.
Values may be sent and summed in bfloat16 or wider, within the bound.
No kernel may reach another device: no remote copies, remote signals or barrier semaphores. Data moves between devices by JAX's collectives and lax.ppermute only.
A program may use at most 64 MiB of HBM per device.

v0:
```python
import functools

import jax
import jax.numpy as jnp
from jax import lax
from jax.experimental import pallas as pl
from jax.experimental.pallas import tpu as pltpu
from jax.sharding import PartitionSpec as P


ITERS = 2
GROUP = 8
GRANT = 16 * 2**20

precise = lax.Precision.HIGHEST
F32 = jnp.float32
BF16 = jnp.bfloat16


def dot(left, right):
    return jnp.dot(left, right, precision=precise, preferred_element_type=F32)


def dot_tn(left, right):
    dims = (((0,), (0,)), ((), ()))
    return lax.dot_general(left, right, dims, precision=precise, preferred_element_type=F32)


def halves_of(value):
    high = value.astype(BF16)
    return high, (value - high.astype(F32)).astype(BF16)


def dot_three(left, right, dims=(((1,), (0,)), ((), ()))):
    times = lambda a, b: lax.dot_general(a, b, dims, preferred_element_type=F32)
    (a, b), (c, d) = halves_of(left), halves_of(right)
    return times(a, c) + (times(a, d) + times(b, c))


def dot_two(left, right, dims=(((1,), (0,)), ((), ()))):
    times = lambda a, b: lax.dot_general(a, b, dims, preferred_element_type=F32)
    c, d = halves_of(right)
    return times(left, c) + times(left, d)


NT = (((1,), (1,)), ((), ()))
TN = (((0,), (0,)), ((), ()))


def like(shape, dtype=F32):
    return pltpu.VMEM(shape, dtype)


def halves_of(value):
    high = value.astype(BF16)
    return high, (value - high.astype(F32)).astype(BF16)


def dot_three(left, right, dims=(((1,), (0,)), ((), ()))):
    times = lambda a, b: lax.dot_general(a, b, dims, preferred_element_type=F32)
    (a, b), (c, d) = halves_of(left), halves_of(right)
    return times(a, c) + (times(a, d) + times(b, c))


def dot_two(left, right, dims=(((1,), (0,)), ((), ()))):
    times = lambda a, b: lax.dot_general(a, b, dims, preferred_element_type=F32)
    c, d = halves_of(right)
    return times(left, c) + times(left, d)


NT = (((1,), (1,)), ((), ()))
TN = (((0,), (0,)), ((), ()))


def local(value):
    return pltpu.with_memory_space_constraint(value, pltpu.VMEM)


def whole(kernel, out_shape, *operands, scratch=(), flops=10**8):
    size = sum(x.size * x.dtype.itemsize for x in operands)
    vmem = pl.BlockSpec(memory_space=pltpu.VMEM)
    return pl.pallas_call(
        kernel,
        out_shape=out_shape,
        in_specs=[vmem for _ in operands],
        out_specs=jax.tree.map(lambda _: vmem, out_shape),
        scratch_shapes=list(scratch),
        cost_estimate=pl.CostEstimate(flops=flops, bytes_accessed=size, transcendentals=0),
        compiler_params=pltpu.CompilerParams(vmem_limit_bytes=GRANT),
    )(*[local(x) for x in operands])


def node_swap(block, step):
    count = lax.axis_size("node")
    return lax.ppermute(block, "node", [(i, i ^ step) for i in range(count)])


def core_swap(block):
    count = lax.axis_size("rows")
    return lax.ppermute(block, "rows", [(i, i ^ 1) for i in range(count)])


def link_swap(block):
    count = lax.axis_size("rows")
    pairs = [(i, i + 1) for i in range(1, count - 1, 2)]
    return lax.ppermute(block, "rows", pairs + [(b, a) for a, b in pairs])


def node_spread(blocks):
    return [node_swap(block, step + 1) for step, block in enumerate(blocks)]


def tree_sum(blocks):
    while len(blocks) > 1:
        odd = blocks[len(blocks) // 2 * 2 :]
        blocks = [a + b for a, b in zip(blocks[::2], blocks[1::2])] + odd
    return blocks[0]


def chip_sum(block):
    count = lax.axis_size("rows")
    chips = count // 2
    if chips <= 4:
        steps = range(1, chips)
        routes = [[(i, i ^ (2 * s)) for i in range(count)] for s in steps]
        return tree_sum([block] + [lax.ppermute(block, "rows", route) for route in routes])
    step = 2
    while step < count:
        block = block + lax.ppermute(block, "rows", [(i, i ^ step) for i in range(count)])
        step *= 2
    return block


def combine(weights, real, imag):
    return weights[:, 0:1] * real - weights[:, 1:2] * imag


def emit_messages(vectors, top, bottom, coupling, out_a, out_b):
    is_even = lax.rem(lax.axis_index("rows"), 2) == 0
    times = lambda block: jnp.dot(block, vectors, preferred_element_type=F32)
    both = lambda rows: jnp.concatenate([times(rows[0]), times(rows[1])], 1).astype(BF16)
    first, last = both(top), both(bottom)
    last = dot_tn(coupling, last.astype(F32)).astype(BF16)
    out_a[...] = jnp.where(is_even, last, first)
    out_b[...] = jnp.where(is_even, first, last)


def start_kernel(source, vectors_at, upper_at, *refs):
    out_a, out_b, coupling, vectors, ends, arrived = refs
    rows = vectors.shape[0]
    band = coupling.shape[0]
    half = rows // 2
    pairs = [(vectors_at.at[pl.ds(at, half)], vectors.at[pl.ds(at, half)]) for at in (0, half)]
    for end, at in ((0, 0), (1, rows - band)):
        pairs += [(source.at[0, c, pl.ds(at, band)], ends.at[end, c]) for c in range(2)]
    pairs.append((upper_at.at[pl.ds(rows - band, band)], coupling))
    copies = [pltpu.make_async_copy(*pair, arrived.at[i]) for i, pair in enumerate(pairs)]
    for copy in copies:
        copy.start()
    for copy in copies:
        copy.wait()
    emit_messages(vectors[...], ends.at[0], ends.at[1], coupling[...], out_a, out_b)


def from_hbm(kernel, outs, scratch, copies, *operands):
    far = lambda x: pltpu.with_memory_space_constraint(x, pltpu.HBM)
    kinds = [pltpu.HBM if is_far else pltpu.VMEM for _, is_far in operands]
    return pl.pallas_call(
        kernel,
        in_specs=[pl.BlockSpec(memory_space=kind) for kind in kinds],
        out_specs=[pl.BlockSpec(memory_space=pltpu.VMEM)] * len(outs),
        out_shape=outs,
        scratch_shapes=scratch + [pltpu.SemaphoreType.DMA((copies,))],
        cost_estimate=pl.CostEstimate(flops=10**8, bytes_accessed=10**6, transcendentals=0),
        compiler_params=pltpu.CompilerParams(vmem_limit_bytes=GRANT),
    )(*[far(x) if is_far else local(x) for x, is_far in operands])


def start(vectors, upper_tiles, inverse):
    rows, columns = vectors.shape
    band = upper_tiles.shape[1]
    message = like((band, 2 * columns), BF16)
    outs = [message, message, like((band, band)), like(vectors.shape, BF16)]
    scratch = [pltpu.VMEM((2, 2, band, rows), BF16)]
    operands = [(inverse, True), (vectors, True), (upper_tiles, True)]
    return from_hbm(start_kernel, outs, scratch, 7, *operands)


def tile_of(rows, band):
    return 2 * band if rows % (2 * band) == 0 else band


def edge_of(weights, got, coupling, rows, on_chip, factor=None):
    columns = got.shape[1] // 2
    band = coupling.shape[0]
    is_even = lax.rem(lax.axis_index("rows"), 2) == 0
    is_next = is_even if on_chip else jnp.logical_not(is_even)
    if factor is None:
        below = dot(coupling[...], got[...].astype(F32)).astype(BF16)
        edge = jnp.where(is_next, below, got[...]).astype(F32)
    else:
        turned = jnp.concatenate([got[:, :columns], got[:, columns:]], 0)
        turned = dot_three(turned, factor, NT)
        edge = jnp.concatenate([turned[:band], turned[band:]], 1)
        edge = jnp.where(is_next, dot_three(coupling[...], edge), edge)
    real, imag = edge[:, :columns], edge[:, columns:]
    at = pl.multiple_of(jnp.where(is_next, rows - band, 0), band)
    under = weights[:, 0:1] * imag + weights[:, 1:2] * real
    return at, jnp.concatenate([combine(weights, real, imag), -under], 0)


def edge_terms(edges, inverse, span, band):
    left = [inverse[0, c, span, pl.ds(at, band)] for at, _ in edges for c in range(2)]
    high, rest = halves_of(jnp.concatenate([edge for _, edge in edges], 0))
    left = jnp.concatenate(left, 1)
    times = lambda right: jnp.dot(left, right, preferred_element_type=F32)
    return times(high) + times(rest)


def products(weights, vectors, inverse, span):
    real = jnp.dot(inverse[0, 0, span], vectors[...], preferred_element_type=F32)
    imag = jnp.dot(inverse[0, 1, span], vectors[...], preferred_element_type=F32)
    return combine(weights, real, imag)


def start_base_kernel(weights_at, source, vectors, coupling, got, base, inverse, weights, arrived):
    rows = vectors.shape[0]
    tile = tile_of(rows, coupling.shape[0])
    spans = [pl.ds(at, tile) for at in range(0, rows, tile)]
    pairs = [(weights_at, weights)]
    pairs += [(source.at[:, :, span], inverse.at[:, :, span]) for span in spans]
    copies = [pltpu.make_async_copy(*pair, arrived.at[i]) for i, pair in enumerate(pairs)]
    for copy in copies:
        copy.start()
    copies[0].wait()
    band = coupling.shape[0]
    edges = [edge_of(weights, got, coupling, rows, True)]
    for copy, span in zip(copies[1:], spans):
        copy.wait()
        term = products(weights, vectors, inverse, span)
        base[span] = term + edge_terms(edges, inverse, span, band)


def start_base(weights, inverse, vectors, coupling, got):
    rows, columns = vectors.shape
    outs = [like((rows, columns)), like(inverse.shape, BF16), like(weights.shape)]
    operands = [(weights, True), (inverse, True), (vectors, False), (coupling, False), (got, False)]
    return from_hbm(start_base_kernel, outs, [], rows // coupling.shape[0] + 1, *operands)


def refined(field, low, factor):
    high, rest = halves_of(factor)
    times = lambda a, b: lax.dot_general(a, b, NT, preferred_element_type=F32)
    return times(field, high) + (times(field, rest) + times(low, high))


def tips_kernel(field, low, coupling, inverse, out_a, out_b):
    band = coupling.shape[0]
    is_even = lax.rem(lax.axis_index("rows"), 2) == 0

    def both(at):
        times = lambda part, x: jnp.dot(
            inverse[0, part, at : at + band], x, preferred_element_type=F32
        )
        of = lambda part: times(part, field[...]) + times(part, low[...])
        return jnp.concatenate([of(0), of(1)], 1)

    first = both(0)
    last = dot_tn(coupling[...], both(field.shape[0] - band))
    out_a[...] = jnp.where(is_even, last, first)
    out_b[...] = jnp.where(is_even, first, last)


def tips(field, low, coupling, inverse):
    message = like((coupling.shape[0], 2 * field.shape[1]))
    return whole(tips_kernel, [message, message], field, low, coupling, inverse)


def emit_term(term, own, sends):
    node = lax.axis_index("node")
    size = own.shape[0]
    steps = lax.axis_size("node")
    for s, out in enumerate((own,) + sends):
        where = pl.multiple_of((node ^ (s if s < steps else s - steps + 1)) * size, 8)
        value = term[pl.ds(where, size), :]
        if s >= steps:
            value = value - value.astype(BF16).astype(F32)
        out[...] = value.astype(out.dtype)


def solve_kernel(weights, field, low, factor, coupling, inverse, got_a, got_b, own, *refs):
    sends, (current, term) = refs[:-2], refs[-2:]
    current[...] = refined(field[...], low[...], factor[...]).astype(BF16)
    rows = field.shape[0]
    band = coupling.shape[0]
    tile = tile_of(rows, band)
    edges = [
        edge_of(weights, got, coupling, rows, on_chip, factor[...])
        for got, on_chip in ((got_a, True), (got_b, False))
    ]
    for at in range(0, rows, tile):
        span = pl.ds(at, tile)
        part = products(weights, current, inverse, span)
        term[span] = part + edge_terms(edges, inverse, span, band)
    emit_term(term, own, sends)


def blocks_of(rows, columns, parts):
    count = lax.axis_size("node")
    size = rows // count
    return [like((size, columns))] + [like((size, columns), BF16)] * (parts * (count - 1))


def solve(weights, field, low, factor, coupling, inverse, got_a, got_b, parts):
    rows, columns = field.shape
    return whole(
        solve_kernel,
        blocks_of(rows, columns, parts),
        weights,
        field,
        low,
        factor,
        coupling,
        inverse,
        got_a,
        got_b,
        scratch=[pltpu.VMEM((rows, columns), BF16), pltpu.VMEM((rows, columns), F32)],
    )


def correct_kernel(weights, base, got, coupling, inverse, own, *refs):
    sends, term = refs[:-1], refs[-1]
    rows = base.shape[0]
    band = coupling.shape[0]
    tile = tile_of(rows, band)
    edges = [edge_of(weights, got, coupling, rows, False)]
    for at in range(0, rows, tile):
        span = pl.ds(at, tile)
        term[span] = base[span] + edge_terms(edges, inverse, span, band)
    emit_term(term, own, sends)


def correct(weights, base, got, coupling, inverse, parts):
    rows, columns = base.shape
    outs = blocks_of(rows, columns, parts)
    scratch = [pltpu.VMEM((rows, columns), F32)]
    return whole(correct_kernel, outs, weights, base, got, coupling, inverse, scratch=scratch)


def place(blocks, out):
    node = lax.axis_index("node")
    size = blocks[0].shape[0]
    for step, block in enumerate(blocks):
        out[pl.ds(pl.multiple_of((node ^ step) * size, 8), size), :] = block[...]


def gram_kernel(*refs):
    *blocks, field, head, part, matrix = refs
    place(blocks, field)
    head[...] = field[: head.shape[0]]
    matrix[...] = lax.dot_general(field[...], field[...], TN, preferred_element_type=F32)
    size = part.shape[0]
    part[...] = matrix[pl.ds(pl.multiple_of(lax.axis_index("node") * size, 8), size), :]


def gram_slice(blocks, band):
    rows, columns = blocks[0].shape
    count = len(blocks)
    outs = [
        like((rows * count, columns), BF16),
        like((band, columns), BF16),
        like((columns // count, columns)),
    ]
    scratch = [pltpu.VMEM((columns, columns), F32)]
    return whole(gram_kernel, outs, *blocks, scratch=scratch)


def join_kernel(*refs):
    place(refs[:-1], refs[-1])


def join(blocks):
    rows, columns = blocks[0].shape
    return whole(join_kernel, like((rows * len(blocks), columns), BF16), *blocks)


def eliminate(block, out, base, spread):
    count = block.shape[0]
    full = (GROUP, count)
    lane = lax.broadcasted_iota(jnp.int32, full, 1)
    span = range(GROUP)
    tiles = [block[t * GROUP : (t + 1) * GROUP] for t in range(count // GROUP)]
    room = GROUP * (GROUP + 1)
    for t in range(len(tiles)):
        k = t * GROUP
        tile = tiles[t]
        slot = (t % 2) * room
        spread[slot : slot + GROUP] = tile
        for j in span:
            at = slot + GROUP * (j + 1)
            spread[at : at + GROUP] = jnp.broadcast_to(tile[:, k + j : k + j + 1], full)
        across = lambda row: spread[pl.ds(slot + row, GROUP, stride=0), :]
        rows = [across(i) for i in span]
        pivot = [[across(GROUP * (j + 1) + i) for j in range(i + 1)] for i in span]
        low = [[None] * GROUP for _ in span]
        inverse = [None] * GROUP
        pivots = [None] * GROUP
        for j in range(0, GROUP, 2):
            lead, side = pivot[j][j], pivot[j + 1][j]
            determinant = lead * pivot[j + 1][j + 1] - side * side
            inverse[j] = 1.0 / lead
            inverse[j + 1] = lead * (1.0 / determinant)
            pivots[j] = lead
            pivots[j + 1] = determinant * inverse[j]
            low[j + 1][j] = side * inverse[j]
            second = [None] * GROUP
            for i in range(j + 2, GROUP):
                low[i][j] = pivot[i][j] * inverse[j]
                second[i] = pivot[i][j + 1] - low[i][j] * side
                low[i][j + 1] = second[i] * inverse[j + 1]
            for i in range(j + 2, GROUP):
                for m in range(j + 2, i + 1):
                    pivot[i][m] = pivot[i][m] - low[i][j] * pivot[m][j] - low[i][j + 1] * second[m]
        inv = [[None] * GROUP for _ in span]
        for j in span:
            for i in range(j + 1, GROUP):
                total = low[i][j]
                for m in range(j + 1, i):
                    total = total + low[i][m] * inv[m][j]
                inv[i][j] = -total
        inside = (lane >= k) & (lane < k + GROUP)
        rows = [jnp.where(inside, jnp.where(lane == k + i, 1.0, 0.0), rows[i]) for i in span]
        done = []
        for i in span:
            total = rows[i]
            for j in range(i):
                total = total + inv[i][j] * rows[j]
            done.append(total)
            at = base + k + i
            row = jnp.where(lane < k + GROUP, total * lax.rsqrt(pivots[i]), 0.0)
            out[at : at + 1, base : base + count] = row[:1]
        if t + 1 < len(tiles):
            scaled = [done[i] * inverse[i] for i in span]
            back = []
            for j in span:
                total = scaled[j]
                for i in range(j + 1, GROUP):
                    total = total + inv[i][j] * scaled[i]
                back.append(total)
            for u in range(t + 1, len(tiles)):
                old = tiles[u]
                new = jnp.where(inside, 0.0, old)
                for j in span:
                    new = new - old[:, k + j : k + j + 1] * back[j]
                tiles[u] = new


def first_factor_kernel(order, *refs):
    *blocks, top, corner, rest, across, matrix, spread = refs
    place(blocks, matrix)
    count = matrix.shape[0]
    half = count // 2
    values = matrix[...] * (1.0 / order)
    eye = lax.broadcasted_iota(jnp.int32, (count, count), 0) == lax.broadcasted_iota(
        jnp.int32, (count, count), 1
    )
    diagonal = jnp.where(eye, values, 0.0)
    scale = lax.rsqrt(jnp.sum(diagonal, 0, keepdims=True))
    down = lax.rsqrt(jnp.sum(diagonal, 1, keepdims=True))
    across[...] = scale
    values = values * scale * down
    eliminate(values[:half, :half], top, 0, spread)
    beside = dot(top[...], values[:half, half:])
    corner[...] = dot_tn(beside, top[...])
    rest[...] = values[half:, half:] - dot_tn(beside, beside)


def second_factor_kernel(top, corner, rest, across, out, spread):
    half = top.shape[0]
    out[:half, :half] = top[...]
    out[:half, half:] = jnp.zeros((half, half), F32)
    eliminate(rest[...], out, half, spread)
    out[half:, :half] = -dot(out[half:, half:], corner[...])
    out[...] = out[...] * across[...]


def spread_room(columns):
    return pltpu.VMEM((2 * GROUP * (GROUP + 1), columns // 2), F32)


def first_factor(blocks, order):
    columns = blocks[0].shape[1]
    half = like((columns // 2, columns // 2))
    return whole(
        functools.partial(first_factor_kernel, order),
        [half, half, half, like((1, columns))],
        *blocks,
        scratch=[pltpu.VMEM((columns, columns), F32), spread_room(columns)],
        flops=6 * 10**9,
    )


def second_factor(halves):
    columns = halves[3].shape[1]
    return whole(
        second_factor_kernel,
        like((columns, columns)),
        *halves,
        scratch=[spread_room(columns)],
        flops=6 * 10**9,
    )


def next_head(head):
    count = lax.axis_size("rows")
    return lax.ppermute(head, "rows", [(i + 1, i) for i in range(count - 1)])


def band_kernel(field, low, after, diag_tiles, upper_tiles, part, image, matrix):
    band = after.shape[0]
    tiles = field.shape[0] // band

    def values(at):
        return field[at].astype(F32) + low[at].astype(F32)

    for t in range(tiles):
        at = slice(t * band, (t + 1) * band)
        following = slice((t + 1) * band, (t + 2) * band)
        following = after[...].astype(F32) if t == tiles - 1 else values(following)
        image[at] = 0.5 * dot_three(diag_tiles[at], values(at)) + dot_three(upper_tiles[at], following)
    matrix[...] = dot_two(field[...], image[...], TN)
    matrix[...] += lax.dot_general(
        low[...], image[...].astype(BF16), TN, preferred_element_type=F32
    )
    size = part.shape[0]
    part[...] = matrix[pl.ds(pl.multiple_of(lax.axis_index("node") * size, 8), size), :]


def band_slice(field, low, after, diag_tiles, upper_tiles):
    rows, columns = field.shape
    return whole(
        band_kernel,
        like((columns // lax.axis_size("node"), columns)),
        field,
        low,
        after,
        diag_tiles,
        upper_tiles,
        scratch=[pltpu.VMEM((rows, columns), F32), pltpu.VMEM((columns, columns), F32)],
    )


def finish_kernel(order, field, low, *refs):
    blocks, factors = refs[: -6 - ITERS], refs[-6 - ITERS : -6]
    vectors_at, projected_at, vectors, projected, matrix, sent = refs[-6:]
    rows = field.shape[0]
    tile = rows // 3 if rows % 48 == 0 else rows
    copies = []

    def send(source, target):
        copies.append(pltpu.make_async_copy(source, target, sent.at[len(copies)]))
        copies[-1].start()

    for at in range(0, rows, tile):
        span = pl.ds(at, tile)
        vectors[span] = refined(field[span], low[span], factors[-1][...])
        send(vectors.at[span], vectors_at.at[span])
    node = lax.axis_index("node")
    size = blocks[0].shape[0] // ITERS
    for k, factor in enumerate(factors):
        for step, block in enumerate(blocks):
            at = pl.multiple_of((node ^ step) * size, 8)
            matrix[pl.ds(at, size), :] = block[k * size : (k + 1) * size]
        value = dot_three(dot_three(factor[...], matrix[...]), factor[...], NT)
        projected[k] = (value + value.T) * (1.0 / order)
        send(projected.at[k], projected_at.at[k])
    for copy in copies:
        copy.wait()


def finish(field, low, blocks, factors, order):
    rows, columns = field.shape
    operands = [field, low, *blocks, *factors]
    vmem = pl.BlockSpec(memory_space=pltpu.VMEM)
    shapes = [(rows, columns), (ITERS, columns, columns)]
    return pl.pallas_call(
        functools.partial(finish_kernel, order),
        in_specs=[vmem for _ in operands],
        out_specs=[pl.BlockSpec(memory_space=pltpu.HBM)] * 2,
        out_shape=[jax.ShapeDtypeStruct(x, F32) for x in shapes],
        scratch_shapes=[pltpu.VMEM(x, F32) for x in shapes]
        + [pltpu.VMEM((columns, columns), F32), pltpu.SemaphoreType.DMA((3 + ITERS,))],
        cost_estimate=pl.CostEstimate(flops=10**9, bytes_accessed=10**6, transcendentals=0),
        compiler_params=pltpu.CompilerParams(vmem_limit_bytes=GRANT),
        name="finish",
    )(*[local(x) for x in operands])


def after(value, *others):
    return lax.optimization_barrier((value,) + others)[0]


def per_device(subspace, inverse, weights, diag_tiles, upper_tiles):
    order = float(subspace.shape[0] * lax.axis_size("rows"))
    band = upper_tiles.shape[1]
    partners = lax.axis_size("node") - 1
    factors, pairs = [], []
    for iteration in range(ITERS):
        final = iteration == ITERS - 1
        parts = 1 if final else 2
        if iteration == 0:
            out_a, out_b, coupling, vectors = start(subspace, upper_tiles, inverse)
            got_b = link_swap(out_b)
            got_a = core_swap(out_a)
            base, inverse, weights = start_base(weights, inverse, vectors, coupling, got_a)
            own, *terms = correct(weights, base, got_b, coupling, inverse, parts)
        else:
            own, *terms = solve(
                weights, field, low, factor, coupling, inverse, got_a, got_b, parts
            )
        got = node_spread(terms[:partners])
        if not final:
            low_got = node_spread(terms[partners:])
        total = tree_sum([own] + [x.astype(F32) for x in got])
        piece = total.astype(BF16)
        blocks = [piece] + node_spread([piece] * partners)
        total, sent = lax.optimization_barrier((total, piece))
        if not final:
            total = total + tree_sum([x.astype(F32) for x in low_got])
        low_piece = (total - sent.astype(F32)).astype(BF16)
        low = join([low_piece] + node_spread([low_piece] * partners))
        field, head, part = gram_slice(blocks, band)
        part = part + core_swap(part)
        following = next_head(after(head, part))
        total = chip_sum(part)
        gathered = [total] + node_spread([total] * partners)
        pair = band_slice(field, low, after(following, total), diag_tiles, upper_tiles)
        if not final:
            out_a, out_b = tips(field, low, coupling, inverse)
            got_b = link_swap(out_b)
            got_a = core_swap(out_a)
        halves = first_factor(gathered, order)
        pair = pair + core_swap(pair)
        pairs.append(chip_sum(after(pair, *gathered)))
        if final:
            pair = after(jnp.concatenate(pairs, 0), *halves)
            spread = [pair] + node_spread([pair] * partners)
        factor = second_factor(halves)
        factors.append(factor)
    orthonormal, projected = finish(field, low, spread, factors, order)
    return orthonormal, projected


def solution(mesh):
    placed = (
        P("rows", None),
        P("node", None, "rows", None),
        P("node", None),
        P("rows", None),
        P("rows", None),
    )
    return jax.shard_map(
        per_device, mesh=mesh, in_specs=placed, out_specs=(P("rows", None), P()), check_vma=False
    )
```

profile of v0, /device:TPU:0, one launch (start us, length us, event | category | flops | bytes accessed | tf_op | source)
XLA Modules:
  0.0 120.4 jit_solution(13426042486565084590)
XLA Ops:
  0.6 2.1 %shard_map.68 = (bf16[128,512]{1,0:T(8,128)(2,1)S(1)}, bf16[128,512]{1,0:T(8,128)(2,1)S(1)}, f32[128,128]{1,0:T(8,128)S(1)}, bf16[768,256]{1,0:T(8,128)(2,1)S(1)}) custom-call(bf16[1,2,768,768]{3,2,1,0:T(8,128)(2,1)} %source.3, bf16[768,256]{1,0:T(8,128)(2,1)} %vectors_at.1, f32[768,128]{1,0:T(8,128)} %upper_tiles.3), custom_call_target="tpu_custom_call" | custom-call | flops 100000000 | bytes 1000000 | tf_op jit(solution)/shard_map/pallas_call | solution.py:168
  4.3 2.7 %shard_map.69 = (f32[768,256]{1,0:T(8,128)S(1)}, bf16[1,2,768,768]{3,2,1,0:T(8,128)(2,1)S(1)}, f32[1,2]{1,0:T(1,128)S(1)}) custom-call(f32[1,2]{1,0:T(1,128)} %weights_at.1, bf16[1,2,768,768]{3,2,1,0:T(8,128)(2,1)} %source.3, bf16[768,256]{1,0:T(8,128)(2,1)S(1)} %get-tuple-element.47.vectors, f32[128,128]{1,0:T(8,128)S(1)} %get-tuple-element.48.coupling, ...), custom_call_target="tpu_custom_call" | custom-call | flops 100000000 | bytes 1000000 | tf_op jit(solution)/shard_map/pallas_call | solution.py:168
  7.9 2.9 %collective-permute-start.2 = (bf16[192,256]{1,0:T(8,128)(2,1)S(1)}, bf16[192,256]{1,0:T(8,128)(2,1)S(1)}, u32[]{:S(2)}, u32[]{:S(2)}) collective-permute-start(bf16[192,256]{1,0:T(8,128)(2,1)S(1)} %get-tuple-element.55), channel_id=1, source_target_pairs={{0,8},{8,0},{16,24},{24,16},{1,9},{9,1},{17,25},{25,17},{2,10},{10... | collective-permute-start | bytes 294920 | tf_op jit(solution)/shard_map/ppermute | solution.py:95
  10.8 1.5 %collective-permute-start.3 = (bf16[192,256]{1,0:T(8,128)(2,1)S(1)}, bf16[192,256]{1,0:T(8,128)(2,1)S(1)}, u32[]{:S(2)}, u32[]{:S(2)}) collective-permute-start(bf16[192,256]{1,0:T(8,128)(2,1)S(1)} %get-tuple-element.56), channel_id=1, source_target_pairs={{0,16},{8,24},{16,0},{24,8},{1,17},{9,25},{17,1},{25,9},{2,18},{10... | collective-permute-start | bytes 294920 | tf_op jit(solution)/shard_map/ppermute | solution.py:95
  12.4 1.1 collective-permute-done.2
  13.4 2.0 %collective-permute-done.3 = bf16[192,256]{1,0:T(8,128)(2,1)S(1)} collective-permute-done((bf16[192,256]{1,0:T(8,128)(2,1)S(1)}, bf16[192,256]{1,0:T(8,128)(2,1)S(1)}, u32[]{:S(2)}, u32[]{:S(2)}) %collective-permute-start.3) | collective-permute-done | bytes 98336 | tf_op jit(solution)/shard_map/ppermute | solution.py:95
  15.4 2.5 %collective-permute-done.4 = bf16[192,256]{1,0:T(8,128)(2,1)S(1)} collective-permute-done((bf16[192,256]{1,0:T(8,128)(2,1)S(1)}, bf16[192,256]{1,0:T(8,128)(2,1)S(1)}, u32[]{:S(2)}, u32[]{:S(2)}) %collective-permute-start.4) | collective-permute-done | bytes 98336 | tf_op jit(solution)/shard_map/ppermute | solution.py:95
  18.8 2.2 %collective-permute-start.6 = (bf16[192,256]{1,0:T(8,128)(2,1)S(1)}, bf16[192,256]{1,0:T(8,128)(2,1)S(1)}, u32[]{:S(2)}, u32[]{:S(2)}) collective-permute-start(bf16[192,256]{1,0:T(8,128)(2,1)S(1)} %get-tuple-element.63.refs_0_), channel_id=1, source_target_pairs={{0,16},{8,24},{16,0},{24,8},{1,17},{9,25},{17,1},{25,9},{2,18},{10... | collective-permute-start | bytes 294920 | tf_op jit(solution)/shard_map/ppermute | solution.py:95
  21.6 1.5 %collective-permute-start.8 = (bf16[192,256]{1,0:T(8,128)(2,1)S(1)}, bf16[192,256]{1,0:T(8,128)(2,1)S(1)}, u32[]{:S(2)}, u32[]{:S(2)}) collective-permute-start(bf16[192,256]{1,0:T(8,128)(2,1)S(1)} %get-tuple-element.60), channel_id=1, source_target_pairs={{0,8},{8,0},{16,24},{24,16},{1,9},{9,1},{17,25},{25,17},{2,10},{10... | collective-permute-start | bytes 294920 | tf_op jit(solution)/shard_map/ppermute | solution.py:95
  23.0 1.7 %collective-permute-done.7.refs_3_ = bf16[192,256]{1,0:T(8,128)(2,1)S(1)} collective-permute-done((bf16[192,256]{1,0:T(8,128)(2,1)S(1)}, bf16[192,256]{1,0:T(8,128)(2,1)S(1)}, u32[]{:S(2)}, u32[]{:S(2)}) %collective-permute-start.7) | collective-permute-done | bytes 98336 | tf_op jit(solution)/shard_map/ppermute | solution.py:95
  25.2 1.6 %collective-permute-done.6.refs_2_ = bf16[192,256]{1,0:T(8,128)(2,1)S(1)} collective-permute-done((bf16[192,256]{1,0:T(8,128)(2,1)S(1)}, bf16[192,256]{1,0:T(8,128)(2,1)S(1)}, u32[]{:S(2)}, u32[]{:S(2)}) %collective-permute-start.6) | collective-permute-done | bytes 98336 | tf_op jit(solution)/shard_map/ppermute | solution.py:95
  27.2 1.2 %collective-permute-done.14 = f32[64,256]{1,0:T(8,128)S(1)} collective-permute-done((f32[64,256]{1,0:T(8,128)S(1)}, f32[64,256]{1,0:T(8,128)S(1)}, u32[]{:S(2)}, u32[]{:S(2)}) %collective-permute-start.14) | collective-permute-done | bytes 65568 | tf_op jit(solution)/shard_map/ppermute | solution.py:100
  28.5 4.4 %collective-permute-start.17 = (f32[64,256]{1,0:T(8,128)S(1)}, f32[64,256]{1,0:T(8,128)S(1)}, u32[]{:S(2)}, u32[]{:S(2)}) collective-permute-start(f32[64,256]{1,0:T(8,128)S(1)} %add.81), channel_id=1, source_target_pairs={{0,6},{1,7},{2,4},{3,5},{4,2},{5,3},{6,0},{7,1},{8,14},{9,15},{10,... | collective-permute-start | bytes 196616 | tf_op jit(solution)/shard_map/ppermute | solution.py:126
  33.9 2.0 %collective-permute-start.13 = (bf16[192,256]{1,0:T(8,128)(2,1)S(1)}, bf16[192,256]{1,0:T(8,128)(2,1)S(1)}, u32[]{:S(2)}, u32[]{:S(2)}) collective-permute-start(bf16[192,256]{1,0:T(8,128)(2,1)S(1)} %subtract_convert_fusion.1.refs_0_), channel_id=1, source_target_pairs={{0,24},{8,16},{16,8},{24,0},{1,25},{9,17},{17,9},{25,1},{2,26},{10... | collective-permute-start | bytes 294920 | tf_op jit(solution)/shard_map/ppermute | solution.py:95
  36.4 1.1 collective-permute-start.11
  37.5 2.0 %collective-permute-done.16 = f32[64,256]{1,0:T(8,128)S(1)} collective-permute-done((f32[64,256]{1,0:T(8,128)S(1)}, f32[64,256]{1,0:T(8,128)S(1)}, u32[]{:S(2)}, u32[]{:S(2)}) %collective-permute-start.16) | collective-permute-done | bytes 65568 | tf_op jit(solution)/shard_map/ppermute | solution.py:126
  39.5 2.0 %collective-permute-start.20 = (f32[64,256]{1,0:T(8,128)S(1)}, f32[64,256]{1,0:T(8,128)S(1)}, u32[]{:S(2)}, u32[]{:S(2)}) collective-permute-start(f32[64,256]{1,0:T(8,128)S(1)} %add_add_fusion.5.refs_0_), channel_id=1, source_target_pairs={{0,24},{8,16},{16,8},{24,0},{1,25},{9,17},{17,9},{25,1},{2,26},{10... | collective-permute-start | bytes 196616 | tf_op jit(solution)/shard_map/ppermute | solution.py:95
  46.6 3.9 %shard_map.73 = (f32[128,128]{1,0:T(8,128)S(1)}, f32[128,128]{1,0:T(8,128)S(1)}, f32[128,128]{1,0:T(8,128)S(1)}, f32[1,256]{1,0:T(1,128)S(1)}) custom-call(f32[64,256]{1,0:T(8,128)S(1)} %add_add_fusion.5.refs_0_, f32[64,256]{1,0:T(8,128)S(1)} %collective-permute-done.18.refs_1_, f32[64,256]{1,0:T(8,128)S(1)} %collective-permute-done.19.refs_2_, ...), custom_call_target="tpu_custom_call" | custom-call | flops 6000000000 | bytes 262144 | tf_op jit(solution)/shard_map/pallas_call | solution.py:82
  50.5 3.4 %shard_map.74.factor.refs_4_ = f32[256,256]{1,0:T(8,128)S(1)} custom-call(f32[128,128]{1,0:T(8,128)S(1)} %get-tuple-element.65.top, f32[128,128]{1,0:T(8,128)S(1)} %get-tuple-element.66.corner, f32[128,128]{1,0:T(8,128)S(1)} %get-tuple-element.67.rest, f32[1,256]{1,0:T(1,128)S(1)} %get-tuple-element.68.across), custom_call_target="tpu_custom_call" | custom-call | flops 6000000000 | bytes 197632 | tf_op jit(solution)/shard_map/pallas_call | solution.py:82
  54.0 2.8 %shard_map.76 = (f32[192,256]{1,0:T(8,128)S(1)}, bf16[192,256]{1,0:T(8,128)(2,1)S(1)}, bf16[192,256]{1,0:T(8,128)(2,1)S(1)}, bf16[192,256]{1,0:T(8,128)(2,1)S(1)}) custom-call(f32[1,2]{1,0:T(1,128)S(1)} %get-tuple-element.50.weights, bf16[768,256]{1,0:T(8,128)(2,1)S(1)} %get-tuple-element.58.field, bf16[768,256]{1,0:T(8,128)(2,1)S(1)} %shard_map.72.low, ...), custom_call_target="tpu_custom_call" | custom-call | flops 100000000 | bytes 3997704 | tf_op jit(solution)/shard_map/pallas_call | solution.py:82
  57.6 1.2 collective-permute-start.24
  58.8 1.6 %collective-permute-start.25 = (bf16[192,256]{1,0:T(8,128)(2,1)S(1)}, bf16[192,256]{1,0:T(8,128)(2,1)S(1)}, u32[]{:S(2)}, u32[]{:S(2)}) collective-permute-start(bf16[192,256]{1,0:T(8,128)(2,1)S(1)} %get-tuple-element.74), channel_id=1, source_target_pairs={{0,24},{8,16},{16,8},{24,0},{1,25},{9,17},{17,9},{25,1},{2,26},{10... | collective-permute-start | bytes 294920 | tf_op jit(solution)/shard_map/ppermute | solution.py:95
  60.4 1.3 %collective-permute-start.32 = (bf16[128,256]{1,0:T(8,128)(2,1)S(1)}, bf16[128,256]{1,0:T(8,128)(2,1)S(1)}, u32[]{:S(2)}, u32[]{:S(2)}) collective-permute-start(bf16[128,256]{1,0:T(8,128)(2,1)S(1)} %get-tuple-element.79), channel_id=1, source_target_pairs={{1,0},{2,1},{3,2},{4,3},{5,4},{6,5},{7,6},{9,8},{10,9},{11,10},{12... | collective-permute-start | bytes 196616 | tf_op jit(solution)/shard_map/ppermute | solution.py:516
  63.2 1.8 %collective-permute-done.25 = bf16[192,256]{1,0:T(8,128)(2,1)S(1)} collective-permute-done((bf16[192,256]{1,0:T(8,128)(2,1)S(1)}, bf16[192,256]{1,0:T(8,128)(2,1)S(1)}, u32[]{:S(2)}, u32[]{:S(2)}) %collective-permute-start.25) | collective-permute-done | bytes 98336 | tf_op jit(solution)/shard_map/ppermute | solution.py:95
  65.1 2.0 %collective-permute-start.28 = (bf16[192,256]{1,0:T(8,128)(2,1)S(1)}, bf16[192,256]{1,0:T(8,128)(2,1)S(1)}, u32[]{:S(2)}, u32[]{:S(2)}) collective-permute-start(bf16[192,256]{1,0:T(8,128)(2,1)S(1)} %get-tuple-element.77.refs_0_), channel_id=1, source_target_pairs={{0,24},{8,16},{16,8},{24,0},{1,25},{9,17},{17,9},{25,1},{2,26},{10... | collective-permute-start | bytes 294920 | tf_op jit(solution)/shard_map/ppermute | solution.py:95
  68.7 2.0 %collective-permute-start.31 = (bf16[192,256]{1,0:T(8,128)(2,1)S(1)}, bf16[192,256]{1,0:T(8,128)(2,1)S(1)}, u32[]{:S(2)}, u32[]{:S(2)}) collective-permute-start(bf16[192,256]{1,0:T(8,128)(2,1)S(1)} %subtract_convert_fusion.refs_0_), channel_id=1, source_target_pairs={{0,24},{8,16},{16,8},{24,0},{1,25},{9,17},{17,9},{25,1},{2,26},{10... | collective-permute-start | bytes 294920 | tf_op jit(solution)/shard_map/ppermute | solution.py:95
  71.5 2.5 %collective-permute-done.27.refs_2_ = bf16[192,256]{1,0:T(8,128)(2,1)S(1)} collective-permute-done((bf16[192,256]{1,0:T(8,128)(2,1)S(1)}, bf16[192,256]{1,0:T(8,128)(2,1)S(1)}, u32[]{:S(2)}, u32[]{:S(2)}) %collective-permute-start.27) | collective-permute-done | bytes 98336 | tf_op jit(solution)/shard_map/ppermute | solution.py:95
  74.5 1.2 %shard_map.79 = f32[64,256]{1,0:T(8,128)S(1)} custom-call(bf16[768,256]{1,0:T(8,128)(2,1)S(1)} %get-tuple-element.58.field, bf16[768,256]{1,0:T(8,128)(2,1)S(1)} %shard_map.72.low, bf16[128,256]{1,0:T(8,128)(2,1)S(1)} %collective-permute-done.32.after, f32[768,128]{1,0:T(8,128)S(1)} %copy-done.1, f32[768,128]{1,0:T(8,128)S(1)} %copy-done), custom_call_target="tpu_custom_call" | custom-call | flops 100000000 | bytes 1638400 | tf_op jit(solution)/shard_map/pallas_call | solution.py:82
  76.9 1.1 collective-permute-start.29
  78.0 2.8 %collective-permute-start.41 = (f32[64,256]{1,0:T(8,128)S(1)}, f32[64,256]{1,0:T(8,128)S(1)}, u32[]{:S(2)}, u32[]{:S(2)}) collective-permute-start(f32[64,256]{1,0:T(8,128)S(1)} %add.92), channel_id=1, source_target_pairs={{0,6},{1,7},{2,4},{3,5},{4,2},{5,3},{6,0},{7,1},{8,14},{9,15},{10,... | collective-permute-start | bytes 196616 | tf_op jit(solution)/shard_map/ppermute | solution.py:126
  82.4 2.8 %collective-permute-start.36 = (f32[64,256]{1,0:T(8,128)S(1)}, f32[64,256]{1,0:T(8,128)S(1)}, u32[]{:S(2)}, u32[]{:S(2)}) collective-permute-start(f32[64,256]{1,0:T(8,128)S(1)} %add.88), channel_id=1, source_target_pairs={{0,6},{1,7},{2,4},{3,5},{4,2},{5,3},{6,0},{7,1},{8,14},{9,15},{10,... | collective-permute-start | bytes 196616 | tf_op jit(solution)/shard_map/ppermute | solution.py:126
  85.3 2.5 %collective-permute-start.34 = (f32[64,256]{1,0:T(8,128)S(1)}, f32[64,256]{1,0:T(8,128)S(1)}, u32[]{:S(2)}, u32[]{:S(2)}) collective-permute-start(f32[64,256]{1,0:T(8,128)S(1)} %add.88), channel_id=1, source_target_pairs={{0,2},{1,3},{2,0},{3,1},{4,6},{5,7},{6,4},{7,5},{8,10},{9,11},{10,... | collective-permute-start | bytes 196616 | tf_op jit(solution)/shard_map/ppermute | solution.py:126
  87.8 2.8 %collective-permute-done.40 = f32[64,256]{1,0:T(8,128)S(1)} collective-permute-done((f32[64,256]{1,0:T(8,128)S(1)}, f32[64,256]{1,0:T(8,128)S(1)}, u32[]{:S(2)}, u32[]{:S(2)}) %collective-permute-start.40) | collective-permute-done | bytes 65568 | tf_op jit(solution)/shard_map/ppermute | solution.py:126
  90.6 1.5 %collective-permute-start.38 = (bf16[128,256]{1,0:T(8,128)(2,1)S(1)}, bf16[128,256]{1,0:T(8,128)(2,1)S(1)}, u32[]{:S(2)}, u32[]{:S(2)}) collective-permute-start(bf16[128,256]{1,0:T(8,128)(2,1)S(1)} %get-tuple-element.84), channel_id=1, source_target_pairs={{1,0},{2,1},{3,2},{4,3},{5,4},{6,5},{7,6},{9,8},{10,9},{11,10},{12... | collective-permute-start | bytes 196616 | tf_op jit(solution)/shard_map/ppermute | solution.py:516
  92.1 1.7 %collective-permute-start.45 = (f32[64,256]{1,0:T(8,128)S(1)}, f32[64,256]{1,0:T(8,128)S(1)}, u32[]{:S(2)}, u32[]{:S(2)}) collective-permute-start(f32[64,256]{1,0:T(8,128)S(1)} %add_add_fusion.3.refs_0_), channel_id=1, source_target_pairs={{0,24},{8,16},{16,8},{24,0},{1,25},{9,17},{17,9},{25,1},{2,26},{10... | collective-permute-start | bytes 196616 | tf_op jit(solution)/shard_map/ppermute | solution.py:95
  93.8 1.0 collective-permute-start.44
  94.9 1.2 %shard_map.80 = f32[64,256]{1,0:T(8,128)S(1)} custom-call(bf16[768,256]{1,0:T(8,128)(2,1)S(1)} %get-tuple-element.75.field, bf16[768,256]{1,0:T(8,128)(2,1)S(1)} %shard_map.78.low, bf16[128,256]{1,0:T(8,128)(2,1)S(1)} %collective-permute-done.38.after, f32[768,128]{1,0:T(8,128)S(1)} %copy-done.1, f32[768,128]{1,0:T(8,128)S(1)} %copy-done), custom_call_target="tpu_custom_call" | custom-call | flops 100000000 | bytes 1638400 | tf_op jit(solution)/shard_map/pallas_call | solution.py:82
  96.1 1.1 collective-permute-start.43
  97.3 1.2 collective-permute-done.42
  99.4 1.6 %collective-permute-done.43.refs_1_ = f32[64,256]{1,0:T(8,128)S(1)} collective-permute-done((f32[64,256]{1,0:T(8,128)S(1)}, f32[64,256]{1,0:T(8,128)S(1)}, u32[]{:S(2)}, u32[]{:S(2)}) %collective-permute-start.43) | collective-permute-done | bytes 65568 | tf_op jit(solution)/shard_map/ppermute | solution.py:95
  101.1 1.9 %collective-permute-start.48 = (f32[64,256]{1,0:T(8,128)S(1)}, f32[64,256]{1,0:T(8,128)S(1)}, u32[]{:S(2)}, u32[]{:S(2)}) collective-permute-start(f32[64,256]{1,0:T(8,128)S(1)} %add.96), channel_id=1, source_target_pairs={{0,6},{1,7},{2,4},{3,5},{4,2},{5,3},{6,0},{7,1},{8,14},{9,15},{10,... | collective-permute-start | bytes 196616 | tf_op jit(solution)/shard_map/ppermute | solution.py:126
  103.0 2.4 %collective-permute-start.46 = (f32[64,256]{1,0:T(8,128)S(1)}, f32[64,256]{1,0:T(8,128)S(1)}, u32[]{:S(2)}, u32[]{:S(2)}) collective-permute-start(f32[64,256]{1,0:T(8,128)S(1)} %add.96), channel_id=1, source_target_pairs={{0,2},{1,3},{2,0},{3,1},{4,6},{5,7},{6,4},{7,5},{8,10},{9,11},{10,... | collective-permute-start | bytes 196616 | tf_op jit(solution)/shard_map/ppermute | solution.py:126
  105.5 3.9 %shard_map.81 = (f32[128,128]{1,0:T(8,128)S(1)}, f32[128,128]{1,0:T(8,128)S(1)}, f32[128,128]{1,0:T(8,128)S(1)}, f32[1,256]{1,0:T(1,128)S(1)}) custom-call(f32[64,256]{1,0:T(8,128)S(1)} %add_add_fusion.3.refs_0_, f32[64,256]{1,0:T(8,128)S(1)} %collective-permute-done.43.refs_1_, f32[64,256]{1,0:T(8,128)S(1)} %collective-permute-done.44.refs_2_, ...), custom_call_target="tpu_custom_call" | custom-call | flops 6000000000 | bytes 262144 | tf_op jit(solution)/shard_map/pallas_call | solution.py:82
  109.6 1.2 collective-permute-start.51
  111.7 1.4 %collective-permute-start.49 = (f32[128,256]{1,0:T(8,128)S(1)}, f32[128,256]{1,0:T(8,128)S(1)}, u32[]{:S(2)}, u32[]{:S(2)}) collective-permute-start(f32[128,256]{1,0:T(8,128)S(1)} %pad_maximum_fusion.refs_0_), channel_id=1, source_target_pairs={{0,8},{8,0},{16,24},{24,16},{1,9},{9,1},{17,25},{25,17},{2,10},{10... | collective-permute-start | bytes 393224 | tf_op jit(solution)/shard_map/ppermute | solution.py:95
  113.1 3.4 %shard_map.82.refs_5_ = f32[256,256]{1,0:T(8,128)S(1)} custom-call(f32[128,128]{1,0:T(8,128)S(1)} %get-tuple-element.87.top, f32[128,128]{1,0:T(8,128)S(1)} %get-tuple-element.88.corner, f32[128,128]{1,0:T(8,128)S(1)} %get-tuple-element.89.rest, f32[1,256]{1,0:T(1,128)S(1)} %get-tuple-element.90.across), custom_call_target="tpu_custom_call" | custom-call | flops 6000000000 | bytes 197632 | tf_op jit(solution)/shard_map/pallas_call | solution.py:82
  116.9 1.3 %collective-permute-done.50.refs_2_ = f32[128,256]{1,0:T(8,128)S(1)} collective-permute-done((f32[128,256]{1,0:T(8,128)S(1)}, f32[128,256]{1,0:T(8,128)S(1)}, u32[]{:S(2)}, u32[]{:S(2)}) %collective-permute-start.50) | collective-permute-done | bytes 131104 | tf_op jit(solution)/shard_map/ppermute | solution.py:95
  118.2 2.0 %finish.1 = (f32[768,256]{1,0:T(8,128)}, f32[2,256,256]{2,1,0:T(8,128)}) custom-call(bf16[768,256]{1,0:T(8,128)(2,1)S(1)} %get-tuple-element.75.field, bf16[768,256]{1,0:T(8,128)(2,1)S(1)} %shard_map.78.low, f32[128,256]{1,0:T(8,128)S(1)} %pad_maximum_fusion.refs_0_, f32[128,256]{1,0:T(8,128)S(1)} %collective-permute-done.49.refs_1_, ...), custom_call_target="tpu_custom_call" | custom-call | flops 1000000000 | bytes 1000000 | tf_op jit(solution)/shard_map/finish/pallas_call | solution.py:586
  (89 shorter events, 22.2 us)
Async XLA Ops:
  3.3 3.7 %collective-permute-start.1 = (bf16[128,512]{1,0:T(8,128)(2,1)S(1)}, bf16[128,512]{1,0:T(8,128)(2,1)S(1)}, u32[]{:S(2)}, u32[]{:S(2)}) collective-permute-start(bf16[128,512]{1,0:T(8,128)(2,1)S(1)} %get-tuple-element.52), channel_id=1, source_target_pairs={{1,2},{3,4},{5,6},{2,1},{4,3},{6,5},{9,10},{11,12},{13,14},{10,9},... | collective-permute-start | bytes 393224 | tf_op jit(solution)/shard_map/ppermute | solution.py:106
  7.9 5.5 %collective-permute-start.2 = (bf16[192,256]{1,0:T(8,128)(2,1)S(1)}, bf16[192,256]{1,0:T(8,128)(2,1)S(1)}, u32[]{:S(2)}, u32[]{:S(2)}) collective-permute-start(bf16[192,256]{1,0:T(8,128)(2,1)S(1)} %get-tuple-element.55), channel_id=1, source_target_pairs={{0,8},{8,0},{16,24},{24,16},{1,9},{9,1},{17,25},{25,17},{2,10},{10... | collective-permute-start | bytes 294920 | tf_op jit(solution)/shard_map/ppermute | solution.py:95
  10.8 4.6 %collective-permute-start.3 = (bf16[192,256]{1,0:T(8,128)(2,1)S(1)}, bf16[192,256]{1,0:T(8,128)(2,1)S(1)}, u32[]{:S(2)}, u32[]{:S(2)}) collective-permute-start(bf16[192,256]{1,0:T(8,128)(2,1)S(1)} %get-tuple-element.56), channel_id=1, source_target_pairs={{0,16},{8,24},{16,0},{24,8},{1,17},{9,25},{17,1},{25,9},{2,18},{10... | collective-permute-start | bytes 294920 | tf_op jit(solution)/shard_map/ppermute | solution.py:95
  12.3 5.6 %collective-permute-start.4 = (bf16[192,256]{1,0:T(8,128)(2,1)S(1)}, bf16[192,256]{1,0:T(8,128)(2,1)S(1)}, u32[]{:S(2)}, u32[]{:S(2)}) collective-permute-start(bf16[192,256]{1,0:T(8,128)(2,1)S(1)} %get-tuple-element.57), channel_id=1, source_target_pairs={{0,24},{8,16},{16,8},{24,0},{1,25},{9,17},{17,9},{25,1},{2,26},{10... | collective-permute-start | bytes 294920 | tf_op jit(solution)/shard_map/ppermute | solution.py:95
  18.0 6.7 %collective-permute-start.7 = (bf16[192,256]{1,0:T(8,128)(2,1)S(1)}, bf16[192,256]{1,0:T(8,128)(2,1)S(1)}, u32[]{:S(2)}, u32[]{:S(2)}) collective-permute-start(bf16[192,256]{1,0:T(8,128)(2,1)S(1)} %get-tuple-element.63.refs_0_), channel_id=1, source_target_pairs={{0,24},{8,16},{16,8},{24,0},{1,25},{9,17},{17,9},{25,1},{2,26},{10... | collective-permute-start | bytes 294920 | tf_op jit(solution)/shard_map/ppermute | solution.py:95
  18.8 7.9 %collective-permute-start.6 = (bf16[192,256]{1,0:T(8,128)(2,1)S(1)}, bf16[192,256]{1,0:T(8,128)(2,1)S(1)}, u32[]{:S(2)}, u32[]{:S(2)}) collective-permute-start(bf16[192,256]{1,0:T(8,128)(2,1)S(1)} %get-tuple-element.63.refs_0_), channel_id=1, source_target_pairs={{0,16},{8,24},{16,0},{24,8},{1,17},{9,25},{17,1},{25,9},{2,18},{10... | collective-permute-start | bytes 294920 | tf_op jit(solution)/shard_map/ppermute | solution.py:95
  21.0 5.7 %collective-permute-start.5 = (bf16[192,256]{1,0:T(8,128)(2,1)S(1)}, bf16[192,256]{1,0:T(8,128)(2,1)S(1)}, u32[]{:S(2)}, u32[]{:S(2)}) collective-permute-start(bf16[192,256]{1,0:T(8,128)(2,1)S(1)} %get-tuple-element.63.refs_0_), channel_id=1, source_target_pairs={{0,8},{8,0},{16,24},{24,16},{1,9},{9,1},{17,25},{25,17},{2,10},{10... | collective-permute-start | bytes 294920 | tf_op jit(solution)/shard_map/ppermute | solution.py:95
  21.6 12.2 %collective-permute-start.8 = (bf16[192,256]{1,0:T(8,128)(2,1)S(1)}, bf16[192,256]{1,0:T(8,128)(2,1)S(1)}, u32[]{:S(2)}, u32[]{:S(2)}) collective-permute-start(bf16[192,256]{1,0:T(8,128)(2,1)S(1)} %get-tuple-element.60), channel_id=1, source_target_pairs={{0,8},{8,0},{16,24},{24,16},{1,9},{9,1},{17,25},{25,17},{2,10},{10... | collective-permute-start | bytes 294920 | tf_op jit(solution)/shard_map/ppermute | solution.py:95
  23.0 10.8 %collective-permute-start.9 = (bf16[192,256]{1,0:T(8,128)(2,1)S(1)}, bf16[192,256]{1,0:T(8,128)(2,1)S(1)}, u32[]{:S(2)}, u32[]{:S(2)}) collective-permute-start(bf16[192,256]{1,0:T(8,128)(2,1)S(1)} %get-tuple-element.61), channel_id=1, source_target_pairs={{0,16},{8,24},{16,0},{24,8},{1,17},{9,25},{17,1},{25,9},{2,18},{10... | collective-permute-start | bytes 294920 | tf_op jit(solution)/shard_map/ppermute | solution.py:95
  24.7 9.2 %collective-permute-start.10 = (bf16[192,256]{1,0:T(8,128)(2,1)S(1)}, bf16[192,256]{1,0:T(8,128)(2,1)S(1)}, u32[]{:S(2)}, u32[]{:S(2)}) collective-permute-start(bf16[192,256]{1,0:T(8,128)(2,1)S(1)} %get-tuple-element.62), channel_id=1, source_target_pairs={{0,24},{8,16},{16,8},{24,0},{1,25},{9,17},{17,9},{25,1},{2,26},{10... | collective-permute-start | bytes 294920 | tf_op jit(solution)/shard_map/ppermute | solution.py:95
  28.5 8.0 %collective-permute-start.17 = (f32[64,256]{1,0:T(8,128)S(1)}, f32[64,256]{1,0:T(8,128)S(1)}, u32[]{:S(2)}, u32[]{:S(2)}) collective-permute-start(f32[64,256]{1,0:T(8,128)S(1)} %add.81), channel_id=1, source_target_pairs={{0,6},{1,7},{2,4},{3,5},{4,2},{5,3},{6,0},{7,1},{8,14},{9,15},{10,... | collective-permute-start | bytes 196616 | tf_op jit(solution)/shard_map/ppermute | solution.py:126
  32.9 6.6 %collective-permute-start.16 = (f32[64,256]{1,0:T(8,128)S(1)}, f32[64,256]{1,0:T(8,128)S(1)}, u32[]{:S(2)}, u32[]{:S(2)}) collective-permute-start(f32[64,256]{1,0:T(8,128)S(1)} %add.81), channel_id=1, source_target_pairs={{0,4},{1,5},{2,6},{3,7},{4,0},{5,1},{6,2},{7,3},{8,12},{9,13},{10,... | collective-permute-start | bytes 196616 | tf_op jit(solution)/shard_map/ppermute | solution.py:126
  33.7 5.7 %collective-permute-start.15 = (f32[64,256]{1,0:T(8,128)S(1)}, f32[64,256]{1,0:T(8,128)S(1)}, u32[]{:S(2)}, u32[]{:S(2)}) collective-permute-start(f32[64,256]{1,0:T(8,128)S(1)} %add.81), channel_id=1, source_target_pairs={{0,2},{1,3},{2,0},{3,1},{4,6},{5,7},{6,4},{7,5},{8,10},{9,11},{10,... | collective-permute-start | bytes 196616 | tf_op jit(solution)/shard_map/ppermute | solution.py:126
  33.9 8.4 %collective-permute-start.13 = (bf16[192,256]{1,0:T(8,128)(2,1)S(1)}, bf16[192,256]{1,0:T(8,128)(2,1)S(1)}, u32[]{:S(2)}, u32[]{:S(2)}) collective-permute-start(bf16[192,256]{1,0:T(8,128)(2,1)S(1)} %subtract_convert_fusion.1.refs_0_), channel_id=1, source_target_pairs={{0,24},{8,16},{16,8},{24,0},{1,25},{9,17},{17,9},{25,1},{2,26},{10... | collective-permute-start | bytes 294920 | tf_op jit(solution)/shard_map/ppermute | solution.py:95
  35.9 7.2 %collective-permute-start.12 = (bf16[192,256]{1,0:T(8,128)(2,1)S(1)}, bf16[192,256]{1,0:T(8,128)(2,1)S(1)}, u32[]{:S(2)}, u32[]{:S(2)}) collective-permute-start(bf16[192,256]{1,0:T(8,128)(2,1)S(1)} %subtract_convert_fusion.1.refs_0_), channel_id=1, source_target_pairs={{0,16},{8,24},{16,0},{24,8},{1,17},{9,25},{17,1},{25,9},{2,18},{10... | collective-permute-start | bytes 294920 | tf_op jit(solution)/shard_map/ppermute | solution.py:95
  36.4 6.6 %collective-permute-start.11 = (bf16[192,256]{1,0:T(8,128)(2,1)S(1)}, bf16[192,256]{1,0:T(8,128)(2,1)S(1)}, u32[]{:S(2)}, u32[]{:S(2)}) collective-permute-start(bf16[192,256]{1,0:T(8,128)(2,1)S(1)} %subtract_convert_fusion.1.refs_0_), channel_id=1, source_target_pairs={{0,8},{8,0},{16,24},{24,16},{1,9},{9,1},{17,25},{25,17},{2,10},{10... | collective-permute-start | bytes 294920 | tf_op jit(solution)/shard_map/ppermute | solution.py:95
  39.5 5.5 %collective-permute-start.20 = (f32[64,256]{1,0:T(8,128)S(1)}, f32[64,256]{1,0:T(8,128)S(1)}, u32[]{:S(2)}, u32[]{:S(2)}) collective-permute-start(f32[64,256]{1,0:T(8,128)S(1)} %add_add_fusion.5.refs_0_), channel_id=1, source_target_pairs={{0,24},{8,16},{16,8},{24,0},{1,25},{9,17},{17,9},{25,1},{2,26},{10... | collective-permute-start | bytes 196616 | tf_op jit(solution)/shard_map/ppermute | solution.py:95
  41.6 4.4 %collective-permute-start.19 = (f32[64,256]{1,0:T(8,128)S(1)}, f32[64,256]{1,0:T(8,128)S(1)}, u32[]{:S(2)}, u32[]{:S(2)}) collective-permute-start(f32[64,256]{1,0:T(8,128)S(1)} %add_add_fusion.5.refs_0_), channel_id=1, source_target_pairs={{0,16},{8,24},{16,0},{24,8},{1,17},{9,25},{17,1},{25,9},{2,18},{10... | collective-permute-start | bytes 196616 | tf_op jit(solution)/shard_map/ppermute | solution.py:95
  42.4 4.3 %collective-permute-start.18 = (f32[64,256]{1,0:T(8,128)S(1)}, f32[64,256]{1,0:T(8,128)S(1)}, u32[]{:S(2)}, u32[]{:S(2)}) collective-permute-start(f32[64,256]{1,0:T(8,128)S(1)} %add_add_fusion.5.refs_0_), channel_id=1, source_target_pairs={{0,8},{8,0},{16,24},{24,16},{1,9},{9,1},{17,25},{25,17},{2,10},{10... | collective-permute-start | bytes 196616 | tf_op jit(solution)/shard_map/ppermute | solution.py:95
  44.1 9.9 %collective-permute-start.21 = (f32[128,512]{1,0:T(8,128)S(1)}, f32[128,512]{1,0:T(8,128)S(1)}, u32[]{:S(2)}, u32[]{:S(2)}) collective-permute-start(f32[128,512]{1,0:T(8,128)S(1)} %get-tuple-element.69), channel_id=1, source_target_pairs={{0,1},{1,0},{2,3},{3,2},{4,5},{5,4},{6,7},{7,6},{8,9},{9,8},{10,11... | collective-permute-start | bytes 786440 | tf_op jit(solution)/shard_map/ppermute | solution.py:100
  44.1 9.8 %collective-permute-start.22 = (f32[128,512]{1,0:T(8,128)S(1)}, f32[128,512]{1,0:T(8,128)S(1)}, u32[]{:S(2)}, u32[]{:S(2)}) collective-permute-start(f32[128,512]{1,0:T(8,128)S(1)} %get-tuple-element.70), channel_id=1, source_target_pairs={{1,2},{3,4},{5,6},{2,1},{4,3},{6,5},{9,10},{11,12},{13,14},{10,9},... | collective-permute-start | bytes 786440 | tf_op jit(solution)/shard_map/ppermute | solution.py:106
  56.8 5.4 %collective-permute-start.23 = (bf16[192,256]{1,0:T(8,128)(2,1)S(1)}, bf16[192,256]{1,0:T(8,128)(2,1)S(1)}, u32[]{:S(2)}, u32[]{:S(2)}) collective-permute-start(bf16[192,256]{1,0:T(8,128)(2,1)S(1)} %get-tuple-element.72), channel_id=1, source_target_pairs={{0,8},{8,0},{16,24},{24,16},{1,9},{9,1},{17,25},{25,17},{2,10},{10... | collective-permute-start | bytes 294920 | tf_op jit(solution)/shard_map/ppermute | solution.py:95
  57.6 5.6 %collective-permute-start.24 = (bf16[192,256]{1,0:T(8,128)(2,1)S(1)}, bf16[192,256]{1,0:T(8,128)(2,1)S(1)}, u32[]{:S(2)}, u32[]{:S(2)}) collective-permute-start(bf16[192,256]{1,0:T(8,128)(2,1)S(1)} %get-tuple-element.73), channel_id=1, source_target_pairs={{0,16},{8,24},{16,0},{24,8},{1,17},{9,25},{17,1},{25,9},{2,18},{10... | collective-permute-start | bytes 294920 | tf_op jit(solution)/shard_map/ppermute | solution.py:95
  58.8 6.3 %collective-permute-start.25 = (bf16[192,256]{1,0:T(8,128)(2,1)S(1)}, bf16[192,256]{1,0:T(8,128)(2,1)S(1)}, u32[]{:S(2)}, u32[]{:S(2)}) collective-permute-start(bf16[192,256]{1,0:T(8,128)(2,1)S(1)} %get-tuple-element.74), channel_id=1, source_target_pairs={{0,24},{8,16},{16,8},{24,0},{1,25},{9,17},{17,9},{25,1},{2,26},{10... | collective-permute-start | bytes 294920 | tf_op jit(solution)/shard_map/ppermute | solution.py:95
  60.4 10.3 %collective-permute-start.32 = (bf16[128,256]{1,0:T(8,128)(2,1)S(1)}, bf16[128,256]{1,0:T(8,128)(2,1)S(1)}, u32[]{:S(2)}, u32[]{:S(2)}) collective-permute-start(bf16[128,256]{1,0:T(8,128)(2,1)S(1)} %get-tuple-element.79), channel_id=1, source_target_pairs={{1,0},{2,1},{3,2},{4,3},{5,4},{6,5},{7,6},{9,8},{10,9},{11,10},{12... | collective-permute-start | bytes 196616 | tf_op jit(solution)/shard_map/ppermute | solution.py:516
  65.1 6.5 %collective-permute-start.28 = (bf16[192,256]{1,0:T(8,128)(2,1)S(1)}, bf16[192,256]{1,0:T(8,128)(2,1)S(1)}, u32[]{:S(2)}, u32[]{:S(2)}) collective-permute-start(bf16[192,256]{1,0:T(8,128)(2,1)S(1)} %get-tuple-element.77.refs_0_), channel_id=1, source_target_pairs={{0,24},{8,16},{16,8},{24,0},{1,25},{9,17},{17,9},{25,1},{2,26},{10... | collective-permute-start | bytes 294920 | tf_op jit(solution)/shard_map/ppermute | solution.py:95
  67.1 7.0 %collective-permute-start.27 = (bf16[192,256]{1,0:T(8,128)(2,1)S(1)}, bf16[192,256]{1,0:T(8,128)(2,1)S(1)}, u32[]{:S(2)}, u32[]{:S(2)}) collective-permute-start(bf16[192,256]{1,0:T(8,128)(2,1)S(1)} %get-tuple-element.77.refs_0_), channel_id=1, source_target_pairs={{0,16},{8,24},{16,0},{24,8},{1,17},{9,25},{17,1},{25,9},{2,18},{10... | collective-permute-start | bytes 294920 | tf_op jit(solution)/shard_map/ppermute | solution.py:95
  67.7 6.4 %collective-permute-start.26 = (bf16[192,256]{1,0:T(8,128)(2,1)S(1)}, bf16[192,256]{1,0:T(8,128)(2,1)S(1)}, u32[]{:S(2)}, u32[]{:S(2)}) collective-permute-start(bf16[192,256]{1,0:T(8,128)(2,1)S(1)} %get-tuple-element.77.refs_0_), channel_id=1, source_target_pairs={{0,8},{8,0},{16,24},{24,16},{1,9},{9,1},{17,25},{25,17},{2,10},{10... | collective-permute-start | bytes 294920 | tf_op jit(solution)/shard_map/ppermute | solution.py:95
  68.7 12.9 %collective-permute-start.31 = (bf16[192,256]{1,0:T(8,128)(2,1)S(1)}, bf16[192,256]{1,0:T(8,128)(2,1)S(1)}, u32[]{:S(2)}, u32[]{:S(2)}) collective-permute-start(bf16[192,256]{1,0:T(8,128)(2,1)S(1)} %subtract_convert_fusion.refs_0_), channel_id=1, source_target_pairs={{0,24},{8,16},{16,8},{24,0},{1,25},{9,17},{17,9},{25,1},{2,26},{10... | collective-permute-start | bytes 294920 | tf_op jit(solution)/shard_map/ppermute | solution.py:95
  74.4 3.5 %collective-permute-start.37 = (f32[64,256]{1,0:T(8,128)S(1)}, f32[64,256]{1,0:T(8,128)S(1)}, u32[]{:S(2)}, u32[]{:S(2)}) collective-permute-start(f32[64,256]{1,0:T(8,128)S(1)} %get-tuple-element.83), channel_id=1, source_target_pairs={{0,1},{1,0},{2,3},{3,2},{4,5},{5,4},{6,7},{7,6},{8,9},{9,8},{10,11... | collective-permute-start | bytes 196616 | tf_op jit(solution)/shard_map/ppermute | solution.py:100
  75.8 5.0 %collective-permute-start.33 = (f32[64,256]{1,0:T(8,128)S(1)}, f32[64,256]{1,0:T(8,128)S(1)}, u32[]{:S(2)}, u32[]{:S(2)}) collective-permute-start(f32[64,256]{1,0:T(8,128)S(1)} %shard_map.79), channel_id=1, source_target_pairs={{0,1},{1,0},{2,3},{3,2},{4,5},{5,4},{6,7},{7,6},{8,9},{9,8},{10,11... | collective-permute-start | bytes 196616 | tf_op jit(solution)/shard_map/ppermute | solution.py:100
  76.3 6.1 %collective-permute-start.30 = (bf16[192,256]{1,0:T(8,128)(2,1)S(1)}, bf16[192,256]{1,0:T(8,128)(2,1)S(1)}, u32[]{:S(2)}, u32[]{:S(2)}) collective-permute-start(bf16[192,256]{1,0:T(8,128)(2,1)S(1)} %subtract_convert_fusion.refs_0_), channel_id=1, source_target_pairs={{0,16},{8,24},{16,0},{24,8},{1,17},{9,25},{17,1},{25,9},{2,18},{10... | collective-permute-start | bytes 294920 | tf_op jit(solution)/shard_map/ppermute | solution.py:95
  76.9 8.3 %collective-permute-start.29 = (bf16[192,256]{1,0:T(8,128)(2,1)S(1)}, bf16[192,256]{1,0:T(8,128)(2,1)S(1)}, u32[]{:S(2)}, u32[]{:S(2)}) collective-permute-start(bf16[192,256]{1,0:T(8,128)(2,1)S(1)} %subtract_convert_fusion.refs_0_), channel_id=1, source_target_pairs={{0,8},{8,0},{16,24},{24,16},{1,9},{9,1},{17,25},{25,17},{2,10},{10... | collective-permute-start | bytes 294920 | tf_op jit(solution)/shard_map/ppermute | solution.py:95
  78.0 7.3 %collective-permute-start.41 = (f32[64,256]{1,0:T(8,128)S(1)}, f32[64,256]{1,0:T(8,128)S(1)}, u32[]{:S(2)}, u32[]{:S(2)}) collective-permute-start(f32[64,256]{1,0:T(8,128)S(1)} %add.92), channel_id=1, source_target_pairs={{0,6},{1,7},{2,4},{3,5},{4,2},{5,3},{6,0},{7,1},{8,14},{9,15},{10,... | collective-permute-start | bytes 196616 | tf_op jit(solution)/shard_map/ppermute | solution.py:126
  80.7 9.8 %collective-permute-start.40 = (f32[64,256]{1,0:T(8,128)S(1)}, f32[64,256]{1,0:T(8,128)S(1)}, u32[]{:S(2)}, u32[]{:S(2)}) collective-permute-start(f32[64,256]{1,0:T(8,128)S(1)} %add.92), channel_id=1, source_target_pairs={{0,4},{1,5},{2,6},{3,7},{4,0},{5,1},{6,2},{7,3},{8,12},{9,13},{10,... | collective-permute-start | bytes 196616 | tf_op jit(solution)/shard_map/ppermute | solution.py:126
  81.5 10.5 %collective-permute-start.39 = (f32[64,256]{1,0:T(8,128)S(1)}, f32[64,256]{1,0:T(8,128)S(1)}, u32[]{:S(2)}, u32[]{:S(2)}) collective-permute-start(f32[64,256]{1,0:T(8,128)S(1)} %add.92), channel_id=1, source_target_pairs={{0,2},{1,3},{2,0},{3,1},{4,6},{5,7},{6,4},{7,5},{8,10},{9,11},{10,... | collective-permute-start | bytes 196616 | tf_op jit(solution)/shard_map/ppermute | solution.py:126
  82.4 13.7 %collective-permute-start.36 = (f32[64,256]{1,0:T(8,128)S(1)}, f32[64,256]{1,0:T(8,128)S(1)}, u32[]{:S(2)}, u32[]{:S(2)}) collective-permute-start(f32[64,256]{1,0:T(8,128)S(1)} %add.88), channel_id=1, source_target_pairs={{0,6},{1,7},{2,4},{3,5},{4,2},{5,3},{6,0},{7,1},{8,14},{9,15},{10,... | collective-permute-start | bytes 196616 | tf_op jit(solution)/shard_map/ppermute | solution.py:126
  85.2 12.0 %collective-permute-start.35 = (f32[64,256]{1,0:T(8,128)S(1)}, f32[64,256]{1,0:T(8,128)S(1)}, u32[]{:S(2)}, u32[]{:S(2)}) collective-permute-start(f32[64,256]{1,0:T(8,128)S(1)} %add.88), channel_id=1, source_target_pairs={{0,4},{1,5},{2,6},{3,7},{4,0},{5,1},{6,2},{7,3},{8,12},{9,13},{10,... | collective-permute-start | bytes 196616 | tf_op jit(solution)/shard_map/ppermute | solution.py:126
  85.3 12.0 %collective-permute-start.34 = (f32[64,256]{1,0:T(8,128)S(1)}, f32[64,256]{1,0:T(8,128)S(1)}, u32[]{:S(2)}, u32[]{:S(2)}) collective-permute-start(f32[64,256]{1,0:T(8,128)S(1)} %add.88), channel_id=1, source_target_pairs={{0,2},{1,3},{2,0},{3,1},{4,6},{5,7},{6,4},{7,5},{8,10},{9,11},{10,... | collective-permute-start | bytes 196616 | tf_op jit(solution)/shard_map/ppermute | solution.py:126
  92.1 6.4 %collective-permute-start.45 = (f32[64,256]{1,0:T(8,128)S(1)}, f32[64,256]{1,0:T(8,128)S(1)}, u32[]{:S(2)}, u32[]{:S(2)}) collective-permute-start(f32[64,256]{1,0:T(8,128)S(1)} %add_add_fusion.3.refs_0_), channel_id=1, source_target_pairs={{0,24},{8,16},{16,8},{24,0},{1,25},{9,17},{17,9},{25,1},{2,26},{10... | collective-permute-start | bytes 196616 | tf_op jit(solution)/shard_map/ppermute | solution.py:95
  93.8 5.6 %collective-permute-start.44 = (f32[64,256]{1,0:T(8,128)S(1)}, f32[64,256]{1,0:T(8,128)S(1)}, u32[]{:S(2)}, u32[]{:S(2)}) collective-permute-start(f32[64,256]{1,0:T(8,128)S(1)} %add_add_fusion.3.refs_0_), channel_id=1, source_target_pairs={{0,16},{8,24},{16,0},{24,8},{1,17},{9,25},{17,1},{25,9},{2,18},{10... | collective-permute-start | bytes 196616 | tf_op jit(solution)/shard_map/ppermute | solution.py:95
  96.1 5.0 %collective-permute-start.43 = (f32[64,256]{1,0:T(8,128)S(1)}, f32[64,256]{1,0:T(8,128)S(1)}, u32[]{:S(2)}, u32[]{:S(2)}) collective-permute-start(f32[64,256]{1,0:T(8,128)S(1)} %add_add_fusion.3.refs_0_), channel_id=1, source_target_pairs={{0,8},{8,0},{16,24},{24,16},{1,9},{9,1},{17,25},{25,17},{2,10},{10... | collective-permute-start | bytes 196616 | tf_op jit(solution)/shard_map/ppermute | solution.py:95
  101.1 8.3 %collective-permute-start.48 = (f32[64,256]{1,0:T(8,128)S(1)}, f32[64,256]{1,0:T(8,128)S(1)}, u32[]{:S(2)}, u32[]{:S(2)}) collective-permute-start(f32[64,256]{1,0:T(8,128)S(1)} %add.96), channel_id=1, source_target_pairs={{0,6},{1,7},{2,4},{3,5},{4,2},{5,3},{6,0},{7,1},{8,14},{9,15},{10,... | collective-permute-start | bytes 196616 | tf_op jit(solution)/shard_map/ppermute | solution.py:126
  103.0 6.5 %collective-permute-start.47 = (f32[64,256]{1,0:T(8,128)S(1)}, f32[64,256]{1,0:T(8,128)S(1)}, u32[]{:S(2)}, u32[]{:S(2)}) collective-permute-start(f32[64,256]{1,0:T(8,128)S(1)} %add.96), channel_id=1, source_target_pairs={{0,4},{1,5},{2,6},{3,7},{4,0},{5,1},{6,2},{7,3},{8,12},{9,13},{10,... | collective-permute-start | bytes 196616 | tf_op jit(solution)/shard_map/ppermute | solution.py:126
  103.0 6.5 %collective-permute-start.46 = (f32[64,256]{1,0:T(8,128)S(1)}, f32[64,256]{1,0:T(8,128)S(1)}, u32[]{:S(2)}, u32[]{:S(2)}) collective-permute-start(f32[64,256]{1,0:T(8,128)S(1)} %add.96), channel_id=1, source_target_pairs={{0,2},{1,3},{2,0},{3,1},{4,6},{5,7},{6,4},{7,5},{8,10},{9,11},{10,... | collective-permute-start | bytes 196616 | tf_op jit(solution)/shard_map/ppermute | solution.py:126
  109.6 7.3 %collective-permute-start.51 = (f32[128,256]{1,0:T(8,128)S(1)}, f32[128,256]{1,0:T(8,128)S(1)}, u32[]{:S(2)}, u32[]{:S(2)}) collective-permute-start(f32[128,256]{1,0:T(8,128)S(1)} %pad_maximum_fusion.refs_0_), channel_id=1, source_target_pairs={{0,24},{8,16},{16,8},{24,0},{1,25},{9,17},{17,9},{25,1},{2,26},{10... | collective-permute-start | bytes 393224 | tf_op jit(solution)/shard_map/ppermute | solution.py:95
  110.7 7.5 %collective-permute-start.50 = (f32[128,256]{1,0:T(8,128)S(1)}, f32[128,256]{1,0:T(8,128)S(1)}, u32[]{:S(2)}, u32[]{:S(2)}) collective-permute-start(f32[128,256]{1,0:T(8,128)S(1)} %pad_maximum_fusion.refs_0_), channel_id=1, source_target_pairs={{0,16},{8,24},{16,0},{24,8},{1,17},{9,25},{17,1},{25,9},{2,18},{10... | collective-permute-start | bytes 393224 | tf_op jit(solution)/shard_map/ppermute | solution.py:95
  111.7 6.5 %collective-permute-start.49 = (f32[128,256]{1,0:T(8,128)S(1)}, f32[128,256]{1,0:T(8,128)S(1)}, u32[]{:S(2)}, u32[]{:S(2)}) collective-permute-start(f32[128,256]{1,0:T(8,128)S(1)} %pad_maximum_fusion.refs_0_), channel_id=1, source_target_pairs={{0,8},{8,0},{16,24},{24,16},{1,9},{9,1},{17,25},{25,17},{2,10},{10... | collective-permute-start | bytes 393224 | tf_op jit(solution)/shard_map/ppermute | solution.py:95
  (6 other events, 48.5 us)
where the time goes:
time: 121 us; the launch traced here: 120 us
  starting transfers between devices  60.4 us (50%)
  Pallas kernels  29.3 us (24%)
  waiting for transfers between devices  29.3 us (24%)
    ppermute x30, starting transfers between devices, node_swap(): return lax.ppermute(block, 'node', [(i, i ^ step) for i in range(count)])  35.2 us
    pallas_call x13, Pallas kernels, whole(): pl.pallas_call(kernel, out_shape=out_shape, in_specs=[vmem for _ in opera...  22.5 us
    ppermute x30, waiting for transfers between devices, node_swap(): return lax.ppermute(block, 'node', [(i, i ^ step) for i in range(count)])  21.6 us
    ppermute x12, starting transfers between devices, chip_sum(): lax.ppermute(block, 'rows', route)  19.5 us
    ppermute x12, waiting for transfers between devices, chip_sum(): lax.ppermute(block, 'rows', route)  4.94 us
    pallas_call x2, Pallas kernels, from_hbm(): pl.pallas_call(kernel, in_specs=[pl.BlockSpec(memory_space=kind) for kind...  4.82 us
    ppermute x2, starting transfers between devices, next_head(): return lax.ppermute(head, 'rows', [(i + 1, i) for i in range(count - 1)])  2.78 us
    ppermute x6, waiting for transfers between devices, core_swap(): return lax.ppermute(block, 'rows', [(i, i ^ 1) for i in range(count)])  2.74 us
  transfers between devices with their start and end apart: 52, of which 22 were waited for; matrix products, arithmetic and copies ran while one was open for 0% of the time, Pallas kernels for 18%

commit v1 on v0

--- a/solution.py
+++ b/solution.py
@@ -135,11 +135,13 @@
     return weights[:, 0:1] * real - weights[:, 1:2] * imag
 
 
-def emit_messages(vectors, top, bottom, coupling, out_a, out_b):
+def end_products(vectors, block):
+    times = lambda part: jnp.dot(block[part], vectors, preferred_element_type=F32)
+    return jnp.concatenate([times(0), times(1)], 1).astype(BF16)
+
+
+def emit_messages(first, last, coupling, out_a, out_b):
     is_even = lax.rem(lax.axis_index("rows"), 2) == 0
-    times = lambda block: jnp.dot(block, vectors, preferred_element_type=F32)
-    both = lambda rows: jnp.concatenate([times(rows[0]), times(rows[1])], 1).astype(BF16)
-    first, last = both(top), both(bottom)
     last = dot_tn(coupling, last.astype(F32)).astype(BF16)
     out_a[...] = jnp.where(is_even, last, first)
     out_b[...] = jnp.where(is_even, first, last)
@@ -157,9 +159,13 @@
     copies = [pltpu.make_async_copy(*pair, arrived.at[i]) for i, pair in enumerate(pairs)]
     for copy in copies:
         copy.start()
-    for copy in copies:
+    for copy in copies[:4]:
         copy.wait()
-    emit_messages(vectors[...], ends.at[0], ends.at[1], coupling[...], out_a, out_b)
+    first = end_products(vectors[...], ends.at[0])
+    for copy in copies[4:]:
+        copy.wait()
+    last = end_products(vectors[...], ends.at[1])
+    emit_messages(first, last, coupling[...], out_a, out_b)
 
 
 def from_hbm(kernel, outs, scratch, copies, *operands):
@@ -485,7 +491,7 @@
 
 
 def spread_room(columns):
-    return pltpu.VMEM((2 * GROUP * (GROUP + 1), columns // 2), F32)
+    return pltpu.VMEM((2 * GROUP * (GROUP + 1) + GROUP, columns // 2), F32)
 
 
 def first_factor(blocks, order):

time: 121 us -> 121 us (level)
  transfers between devices with their start and end apart: 52 -> 52, of which waited for: 22 -> 23; matrix products, arithmetic and copies ran while one was open for 0% -> 0% of each run, Pallas kernels for 18% -> 18%
where the time goes in v1:
time: 121 us
  starting transfers between devices  61.2 us (51%)
  Pallas kernels  29.3 us (24%)
  waiting for transfers between devices  28.5 us (24%)
    ppermute x30, starting transfers between devices, node_swap(): return lax.ppermute(block, 'node', [(i, i ^ step) for i in range(count)])  34.5 us
    pallas_call x13, Pallas kernels, whole(): pl.pallas_call(kernel, out_shape=out_shape, in_specs=[vmem for _ in opera...  22.5 us
    ppermute x30, waiting for transfers between devices, node_swap(): return lax.ppermute(block, 'node', [(i, i ^ step) for i in range(count)])  21.3 us
    ppermute x12, starting transfers between devices, chip_sum(): lax.ppermute(block, 'rows', route)  20.8 us
    pallas_call x2, Pallas kernels, from_hbm(): pl.pallas_call(kernel, in_specs=[pl.BlockSpec(memory_space=kind) for kind...  4.87 us
    ppermute x12, waiting for transfers between devices, chip_sum(): lax.ppermute(block, 'rows', route)  4.4 us
    ppermute x2, starting transfers between devices, next_head(): return lax.ppermute(head, 'rows', [(i + 1, i) for i in range(count - 1)])  2.78 us
    ppermute x6, waiting for transfers between devices, core_swap(): return lax.ppermute(block, 'rows', [(i, i ^ 1) for i in range(count)])  2.51 us
  transfers between devices with their start and end apart: 52, of which 23 were waited for; matrix products, arithmetic and copies ran while one was open for 0% of the time, Pallas kernels for 18%

profile of v1, /device:TPU:0, one launch (start us, length us, event | category | flops | bytes accessed | tf_op | source)
XLA Modules:
  0.0 120.5 jit_solution(10014156012173276417)
XLA Ops:
  0.6 2.2 %shard_map.68 = (bf16[128,512]{1,0:T(8,128)(2,1)S(1)}, bf16[128,512]{1,0:T(8,128)(2,1)S(1)}, f32[128,128]{1,0:T(8,128)S(1)}, bf16[768,256]{1,0:T(8,128)(2,1)S(1)}) custom-call(bf16[1,2,768,768]{3,2,1,0:T(8,128)(2,1)} %source.3, bf16[768,256]{1,0:T(8,128)(2,1)} %vectors_at.1, f32[768,128]{1,0:T(8,128)} %upper_tiles.3), custom_call_target="tpu_custom_call" | custom-call | flops 100000000 | bytes 1000000 | tf_op jit(solution)/shard_map/pallas_call | solution.py:174
  4.4 2.7 %shard_map.69 = (f32[768,256]{1,0:T(8,128)S(1)}, bf16[1,2,768,768]{3,2,1,0:T(8,128)(2,1)S(1)}, f32[1,2]{1,0:T(1,128)S(1)}) custom-call(f32[1,2]{1,0:T(1,128)} %weights_at.1, bf16[1,2,768,768]{3,2,1,0:T(8,128)(2,1)} %source.3, bf16[768,256]{1,0:T(8,128)(2,1)S(1)} %get-tuple-element.47.vectors, f32[128,128]{1,0:T(8,128)S(1)} %get-tuple-element.48.coupling, ...), custom_call_target="tpu_custom_call" | custom-call | flops 100000000 | bytes 1000000 | tf_op jit(solution)/shard_map/pallas_call | solution.py:174
  8.0 2.9 %collective-permute-start.2 = (bf16[192,256]{1,0:T(8,128)(2,1)S(1)}, bf16[192,256]{1,0:T(8,128)(2,1)S(1)}, u32[]{:S(2)}, u32[]{:S(2)}) collective-permute-start(bf16[192,256]{1,0:T(8,128)(2,1)S(1)} %get-tuple-element.55), channel_id=1, source_target_pairs={{0,8},{8,0},{16,24},{24,16},{1,9},{9,1},{17,25},{25,17},{2,10},{10... | collective-permute-start | bytes 294920 | tf_op jit(solution)/shard_map/ppermute | solution.py:95
  10.9 1.5 %collective-permute-start.3 = (bf16[192,256]{1,0:T(8,128)(2,1)S(1)}, bf16[192,256]{1,0:T(8,128)(2,1)S(1)}, u32[]{:S(2)}, u32[]{:S(2)}) collective-permute-start(bf16[192,256]{1,0:T(8,128)(2,1)S(1)} %get-tuple-element.56), channel_id=1, source_target_pairs={{0,16},{8,24},{16,0},{24,8},{1,17},{9,25},{17,1},{25,9},{2,18},{10... | collective-permute-start | bytes 294920 | tf_op jit(solution)/shard_map/ppermute | solution.py:95
  12.4 1.1 collective-permute-done.2
  13.5 2.0 %collective-permute-done.3 = bf16[192,256]{1,0:T(8,128)(2,1)S(1)} collective-permute-done((bf16[192,256]{1,0:T(8,128)(2,1)S(1)}, bf16[192,256]{1,0:T(8,128)(2,1)S(1)}, u32[]{:S(2)}, u32[]{:S(2)}) %collective-permute-start.3) | collective-permute-done | bytes 98336 | tf_op jit(solution)/shard_map/ppermute | solution.py:95
  15.5 2.5 %collective-permute-done.4 = bf16[192,256]{1,0:T(8,128)(2,1)S(1)} collective-permute-done((bf16[192,256]{1,0:T(8,128)(2,1)S(1)}, bf16[192,256]{1,0:T(8,128)(2,1)S(1)}, u32[]{:S(2)}, u32[]{:S(2)}) %collective-permute-start.4) | collective-permute-done | bytes 98336 | tf_op jit(solution)/shard_map/ppermute | solution.py:95
  18.9 2.2 %collective-permute-start.6 = (bf16[192,256]{1,0:T(8,128)(2,1)S(1)}, bf16[192,256]{1,0:T(8,128)(2,1)S(1)}, u32[]{:S(2)}, u32[]{:S(2)}) collective-permute-start(bf16[192,256]{1,0:T(8,128)(2,1)S(1)} %get-tuple-element.63.refs_0_), channel_id=1, source_target_pairs={{0,16},{8,24},{16,0},{24,8},{1,17},{9,25},{17,1},{25,9},{2,18},{10... | collective-permute-start | bytes 294920 | tf_op jit(solution)/shard_map/ppermute | solution.py:95
  21.6 1.5 %collective-permute-start.8 = (bf16[192,256]{1,0:T(8,128)(2,1)S(1)}, bf16[192,256]{1,0:T(8,128)(2,1)S(1)}, u32[]{:S(2)}, u32[]{:S(2)}) collective-permute-start(bf16[192,256]{1,0:T(8,128)(2,1)S(1)} %get-tuple-element.60), channel_id=1, source_target_pairs={{0,8},{8,0},{16,24},{24,16},{1,9},{9,1},{17,25},{25,17},{2,10},{10... | collective-permute-start | bytes 294920 | tf_op jit(solution)/shard_map/ppermute | solution.py:95
  23.1 1.6 %collective-permute-done.7.refs_3_ = bf16[192,256]{1,0:T(8,128)(2,1)S(1)} collective-permute-done((bf16[192,256]{1,0:T(8,128)(2,1)S(1)}, bf16[192,256]{1,0:T(8,128)(2,1)S(1)}, u32[]{:S(2)}, u32[]{:S(2)}) %collective-permute-start.7) | collective-permute-done | bytes 98336 | tf_op jit(solution)/shard_map/ppermute | solution.py:95
  25.2 1.6 %collective-permute-done.6.refs_2_ = bf16[192,256]{1,0:T(8,128)(2,1)S(1)} collective-permute-done((bf16[192,256]{1,0:T(8,128)(2,1)S(1)}, bf16[192,256]{1,0:T(8,128)(2,1)S(1)}, u32[]{:S(2)}, u32[]{:S(2)}) %collective-permute-start.6) | collective-permute-done | bytes 98336 | tf_op jit(solution)/shard_map/ppermute | solution.py:95
  27.3 1.2 %collective-permute-done.14 = f32[64,256]{1,0:T(8,128)S(1)} collective-permute-done((f32[64,256]{1,0:T(8,128)S(1)}, f32[64,256]{1,0:T(8,128)S(1)}, u32[]{:S(2)}, u32[]{:S(2)}) %collective-permute-start.14) | collective-permute-done | bytes 65568 | tf_op jit(solution)/shard_map/ppermute | solution.py:100
  28.5 4.4 %collective-permute-start.17 = (f32[64,256]{1,0:T(8,128)S(1)}, f32[64,256]{1,0:T(8,128)S(1)}, u32[]{:S(2)}, u32[]{:S(2)}) collective-permute-start(f32[64,256]{1,0:T(8,128)S(1)} %add.81), channel_id=1, source_target_pairs={{0,6},{1,7},{2,4},{3,5},{4,2},{5,3},{6,0},{7,1},{8,14},{9,15},{10,... | collective-permute-start | bytes 196616 | tf_op jit(solution)/shard_map/ppermute | solution.py:126
  34.0 2.0 %collective-permute-start.13 = (bf16[192,256]{1,0:T(8,128)(2,1)S(1)}, bf16[192,256]{1,0:T(8,128)(2,1)S(1)}, u32[]{:S(2)}, u32[]{:S(2)}) collective-permute-start(bf16[192,256]{1,0:T(8,128)(2,1)S(1)} %subtract_convert_fusion.1.refs_0_), channel_id=1, source_target_pairs={{0,24},{8,16},{16,8},{24,0},{1,25},{9,17},{17,9},{25,1},{2,26},{10... | collective-permute-start | bytes 294920 | tf_op jit(solution)/shard_map/ppermute | solution.py:95
  36.5 1.1 collective-permute-start.11
  37.6 2.0 %collective-permute-done.16 = f32[64,256]{1,0:T(8,128)S(1)} collective-permute-done((f32[64,256]{1,0:T(8,128)S(1)}, f32[64,256]{1,0:T(8,128)S(1)}, u32[]{:S(2)}, u32[]{:S(2)}) %collective-permute-start.16) | collective-permute-done | bytes 65568 | tf_op jit(solution)/shard_map/ppermute | solution.py:126
  39.5 2.1 %collective-permute-start.20 = (f32[64,256]{1,0:T(8,128)S(1)}, f32[64,256]{1,0:T(8,128)S(1)}, u32[]{:S(2)}, u32[]{:S(2)}) collective-permute-start(f32[64,256]{1,0:T(8,128)S(1)} %add_add_fusion.5.refs_0_), channel_id=1, source_target_pairs={{0,24},{8,16},{16,8},{24,0},{1,25},{9,17},{17,9},{25,1},{2,26},{10... | collective-permute-start | bytes 196616 | tf_op jit(solution)/shard_map/ppermute | solution.py:95
  46.7 3.9 %shard_map.73 = (f32[128,128]{1,0:T(8,128)S(1)}, f32[128,128]{1,0:T(8,128)S(1)}, f32[128,128]{1,0:T(8,128)S(1)}, f32[1,256]{1,0:T(1,128)S(1)}) custom-call(f32[64,256]{1,0:T(8,128)S(1)} %add_add_fusion.5.refs_0_, f32[64,256]{1,0:T(8,128)S(1)} %collective-permute-done.18.refs_1_, f32[64,256]{1,0:T(8,128)S(1)} %collective-permute-done.19.refs_2_, ...), custom_call_target="tpu_custom_call" | custom-call | flops 6000000000 | bytes 262144 | tf_op jit(solution)/shard_map/pallas_call | solution.py:82
  50.5 3.4 %shard_map.74.factor.refs_4_ = f32[256,256]{1,0:T(8,128)S(1)} custom-call(f32[128,128]{1,0:T(8,128)S(1)} %get-tuple-element.65.top, f32[128,128]{1,0:T(8,128)S(1)} %get-tuple-element.66.corner, f32[128,128]{1,0:T(8,128)S(1)} %get-tuple-element.67.rest, f32[1,256]{1,0:T(1,128)S(1)} %get-tuple-element.68.across), custom_call_target="tpu_custom_call" | custom-call | flops 6000000000 | bytes 197632 | tf_op jit(solution)/shard_map/pallas_call | solution.py:82
  54.0 2.8 %shard_map.76 = (f32[192,256]{1,0:T(8,128)S(1)}, bf16[192,256]{1,0:T(8,128)(2,1)S(1)}, bf16[192,256]{1,0:T(8,128)(2,1)S(1)}, bf16[192,256]{1,0:T(8,128)(2,1)S(1)}) custom-call(f32[1,2]{1,0:T(1,128)S(1)} %get-tuple-element.50.weights, bf16[768,256]{1,0:T(8,128)(2,1)S(1)} %get-tuple-element.58.field, bf16[768,256]{1,0:T(8,128)(2,1)S(1)} %shard_map.72.low, ...), custom_call_target="tpu_custom_call" | custom-call | flops 100000000 | bytes 3997704 | tf_op jit(solution)/shard_map/pallas_call | solution.py:82
  57.6 1.2 %collective-permute-start.24 = (bf16[192,256]{1,0:T(8,128)(2,1)S(1)}, bf16[192,256]{1,0:T(8,128)(2,1)S(1)}, u32[]{:S(2)}, u32[]{:S(2)}) collective-permute-start(bf16[192,256]{1,0:T(8,128)(2,1)S(1)} %get-tuple-element.73), channel_id=1, source_target_pairs={{0,16},{8,24},{16,0},{24,8},{1,17},{9,25},{17,1},{25,9},{2,18},{10... | collective-permute-start | bytes 294920 | tf_op jit(solution)/shard_map/ppermute | solution.py:95
  58.8 1.6 %collective-permute-start.25 = (bf16[192,256]{1,0:T(8,128)(2,1)S(1)}, bf16[192,256]{1,0:T(8,128)(2,1)S(1)}, u32[]{:S(2)}, u32[]{:S(2)}) collective-permute-start(bf16[192,256]{1,0:T(8,128)(2,1)S(1)} %get-tuple-element.74), channel_id=1, source_target_pairs={{0,24},{8,16},{16,8},{24,0},{1,25},{9,17},{17,9},{25,1},{2,26},{10... | collective-permute-start | bytes 294920 | tf_op jit(solution)/shard_map/ppermute | solution.py:95
  60.4 1.3 %collective-permute-start.32 = (bf16[128,256]{1,0:T(8,128)(2,1)S(1)}, bf16[128,256]{1,0:T(8,128)(2,1)S(1)}, u32[]{:S(2)}, u32[]{:S(2)}) collective-permute-start(bf16[128,256]{1,0:T(8,128)(2,1)S(1)} %get-tuple-element.79), channel_id=1, source_target_pairs={{1,0},{2,1},{3,2},{4,3},{5,4},{6,5},{7,6},{9,8},{10,9},{11,10},{12... | collective-permute-start | bytes 196616 | tf_op jit(solution)/shard_map/ppermute | solution.py:522
  63.2 1.9 %collective-permute-done.25 = bf16[192,256]{1,0:T(8,128)(2,1)S(1)} collective-permute-done((bf16[192,256]{1,0:T(8,128)(2,1)S(1)}, bf16[192,256]{1,0:T(8,128)(2,1)S(1)}, u32[]{:S(2)}, u32[]{:S(2)}) %collective-permute-start.25) | collective-permute-done | bytes 98336 | tf_op jit(solution)/shard_map/ppermute | solution.py:95
  65.1 1.9 %collective-permute-start.28 = (bf16[192,256]{1,0:T(8,128)(2,1)S(1)}, bf16[192,256]{1,0:T(8,128)(2,1)S(1)}, u32[]{:S(2)}, u32[]{:S(2)}) collective-permute-start(bf16[192,256]{1,0:T(8,128)(2,1)S(1)} %get-tuple-element.77.refs_0_), channel_id=1, source_target_pairs={{0,24},{8,16},{16,8},{24,0},{1,25},{9,17},{17,9},{25,1},{2,26},{10... | collective-permute-start | bytes 294920 | tf_op jit(solution)/shard_map/ppermute | solution.py:95
  68.7 1.9 %collective-permute-start.31 = (bf16[192,256]{1,0:T(8,128)(2,1)S(1)}, bf16[192,256]{1,0:T(8,128)(2,1)S(1)}, u32[]{:S(2)}, u32[]{:S(2)}) collective-permute-start(bf16[192,256]{1,0:T(8,128)(2,1)S(1)} %subtract_convert_fusion.refs_0_), channel_id=1, source_target_pairs={{0,24},{8,16},{16,8},{24,0},{1,25},{9,17},{17,9},{25,1},{2,26},{10... | collective-permute-start | bytes 294920 | tf_op jit(solution)/shard_map/ppermute | solution.py:95
  71.6 2.5 %collective-permute-done.27.refs_2_ = bf16[192,256]{1,0:T(8,128)(2,1)S(1)} collective-permute-done((bf16[192,256]{1,0:T(8,128)(2,1)S(1)}, bf16[192,256]{1,0:T(8,128)(2,1)S(1)}, u32[]{:S(2)}, u32[]{:S(2)}) %collective-permute-start.27) | collective-permute-done | bytes 98336 | tf_op jit(solution)/shard_map/ppermute | solution.py:95
  74.6 1.2 %shard_map.79 = f32[64,256]{1,0:T(8,128)S(1)} custom-call(bf16[768,256]{1,0:T(8,128)(2,1)S(1)} %get-tuple-element.58.field, bf16[768,256]{1,0:T(8,128)(2,1)S(1)} %shard_map.72.low, bf16[128,256]{1,0:T(8,128)(2,1)S(1)} %collective-permute-done.32.after, f32[768,128]{1,0:T(8,128)S(1)} %copy-done.1, f32[768,128]{1,0:T(8,128)S(1)} %copy-done), custom_call_target="tpu_custom_call" | custom-call | flops 100000000 | bytes 1638400 | tf_op jit(solution)/shard_map/pallas_call | solution.py:82
  77.9 2.8 %collective-permute-start.41 = (f32[64,256]{1,0:T(8,128)S(1)}, f32[64,256]{1,0:T(8,128)S(1)}, u32[]{:S(2)}, u32[]{:S(2)}) collective-permute-start(f32[64,256]{1,0:T(8,128)S(1)} %add.92), channel_id=1, source_target_pairs={{0,6},{1,7},{2,4},{3,5},{4,2},{5,3},{6,0},{7,1},{8,14},{9,15},{10,... | collective-permute-start | bytes 196616 | tf_op jit(solution)/shard_map/ppermute | solution.py:126
  80.7 1.4 %collective-permute-start.40 = (f32[64,256]{1,0:T(8,128)S(1)}, f32[64,256]{1,0:T(8,128)S(1)}, u32[]{:S(2)}, u32[]{:S(2)}) collective-permute-start(f32[64,256]{1,0:T(8,128)S(1)} %add.92), channel_id=1, source_target_pairs={{0,4},{1,5},{2,6},{3,7},{4,0},{5,1},{6,2},{7,3},{8,12},{9,13},{10,... | collective-permute-start | bytes 196616 | tf_op jit(solution)/shard_map/ppermute | solution.py:126
  82.4 2.8 %collective-permute-start.36 = (f32[64,256]{1,0:T(8,128)S(1)}, f32[64,256]{1,0:T(8,128)S(1)}, u32[]{:S(2)}, u32[]{:S(2)}) collective-permute-start(f32[64,256]{1,0:T(8,128)S(1)} %add.88), channel_id=1, source_target_pairs={{0,6},{1,7},{2,4},{3,5},{4,2},{5,3},{6,0},{7,1},{8,14},{9,15},{10,... | collective-permute-start | bytes 196616 | tf_op jit(solution)/shard_map/ppermute | solution.py:126
  85.7 3.2 %collective-permute-start.34 = (f32[64,256]{1,0:T(8,128)S(1)}, f32[64,256]{1,0:T(8,128)S(1)}, u32[]{:S(2)}, u32[]{:S(2)}) collective-permute-start(f32[64,256]{1,0:T(8,128)S(1)} %add.88), channel_id=1, source_target_pairs={{0,2},{1,3},{2,0},{3,1},{4,6},{5,7},{6,4},{7,5},{8,10},{9,11},{10,... | collective-permute-start | bytes 196616 | tf_op jit(solution)/shard_map/ppermute | solution.py:126
  89.0 2.2 %collective-permute-done.40 = f32[64,256]{1,0:T(8,128)S(1)} collective-permute-done((f32[64,256]{1,0:T(8,128)S(1)}, f32[64,256]{1,0:T(8,128)S(1)}, u32[]{:S(2)}, u32[]{:S(2)}) %collective-permute-start.40) | collective-permute-done | bytes 65568 | tf_op jit(solution)/shard_map/ppermute | solution.py:126
  91.1 1.5 %collective-permute-start.38 = (bf16[128,256]{1,0:T(8,128)(2,1)S(1)}, bf16[128,256]{1,0:T(8,128)(2,1)S(1)}, u32[]{:S(2)}, u32[]{:S(2)}) collective-permute-start(bf16[128,256]{1,0:T(8,128)(2,1)S(1)} %get-tuple-element.84), channel_id=1, source_target_pairs={{1,0},{2,1},{3,2},{4,3},{5,4},{6,5},{7,6},{9,8},{10,9},{11,10},{12... | collective-permute-start | bytes 196616 | tf_op jit(solution)/shard_map/ppermute | solution.py:522
  92.7 1.3 %collective-permute-start.45 = (f32[64,256]{1,0:T(8,128)S(1)}, f32[64,256]{1,0:T(8,128)S(1)}, u32[]{:S(2)}, u32[]{:S(2)}) collective-permute-start(f32[64,256]{1,0:T(8,128)S(1)} %add_add_fusion.3.refs_0_), channel_id=1, source_target_pairs={{0,24},{8,16},{16,8},{24,0},{1,25},{9,17},{17,9},{25,1},{2,26},{10... | collective-permute-start | bytes 196616 | tf_op jit(solution)/shard_map/ppermute | solution.py:95
  94.9 1.2 %shard_map.80 = f32[64,256]{1,0:T(8,128)S(1)} custom-call(bf16[768,256]{1,0:T(8,128)(2,1)S(1)} %get-tuple-element.75.field, bf16[768,256]{1,0:T(8,128)(2,1)S(1)} %shard_map.78.low, bf16[128,256]{1,0:T(8,128)(2,1)S(1)} %collective-permute-done.38.after, f32[768,128]{1,0:T(8,128)S(1)} %copy-done.1, f32[768,128]{1,0:T(8,128)S(1)} %copy-done), custom_call_target="tpu_custom_call" | custom-call | flops 100000000 | bytes 1638400 | tf_op jit(solution)/shard_map/pallas_call | solution.py:82
  96.2 1.4 %collective-permute-start.43 = (f32[64,256]{1,0:T(8,128)S(1)}, f32[64,256]{1,0:T(8,128)S(1)}, u32[]{:S(2)}, u32[]{:S(2)}) collective-permute-start(f32[64,256]{1,0:T(8,128)S(1)} %add_add_fusion.3.refs_0_), channel_id=1, source_target_pairs={{0,8},{8,0},{16,24},{24,16},{1,9},{9,1},{17,25},{25,17},{2,10},{10... | collective-permute-start | bytes 196616 | tf_op jit(solution)/shard_map/ppermute | solution.py:95
  98.8 1.2 collective-permute-done.44.refs_2_
  100.0 1.0 collective-permute-done.43.refs_1_
  101.0 2.2 %collective-permute-start.48 = (f32[64,256]{1,0:T(8,128)S(1)}, f32[64,256]{1,0:T(8,128)S(1)}, u32[]{:S(2)}, u32[]{:S(2)}) collective-permute-start(f32[64,256]{1,0:T(8,128)S(1)} %add.96), channel_id=1, source_target_pairs={{0,6},{1,7},{2,4},{3,5},{4,2},{5,3},{6,0},{7,1},{8,14},{9,15},{10,... | collective-permute-start | bytes 196616 | tf_op jit(solution)/shard_map/ppermute | solution.py:126
  103.2 2.2 %collective-permute-start.46 = (f32[64,256]{1,0:T(8,128)S(1)}, f32[64,256]{1,0:T(8,128)S(1)}, u32[]{:S(2)}, u32[]{:S(2)}) collective-permute-start(f32[64,256]{1,0:T(8,128)S(1)} %add.96), channel_id=1, source_target_pairs={{0,2},{1,3},{2,0},{3,1},{4,6},{5,7},{6,4},{7,5},{8,10},{9,11},{10,... | collective-permute-start | bytes 196616 | tf_op jit(solution)/shard_map/ppermute | solution.py:126
  105.4 3.9 %shard_map.81 = (f32[128,128]{1,0:T(8,128)S(1)}, f32[128,128]{1,0:T(8,128)S(1)}, f32[128,128]{1,0:T(8,128)S(1)}, f32[1,256]{1,0:T(1,128)S(1)}) custom-call(f32[64,256]{1,0:T(8,128)S(1)} %add_add_fusion.3.refs_0_, f32[64,256]{1,0:T(8,128)S(1)} %collective-permute-done.43.refs_1_, f32[64,256]{1,0:T(8,128)S(1)} %collective-permute-done.44.refs_2_, ...), custom_call_target="tpu_custom_call" | custom-call | flops 6000000000 | bytes 262144 | tf_op jit(solution)/shard_map/pallas_call | solution.py:82
  109.6 1.3 %collective-permute-start.51 = (f32[128,256]{1,0:T(8,128)S(1)}, f32[128,256]{1,0:T(8,128)S(1)}, u32[]{:S(2)}, u32[]{:S(2)}) collective-permute-start(f32[128,256]{1,0:T(8,128)S(1)} %pad_maximum_fusion.refs_0_), channel_id=1, source_target_pairs={{0,24},{8,16},{16,8},{24,0},{1,25},{9,17},{17,9},{25,1},{2,26},{10... | collective-permute-start | bytes 393224 | tf_op jit(solution)/shard_map/ppermute | solution.py:95
  110.9 1.1 collective-permute-start.50
  112.0 1.2 collective-permute-start.49
  113.1 3.4 %shard_map.82.refs_5_ = f32[256,256]{1,0:T(8,128)S(1)} custom-call(f32[128,128]{1,0:T(8,128)S(1)} %get-tuple-element.87.top, f32[128,128]{1,0:T(8,128)S(1)} %get-tuple-element.88.corner, f32[128,128]{1,0:T(8,128)S(1)} %get-tuple-element.89.rest, f32[1,256]{1,0:T(1,128)S(1)} %get-tuple-element.90.across), custom_call_target="tpu_custom_call" | custom-call | flops 6000000000 | bytes 197632 | tf_op jit(solution)/shard_map/pallas_call | solution.py:82
  116.9 1.4 %collective-permute-done.50.refs_2_ = f32[128,256]{1,0:T(8,128)S(1)} collective-permute-done((f32[128,256]{1,0:T(8,128)S(1)}, f32[128,256]{1,0:T(8,128)S(1)}, u32[]{:S(2)}, u32[]{:S(2)}) %collective-permute-start.50) | collective-permute-done | bytes 131104 | tf_op jit(solution)/shard_map/ppermute | solution.py:95
  118.4 2.0 %finish.1 = (f32[768,256]{1,0:T(8,128)}, f32[2,256,256]{2,1,0:T(8,128)}) custom-call(bf16[768,256]{1,0:T(8,128)(2,1)S(1)} %get-tuple-element.75.field, bf16[768,256]{1,0:T(8,128)(2,1)S(1)} %shard_map.78.low, f32[128,256]{1,0:T(8,128)S(1)} %pad_maximum_fusion.refs_0_, f32[128,256]{1,0:T(8,128)S(1)} %collective-permute-done.49.refs_1_, ...), custom_call_target="tpu_custom_call" | custom-call | flops 1000000000 | bytes 1000000 | tf_op jit(solution)/shard_map/finish/pallas_call | solution.py:592
  (89 shorter events, 22.6 us)
Async XLA Ops:
  3.4 3.7 %collective-permute-start.1 = (bf16[128,512]{1,0:T(8,128)(2,1)S(1)}, bf16[128,512]{1,0:T(8,128)(2,1)S(1)}, u32[]{:S(2)}, u32[]{:S(2)}) collective-permute-start(bf16[128,512]{1,0:T(8,128)(2,1)S(1)} %get-tuple-element.52), channel_id=1, source_target_pairs={{1,2},{3,4},{5,6},{2,1},{4,3},{6,5},{9,10},{11,12},{13,14},{10,9},... | collective-permute-start | bytes 393224 | tf_op jit(solution)/shard_map/ppermute | solution.py:106
  8.0 5.5 %collective-permute-start.2 = (bf16[192,256]{1,0:T(8,128)(2,1)S(1)}, bf16[192,256]{1,0:T(8,128)(2,1)S(1)}, u32[]{:S(2)}, u32[]{:S(2)}) collective-permute-start(bf16[192,256]{1,0:T(8,128)(2,1)S(1)} %get-tuple-element.55), channel_id=1, source_target_pairs={{0,8},{8,0},{16,24},{24,16},{1,9},{9,1},{17,25},{25,17},{2,10},{10... | collective-permute-start | bytes 294920 | tf_op jit(solution)/shard_map/ppermute | solution.py:95
  10.9 4.6 %collective-permute-start.3 = (bf16[192,256]{1,0:T(8,128)(2,1)S(1)}, bf16[192,256]{1,0:T(8,128)(2,1)S(1)}, u32[]{:S(2)}, u32[]{:S(2)}) collective-permute-start(bf16[192,256]{1,0:T(8,128)(2,1)S(1)} %get-tuple-element.56), channel_id=1, source_target_pairs={{0,16},{8,24},{16,0},{24,8},{1,17},{9,25},{17,1},{25,9},{2,18},{10... | collective-permute-start | bytes 294920 | tf_op jit(solution)/shard_map/ppermute | solution.py:95
  12.4 5.6 %collective-permute-start.4 = (bf16[192,256]{1,0:T(8,128)(2,1)S(1)}, bf16[192,256]{1,0:T(8,128)(2,1)S(1)}, u32[]{:S(2)}, u32[]{:S(2)}) collective-permute-start(bf16[192,256]{1,0:T(8,128)(2,1)S(1)} %get-tuple-element.57), channel_id=1, source_target_pairs={{0,24},{8,16},{16,8},{24,0},{1,25},{9,17},{17,9},{25,1},{2,26},{10... | collective-permute-start | bytes 294920 | tf_op jit(solution)/shard_map/ppermute | solution.py:95
  18.1 6.7 %collective-permute-start.7 = (bf16[192,256]{1,0:T(8,128)(2,1)S(1)}, bf16[192,256]{1,0:T(8,128)(2,1)S(1)}, u32[]{:S(2)}, u32[]{:S(2)}) collective-permute-start(bf16[192,256]{1,0:T(8,128)(2,1)S(1)} %get-tuple-element.63.refs_0_), channel_id=1, source_target_pairs={{0,24},{8,16},{16,8},{24,0},{1,25},{9,17},{17,9},{25,1},{2,26},{10... | collective-permute-start | bytes 294920 | tf_op jit(solution)/shard_map/ppermute | solution.py:95
  18.9 7.9 %collective-permute-start.6 = (bf16[192,256]{1,0:T(8,128)(2,1)S(1)}, bf16[192,256]{1,0:T(8,128)(2,1)S(1)}, u32[]{:S(2)}, u32[]{:S(2)}) collective-permute-start(bf16[192,256]{1,0:T(8,128)(2,1)S(1)} %get-tuple-element.63.refs_0_), channel_id=1, source_target_pairs={{0,16},{8,24},{16,0},{24,8},{1,17},{9,25},{17,1},{25,9},{2,18},{10... | collective-permute-start | bytes 294920 | tf_op jit(solution)/shard_map/ppermute | solution.py:95
  21.1 5.7 %collective-permute-start.5 = (bf16[192,256]{1,0:T(8,128)(2,1)S(1)}, bf16[192,256]{1,0:T(8,128)(2,1)S(1)}, u32[]{:S(2)}, u32[]{:S(2)}) collective-permute-start(bf16[192,256]{1,0:T(8,128)(2,1)S(1)} %get-tuple-element.63.refs_0_), channel_id=1, source_target_pairs={{0,8},{8,0},{16,24},{24,16},{1,9},{9,1},{17,25},{25,17},{2,10},{10... | collective-permute-start | bytes 294920 | tf_op jit(solution)/shard_map/ppermute | solution.py:95
  21.6 12.2 %collective-permute-start.8 = (bf16[192,256]{1,0:T(8,128)(2,1)S(1)}, bf16[192,256]{1,0:T(8,128)(2,1)S(1)}, u32[]{:S(2)}, u32[]{:S(2)}) collective-permute-start(bf16[192,256]{1,0:T(8,128)(2,1)S(1)} %get-tuple-element.60), channel_id=1, source_target_pairs={{0,8},{8,0},{16,24},{24,16},{1,9},{9,1},{17,25},{25,17},{2,10},{10... | collective-permute-start | bytes 294920 | tf_op jit(solution)/shard_map/ppermute | solution.py:95
  23.1 10.8 %collective-permute-start.9 = (bf16[192,256]{1,0:T(8,128)(2,1)S(1)}, bf16[192,256]{1,0:T(8,128)(2,1)S(1)}, u32[]{:S(2)}, u32[]{:S(2)}) collective-permute-start(bf16[192,256]{1,0:T(8,128)(2,1)S(1)} %get-tuple-element.61), channel_id=1, source_target_pairs={{0,16},{8,24},{16,0},{24,8},{1,17},{9,25},{17,1},{25,9},{2,18},{10... | collective-permute-start | bytes 294920 | tf_op jit(solution)/shard_map/ppermute | solution.py:95
  24.8 9.2 %collective-permute-start.10 = (bf16[192,256]{1,0:T(8,128)(2,1)S(1)}, bf16[192,256]{1,0:T(8,128)(2,1)S(1)}, u32[]{:S(2)}, u32[]{:S(2)}) collective-permute-start(bf16[192,256]{1,0:T(8,128)(2,1)S(1)} %get-tuple-element.62), channel_id=1, source_target_pairs={{0,24},{8,16},{16,8},{24,0},{1,25},{9,17},{17,9},{25,1},{2,26},{10... | collective-permute-start | bytes 294920 | tf_op jit(solution)/shard_map/ppermute | solution.py:95
  28.5 8.0 %collective-permute-start.17 = (f32[64,256]{1,0:T(8,128)S(1)}, f32[64,256]{1,0:T(8,128)S(1)}, u32[]{:S(2)}, u32[]{:S(2)}) collective-permute-start(f32[64,256]{1,0:T(8,128)S(1)} %add.81), channel_id=1, source_target_pairs={{0,6},{1,7},{2,4},{3,5},{4,2},{5,3},{6,0},{7,1},{8,14},{9,15},{10,... | collective-permute-start | bytes 196616 | tf_op jit(solution)/shard_map/ppermute | solution.py:126
  32.9 6.6 %collective-permute-start.16 = (f32[64,256]{1,0:T(8,128)S(1)}, f32[64,256]{1,0:T(8,128)S(1)}, u32[]{:S(2)}, u32[]{:S(2)}) collective-permute-start(f32[64,256]{1,0:T(8,128)S(1)} %add.81), channel_id=1, source_target_pairs={{0,4},{1,5},{2,6},{3,7},{4,0},{5,1},{6,2},{7,3},{8,12},{9,13},{10,... | collective-permute-start | bytes 196616 | tf_op jit(solution)/shard_map/ppermute | solution.py:126
  33.8 5.7 %collective-permute-start.15 = (f32[64,256]{1,0:T(8,128)S(1)}, f32[64,256]{1,0:T(8,128)S(1)}, u32[]{:S(2)}, u32[]{:S(2)}) collective-permute-start(f32[64,256]{1,0:T(8,128)S(1)} %add.81), channel_id=1, source_target_pairs={{0,2},{1,3},{2,0},{3,1},{4,6},{5,7},{6,4},{7,5},{8,10},{9,11},{10,... | collective-permute-start | bytes 196616 | tf_op jit(solution)/shard_map/ppermute | solution.py:126
  34.0 8.4 %collective-permute-start.13 = (bf16[192,256]{1,0:T(8,128)(2,1)S(1)}, bf16[192,256]{1,0:T(8,128)(2,1)S(1)}, u32[]{:S(2)}, u32[]{:S(2)}) collective-permute-start(bf16[192,256]{1,0:T(8,128)(2,1)S(1)} %subtract_convert_fusion.1.refs_0_), channel_id=1, source_target_pairs={{0,24},{8,16},{16,8},{24,0},{1,25},{9,17},{17,9},{25,1},{2,26},{10... | collective-permute-start | bytes 294920 | tf_op jit(solution)/shard_map/ppermute | solution.py:95
  36.0 7.1 %collective-permute-start.12 = (bf16[192,256]{1,0:T(8,128)(2,1)S(1)}, bf16[192,256]{1,0:T(8,128)(2,1)S(1)}, u32[]{:S(2)}, u32[]{:S(2)}) collective-permute-start(bf16[192,256]{1,0:T(8,128)(2,1)S(1)} %subtract_convert_fusion.1.refs_0_), channel_id=1, source_target_pairs={{0,16},{8,24},{16,0},{24,8},{1,17},{9,25},{17,1},{25,9},{2,18},{10... | collective-permute-start | bytes 294920 | tf_op jit(solution)/shard_map/ppermute | solution.py:95
  36.5 6.6 %collective-permute-start.11 = (bf16[192,256]{1,0:T(8,128)(2,1)S(1)}, bf16[192,256]{1,0:T(8,128)(2,1)S(1)}, u32[]{:S(2)}, u32[]{:S(2)}) collective-permute-start(bf16[192,256]{1,0:T(8,128)(2,1)S(1)} %subtract_convert_fusion.1.refs_0_), channel_id=1, source_target_pairs={{0,8},{8,0},{16,24},{24,16},{1,9},{9,1},{17,25},{25,17},{2,10},{10... | collective-permute-start | bytes 294920 | tf_op jit(solution)/shard_map/ppermute | solution.py:95
  39.5 5.5 %collective-permute-start.20 = (f32[64,256]{1,0:T(8,128)S(1)}, f32[64,256]{1,0:T(8,128)S(1)}, u32[]{:S(2)}, u32[]{:S(2)}) collective-permute-start(f32[64,256]{1,0:T(8,128)S(1)} %add_add_fusion.5.refs_0_), channel_id=1, source_target_pairs={{0,24},{8,16},{16,8},{24,0},{1,25},{9,17},{17,9},{25,1},{2,26},{10... | collective-permute-start | bytes 196616 | tf_op jit(solution)/shard_map/ppermute | solution.py:95
  41.6 4.3 %collective-permute-start.19 = (f32[64,256]{1,0:T(8,128)S(1)}, f32[64,256]{1,0:T(8,128)S(1)}, u32[]{:S(2)}, u32[]{:S(2)}) collective-permute-start(f32[64,256]{1,0:T(8,128)S(1)} %add_add_fusion.5.refs_0_), channel_id=1, source_target_pairs={{0,16},{8,24},{16,0},{24,8},{1,17},{9,25},{17,1},{25,9},{2,18},{10... | collective-permute-start | bytes 196616 | tf_op jit(solution)/shard_map/ppermute | solution.py:95
  42.4 4.3 %collective-permute-start.18 = (f32[64,256]{1,0:T(8,128)S(1)}, f32[64,256]{1,0:T(8,128)S(1)}, u32[]{:S(2)}, u32[]{:S(2)}) collective-permute-start(f32[64,256]{1,0:T(8,128)S(1)} %add_add_fusion.5.refs_0_), channel_id=1, source_target_pairs={{0,8},{8,0},{16,24},{24,16},{1,9},{9,1},{17,25},{25,17},{2,10},{10... | collective-permute-start | bytes 196616 | tf_op jit(solution)/shard_map/ppermute | solution.py:95
  44.1 9.9 %collective-permute-start.21 = (f32[128,512]{1,0:T(8,128)S(1)}, f32[128,512]{1,0:T(8,128)S(1)}, u32[]{:S(2)}, u32[]{:S(2)}) collective-permute-start(f32[128,512]{1,0:T(8,128)S(1)} %get-tuple-element.69), channel_id=1, source_target_pairs={{0,1},{1,0},{2,3},{3,2},{4,5},{5,4},{6,7},{7,6},{8,9},{9,8},{10,11... | collective-permute-start | bytes 786440 | tf_op jit(solution)/shard_map/ppermute | solution.py:100
  44.2 9.9 %collective-permute-start.22 = (f32[128,512]{1,0:T(8,128)S(1)}, f32[128,512]{1,0:T(8,128)S(1)}, u32[]{:S(2)}, u32[]{:S(2)}) collective-permute-start(f32[128,512]{1,0:T(8,128)S(1)} %get-tuple-element.70), channel_id=1, source_target_pairs={{1,2},{3,4},{5,6},{2,1},{4,3},{6,5},{9,10},{11,12},{13,14},{10,9},... | collective-permute-start | bytes 786440 | tf_op jit(solution)/shard_map/ppermute | solution.py:106
  56.9 5.5 %collective-permute-start.23 = (bf16[192,256]{1,0:T(8,128)(2,1)S(1)}, bf16[192,256]{1,0:T(8,128)(2,1)S(1)}, u32[]{:S(2)}, u32[]{:S(2)}) collective-permute-start(bf16[192,256]{1,0:T(8,128)(2,1)S(1)} %get-tuple-element.72), channel_id=1, source_target_pairs={{0,8},{8,0},{16,24},{24,16},{1,9},{9,1},{17,25},{25,17},{2,10},{10... | collective-permute-start | bytes 294920 | tf_op jit(solution)/shard_map/ppermute | solution.py:95
  57.6 5.6 %collective-permute-start.24 = (bf16[192,256]{1,0:T(8,128)(2,1)S(1)}, bf16[192,256]{1,0:T(8,128)(2,1)S(1)}, u32[]{:S(2)}, u32[]{:S(2)}) collective-permute-start(bf16[192,256]{1,0:T(8,128)(2,1)S(1)} %get-tuple-element.73), channel_id=1, source_target_pairs={{0,16},{8,24},{16,0},{24,8},{1,17},{9,25},{17,1},{25,9},{2,18},{10... | collective-permute-start | bytes 294920 | tf_op jit(solution)/shard_map/ppermute | solution.py:95
  58.8 6.3 %collective-permute-start.25 = (bf16[192,256]{1,0:T(8,128)(2,1)S(1)}, bf16[192,256]{1,0:T(8,128)(2,1)S(1)}, u32[]{:S(2)}, u32[]{:S(2)}) collective-permute-start(bf16[192,256]{1,0:T(8,128)(2,1)S(1)} %get-tuple-element.74), channel_id=1, source_target_pairs={{0,24},{8,16},{16,8},{24,0},{1,25},{9,17},{17,9},{25,1},{2,26},{10... | collective-permute-start | bytes 294920 | tf_op jit(solution)/shard_map/ppermute | solution.py:95
  60.4 10.2 %collective-permute-start.32 = (bf16[128,256]{1,0:T(8,128)(2,1)S(1)}, bf16[128,256]{1,0:T(8,128)(2,1)S(1)}, u32[]{:S(2)}, u32[]{:S(2)}) collective-permute-start(bf16[128,256]{1,0:T(8,128)(2,1)S(1)} %get-tuple-element.79), channel_id=1, source_target_pairs={{1,0},{2,1},{3,2},{4,3},{5,4},{6,5},{7,6},{9,8},{10,9},{11,10},{12... | collective-permute-start | bytes 196616 | tf_op jit(solution)/shard_map/ppermute | solution.py:522
  65.1 6.5 %collective-permute-start.28 = (bf16[192,256]{1,0:T(8,128)(2,1)S(1)}, bf16[192,256]{1,0:T(8,128)(2,1)S(1)}, u32[]{:S(2)}, u32[]{:S(2)}) collective-permute-start(bf16[192,256]{1,0:T(8,128)(2,1)S(1)} %get-tuple-element.77.refs_0_), channel_id=1, source_target_pairs={{0,24},{8,16},{16,8},{24,0},{1,25},{9,17},{17,9},{25,1},{2,26},{10... | collective-permute-start | bytes 294920 | tf_op jit(solution)/shard_map/ppermute | solution.py:95
  67.1 7.0 %collective-permute-start.27 = (bf16[192,256]{1,0:T(8,128)(2,1)S(1)}, bf16[192,256]{1,0:T(8,128)(2,1)S(1)}, u32[]{:S(2)}, u32[]{:S(2)}) collective-permute-start(bf16[192,256]{1,0:T(8,128)(2,1)S(1)} %get-tuple-element.77.refs_0_), channel_id=1, source_target_pairs={{0,16},{8,24},{16,0},{24,8},{1,17},{9,25},{17,1},{25,9},{2,18},{10... | collective-permute-start | bytes 294920 | tf_op jit(solution)/shard_map/ppermute | solution.py:95
  67.8 6.3 %collective-permute-start.26 = (bf16[192,256]{1,0:T(8,128)(2,1)S(1)}, bf16[192,256]{1,0:T(8,128)(2,1)S(1)}, u32[]{:S(2)}, u32[]{:S(2)}) collective-permute-start(bf16[192,256]{1,0:T(8,128)(2,1)S(1)} %get-tuple-element.77.refs_0_), channel_id=1, source_target_pairs={{0,8},{8,0},{16,24},{24,16},{1,9},{9,1},{17,25},{25,17},{2,10},{10... | collective-permute-start | bytes 294920 | tf_op jit(solution)/shard_map/ppermute | solution.py:95
  68.7 13.4 %collective-permute-start.31 = (bf16[192,256]{1,0:T(8,128)(2,1)S(1)}, bf16[192,256]{1,0:T(8,128)(2,1)S(1)}, u32[]{:S(2)}, u32[]{:S(2)}) collective-permute-start(bf16[192,256]{1,0:T(8,128)(2,1)S(1)} %subtract_convert_fusion.refs_0_), channel_id=1, source_target_pairs={{0,24},{8,16},{16,8},{24,0},{1,25},{9,17},{17,9},{25,1},{2,26},{10... | collective-permute-start | bytes 294920 | tf_op jit(solution)/shard_map/ppermute | solution.py:95
  74.5 3.4 %collective-permute-start.37 = (f32[64,256]{1,0:T(8,128)S(1)}, f32[64,256]{1,0:T(8,128)S(1)}, u32[]{:S(2)}, u32[]{:S(2)}) collective-permute-start(f32[64,256]{1,0:T(8,128)S(1)} %get-tuple-element.83), channel_id=1, source_target_pairs={{0,1},{1,0},{2,3},{3,2},{4,5},{5,4},{6,7},{7,6},{8,9},{9,8},{10,11... | collective-permute-start | bytes 196616 | tf_op jit(solution)/shard_map/ppermute | solution.py:100
  75.8 4.9 %collective-permute-start.33 = (f32[64,256]{1,0:T(8,128)S(1)}, f32[64,256]{1,0:T(8,128)S(1)}, u32[]{:S(2)}, u32[]{:S(2)}) collective-permute-start(f32[64,256]{1,0:T(8,128)S(1)} %shard_map.79), channel_id=1, source_target_pairs={{0,1},{1,0},{2,3},{3,2},{4,5},{5,4},{6,7},{7,6},{8,9},{9,8},{10,11... | collective-permute-start | bytes 196616 | tf_op jit(solution)/shard_map/ppermute | solution.py:100
  76.3 6.0 %collective-permute-start.30 = (bf16[192,256]{1,0:T(8,128)(2,1)S(1)}, bf16[192,256]{1,0:T(8,128)(2,1)S(1)}, u32[]{:S(2)}, u32[]{:S(2)}) collective-permute-start(bf16[192,256]{1,0:T(8,128)(2,1)S(1)} %subtract_convert_fusion.refs_0_), channel_id=1, source_target_pairs={{0,16},{8,24},{16,0},{24,8},{1,17},{9,25},{17,1},{25,9},{2,18},{10... | collective-permute-start | bytes 294920 | tf_op jit(solution)/shard_map/ppermute | solution.py:95
  76.9 8.3 %collective-permute-start.29 = (bf16[192,256]{1,0:T(8,128)(2,1)S(1)}, bf16[192,256]{1,0:T(8,128)(2,1)S(1)}, u32[]{:S(2)}, u32[]{:S(2)}) collective-permute-start(bf16[192,256]{1,0:T(8,128)(2,1)S(1)} %subtract_convert_fusion.refs_0_), channel_id=1, source_target_pairs={{0,8},{8,0},{16,24},{24,16},{1,9},{9,1},{17,25},{25,17},{2,10},{10... | collective-permute-start | bytes 294920 | tf_op jit(solution)/shard_map/ppermute | solution.py:95
  77.9 7.8 %collective-permute-start.41 = (f32[64,256]{1,0:T(8,128)S(1)}, f32[64,256]{1,0:T(8,128)S(1)}, u32[]{:S(2)}, u32[]{:S(2)}) collective-permute-start(f32[64,256]{1,0:T(8,128)S(1)} %add.92), channel_id=1, source_target_pairs={{0,6},{1,7},{2,4},{3,5},{4,2},{5,3},{6,0},{7,1},{8,14},{9,15},{10,... | collective-permute-start | bytes 196616 | tf_op jit(solution)/shard_map/ppermute | solution.py:126
  80.7 10.4 %collective-permute-start.40 = (f32[64,256]{1,0:T(8,128)S(1)}, f32[64,256]{1,0:T(8,128)S(1)}, u32[]{:S(2)}, u32[]{:S(2)}) collective-permute-start(f32[64,256]{1,0:T(8,128)S(1)} %add.92), channel_id=1, source_target_pairs={{0,4},{1,5},{2,6},{3,7},{4,0},{5,1},{6,2},{7,3},{8,12},{9,13},{10,... | collective-permute-start | bytes 196616 | tf_op jit(solution)/shard_map/ppermute | solution.py:126
  82.1 10.5 %collective-permute-start.39 = (f32[64,256]{1,0:T(8,128)S(1)}, f32[64,256]{1,0:T(8,128)S(1)}, u32[]{:S(2)}, u32[]{:S(2)}) collective-permute-start(f32[64,256]{1,0:T(8,128)S(1)} %add.92), channel_id=1, source_target_pairs={{0,2},{1,3},{2,0},{3,1},{4,6},{5,7},{6,4},{7,5},{8,10},{9,11},{10,... | collective-permute-start | bytes 196616 | tf_op jit(solution)/shard_map/ppermute | solution.py:126
  82.4 13.8 %collective-permute-start.36 = (f32[64,256]{1,0:T(8,128)S(1)}, f32[64,256]{1,0:T(8,128)S(1)}, u32[]{:S(2)}, u32[]{:S(2)}) collective-permute-start(f32[64,256]{1,0:T(8,128)S(1)} %add.88), channel_id=1, source_target_pairs={{0,6},{1,7},{2,4},{3,5},{4,2},{5,3},{6,0},{7,1},{8,14},{9,15},{10,... | collective-permute-start | bytes 196616 | tf_op jit(solution)/shard_map/ppermute | solution.py:126
  85.2 12.4 %collective-permute-start.35 = (f32[64,256]{1,0:T(8,128)S(1)}, f32[64,256]{1,0:T(8,128)S(1)}, u32[]{:S(2)}, u32[]{:S(2)}) collective-permute-start(f32[64,256]{1,0:T(8,128)S(1)} %add.88), channel_id=1, source_target_pairs={{0,4},{1,5},{2,6},{3,7},{4,0},{5,1},{6,2},{7,3},{8,12},{9,13},{10,... | collective-permute-start | bytes 196616 | tf_op jit(solution)/shard_map/ppermute | solution.py:126
  85.7 12.1 %collective-permute-start.34 = (f32[64,256]{1,0:T(8,128)S(1)}, f32[64,256]{1,0:T(8,128)S(1)}, u32[]{:S(2)}, u32[]{:S(2)}) collective-permute-start(f32[64,256]{1,0:T(8,128)S(1)} %add.88), channel_id=1, source_target_pairs={{0,2},{1,3},{2,0},{3,1},{4,6},{5,7},{6,4},{7,5},{8,10},{9,11},{10,... | collective-permute-start | bytes 196616 | tf_op jit(solution)/shard_map/ppermute | solution.py:126
  92.7 6.1 %collective-permute-start.45 = (f32[64,256]{1,0:T(8,128)S(1)}, f32[64,256]{1,0:T(8,128)S(1)}, u32[]{:S(2)}, u32[]{:S(2)}) collective-permute-start(f32[64,256]{1,0:T(8,128)S(1)} %add_add_fusion.3.refs_0_), channel_id=1, source_target_pairs={{0,24},{8,16},{16,8},{24,0},{1,25},{9,17},{17,9},{25,1},{2,26},{10... | collective-permute-start | bytes 196616 | tf_op jit(solution)/shard_map/ppermute | solution.py:95
  94.3 5.7 %collective-permute-start.44 = (f32[64,256]{1,0:T(8,128)S(1)}, f32[64,256]{1,0:T(8,128)S(1)}, u32[]{:S(2)}, u32[]{:S(2)}) collective-permute-start(f32[64,256]{1,0:T(8,128)S(1)} %add_add_fusion.3.refs_0_), channel_id=1, source_target_pairs={{0,16},{8,24},{16,0},{24,8},{1,17},{9,25},{17,1},{25,9},{2,18},{10... | collective-permute-start | bytes 196616 | tf_op jit(solution)/shard_map/ppermute | solution.py:95
  96.2 4.9 %collective-permute-start.43 = (f32[64,256]{1,0:T(8,128)S(1)}, f32[64,256]{1,0:T(8,128)S(1)}, u32[]{:S(2)}, u32[]{:S(2)}) collective-permute-start(f32[64,256]{1,0:T(8,128)S(1)} %add_add_fusion.3.refs_0_), channel_id=1, source_target_pairs={{0,8},{8,0},{16,24},{24,16},{1,9},{9,1},{17,25},{25,17},{2,10},{10... | collective-permute-start | bytes 196616 | tf_op jit(solution)/shard_map/ppermute | solution.py:95
  101.0 8.3 %collective-permute-start.48 = (f32[64,256]{1,0:T(8,128)S(1)}, f32[64,256]{1,0:T(8,128)S(1)}, u32[]{:S(2)}, u32[]{:S(2)}) collective-permute-start(f32[64,256]{1,0:T(8,128)S(1)} %add.96), channel_id=1, source_target_pairs={{0,6},{1,7},{2,4},{3,5},{4,2},{5,3},{6,0},{7,1},{8,14},{9,15},{10,... | collective-permute-start | bytes 196616 | tf_op jit(solution)/shard_map/ppermute | solution.py:126
  103.2 6.4 %collective-permute-start.47 = (f32[64,256]{1,0:T(8,128)S(1)}, f32[64,256]{1,0:T(8,128)S(1)}, u32[]{:S(2)}, u32[]{:S(2)}) collective-permute-start(f32[64,256]{1,0:T(8,128)S(1)} %add.96), channel_id=1, source_target_pairs={{0,4},{1,5},{2,6},{3,7},{4,0},{5,1},{6,2},{7,3},{8,12},{9,13},{10,... | collective-permute-start | bytes 196616 | tf_op jit(solution)/shard_map/ppermute | solution.py:126
  103.2 6.4 %collective-permute-start.46 = (f32[64,256]{1,0:T(8,128)S(1)}, f32[64,256]{1,0:T(8,128)S(1)}, u32[]{:S(2)}, u32[]{:S(2)}) collective-permute-start(f32[64,256]{1,0:T(8,128)S(1)} %add.96), channel_id=1, source_target_pairs={{0,2},{1,3},{2,0},{3,1},{4,6},{5,7},{6,4},{7,5},{8,10},{9,11},{10,... | collective-permute-start | bytes 196616 | tf_op jit(solution)/shard_map/ppermute | solution.py:126
  109.6 7.3 %collective-permute-start.51 = (f32[128,256]{1,0:T(8,128)S(1)}, f32[128,256]{1,0:T(8,128)S(1)}, u32[]{:S(2)}, u32[]{:S(2)}) collective-permute-start(f32[128,256]{1,0:T(8,128)S(1)} %pad_maximum_fusion.refs_0_), channel_id=1, source_target_pairs={{0,24},{8,16},{16,8},{24,0},{1,25},{9,17},{17,9},{25,1},{2,26},{10... | collective-permute-start | bytes 393224 | tf_op jit(solution)/shard_map/ppermute | solution.py:95
  110.9 7.5 %collective-permute-start.50 = (f32[128,256]{1,0:T(8,128)S(1)}, f32[128,256]{1,0:T(8,128)S(1)}, u32[]{:S(2)}, u32[]{:S(2)}) collective-permute-start(f32[128,256]{1,0:T(8,128)S(1)} %pad_maximum_fusion.refs_0_), channel_id=1, source_target_pairs={{0,16},{8,24},{16,0},{24,8},{1,17},{9,25},{17,1},{25,9},{2,18},{10... | collective-permute-start | bytes 393224 | tf_op jit(solution)/shard_map/ppermute | solution.py:95
  112.0 6.4 %collective-permute-start.49 = (f32[128,256]{1,0:T(8,128)S(1)}, f32[128,256]{1,0:T(8,128)S(1)}, u32[]{:S(2)}, u32[]{:S(2)}) collective-permute-start(f32[128,256]{1,0:T(8,128)S(1)} %pad_maximum_fusion.refs_0_), channel_id=1, source_target_pairs={{0,8},{8,0},{16,24},{24,16},{1,9},{9,1},{17,25},{25,17},{2,10},{10... | collective-permute-start | bytes 393224 | tf_op jit(solution)/shard_map/ppermute | solution.py:95
  (6 other events, 48.4 us)

commit v2 on v1

--- a/solution.py
+++ b/solution.py
@@ -556,21 +556,24 @@
     )
 
 
-def finish_kernel(order, field, low, *refs):
-    blocks, factors = refs[: -6 - ITERS], refs[-6 - ITERS : -6]
-    vectors_at, projected_at, vectors, projected, matrix, sent = refs[-6:]
-    rows = field.shape[0]
-    tile = rows // 3 if rows % 48 == 0 else rows
+def last_kernel(field, low, factor, out):
+    out[...] = refined(field[...], low[...], factor[...])
+
+
+def last(field, low, factor):
+    return whole(last_kernel, like(field.shape), field, low, factor)
+
+
+def finish_kernel(order, vectors, *refs):
+    blocks, factors = refs[: -5 - ITERS], refs[-5 - ITERS : -5]
+    vectors_at, projected_at, projected, matrix, sent = refs[-5:]
     copies = []
 
     def send(source, target):
         copies.append(pltpu.make_async_copy(source, target, sent.at[len(copies)]))
         copies[-1].start()
 
-    for at in range(0, rows, tile):
-        span = pl.ds(at, tile)
-        vectors[span] = refined(field[span], low[span], factors[-1][...])
-        send(vectors.at[span], vectors_at.at[span])
+    send(vectors, vectors_at)
     node = lax.axis_index("node")
     size = blocks[0].shape[0] // ITERS
     for k, factor in enumerate(factors):
@@ -584,9 +587,9 @@
         copy.wait()
 
 
-def finish(field, low, blocks, factors, order):
-    rows, columns = field.shape
-    operands = [field, low, *blocks, *factors]
+def finish(vectors, blocks, factors, order):
+    rows, columns = vectors.shape
+    operands = [vectors, *blocks, *factors]
     vmem = pl.BlockSpec(memory_space=pltpu.VMEM)
     shapes = [(rows, columns), (ITERS, columns, columns)]
     return pl.pallas_call(
@@ -594,8 +597,11 @@
         in_specs=[vmem for _ in operands],
         out_specs=[pl.BlockSpec(memory_space=pltpu.HBM)] * 2,
         out_shape=[jax.ShapeDtypeStruct(x, F32) for x in shapes],
-        scratch_shapes=[pltpu.VMEM(x, F32) for x in shapes]
-        + [pltpu.VMEM((columns, columns), F32), pltpu.SemaphoreType.DMA((3 + ITERS,))],
+        scratch_shapes=[
+            pltpu.VMEM(shapes[1], F32),
+            pltpu.VMEM((columns, columns), F32),
+            pltpu.SemaphoreType.DMA((1 + ITERS,)),
+        ],
         cost_estimate=pl.CostEstimate(flops=10**9, bytes_accessed=10**6, transcendentals=0),
         compiler_params=pltpu.CompilerParams(vmem_limit_bytes=GRANT),
         name="finish",
@@ -653,7 +659,8 @@
             spread = [pair] + node_spread([pair] * partners)
         factor = second_factor(halves)
         factors.append(factor)
-    orthonormal, projected = finish(field, low, spread, factors, order)
+    vectors = last(field, low, factor)
+    orthonormal, projected = finish(vectors, spread, factors, order)
     return orthonormal, projected
 
 

time: 121 us -> 120 us (level)
    pallas_call x13 -> x14, Pallas kernels: 22.5 us -> 23 us  [whole(): pl.pallas_call(kernel, out_shape=out_shape, in_specs=[vmem for _ in opera...]
  transfers between devices with their start and end apart: 52 -> 52, of which waited for: 23 -> 22; matrix products, arithmetic and copies ran while one was open for 0% -> 0% of each run, Pallas kernels for 18% -> 18%
where the time goes in v2:
time: 120 us
  starting transfers between devices  61.2 us (51%)
  Pallas kernels  29.5 us (25%)
  waiting for transfers between devices  28 us (23%)
  between operations  1.2 us (1%)
    ppermute x30, starting transfers between devices, node_swap(): return lax.ppermute(block, 'node', [(i, i ^ step) for i in range(count)])  34.5 us
    pallas_call x14, Pallas kernels, whole(): pl.pallas_call(kernel, out_shape=out_shape, in_specs=[vmem for _ in opera...  23 us
    ppermute x12, starting transfers between devices, chip_sum(): lax.ppermute(block, 'rows', route)  20.8 us
    ppermute x30, waiting for transfers between devices, node_swap(): return lax.ppermute(block, 'node', [(i, i ^ step) for i in range(count)])  20.8 us
    pallas_call x2, Pallas kernels, from_hbm(): pl.pallas_call(kernel, in_specs=[pl.BlockSpec(memory_space=kind) for kind...  4.87 us
    ppermute x12, waiting for transfers between devices, chip_sum(): lax.ppermute(block, 'rows', route)  4.41 us
    ppermute x2, starting transfers between devices, next_head(): return lax.ppermute(head, 'rows', [(i + 1, i) for i in range(count - 1)])  2.78 us
    ppermute x6, waiting for transfers between devices, core_swap(): return lax.ppermute(block, 'rows', [(i, i ^ 1) for i in range(count)])  2.51 us
  transfers between devices with their start and end apart: 52, of which 22 were waited for; matrix products, arithmetic and copies ran while one was open for 0% of the time, Pallas kernels for 18%

profile of v2, /device:TPU:0, one launch (start us, length us, event | category | flops | bytes accessed | tf_op | source)
XLA Modules:
  0.0 120.2 jit_solution(9421693583091947617)
XLA Ops:
  0.6 2.2 %shard_map.68 = (bf16[128,512]{1,0:T(8,128)(2,1)S(1)}, bf16[128,512]{1,0:T(8,128)(2,1)S(1)}, f32[128,128]{1,0:T(8,128)S(1)}, bf16[768,256]{1,0:T(8,128)(2,1)S(1)}) custom-call(bf16[1,2,768,768]{3,2,1,0:T(8,128)(2,1)} %source.3, bf16[768,256]{1,0:T(8,128)(2,1)} %vectors_at.1, f32[768,128]{1,0:T(8,128)} %upper_tiles.3), custom_call_target="tpu_custom_call" | custom-call | flops 100000000 | bytes 1000000 | tf_op jit(solution)/shard_map/pallas_call | solution.py:174
  4.4 2.7 %shard_map.69 = (f32[768,256]{1,0:T(8,128)S(1)}, bf16[1,2,768,768]{3,2,1,0:T(8,128)(2,1)S(1)}, f32[1,2]{1,0:T(1,128)S(1)}) custom-call(f32[1,2]{1,0:T(1,128)} %weights_at.1, bf16[1,2,768,768]{3,2,1,0:T(8,128)(2,1)} %source.3, bf16[768,256]{1,0:T(8,128)(2,1)S(1)} %get-tuple-element.47.vectors, f32[128,128]{1,0:T(8,128)S(1)} %get-tuple-element.48.coupling, ...), custom_call_target="tpu_custom_call" | custom-call | flops 100000000 | bytes 1000000 | tf_op jit(solution)/shard_map/pallas_call | solution.py:174
  8.0 2.9 %collective-permute-start.2 = (bf16[192,256]{1,0:T(8,128)(2,1)S(1)}, bf16[192,256]{1,0:T(8,128)(2,1)S(1)}, u32[]{:S(2)}, u32[]{:S(2)}) collective-permute-start(bf16[192,256]{1,0:T(8,128)(2,1)S(1)} %get-tuple-element.55), channel_id=1, source_target_pairs={{0,8},{8,0},{16,24},{24,16},{1,9},{9,1},{17,25},{25,17},{2,10},{10... | collective-permute-start | bytes 294920 | tf_op jit(solution)/shard_map/ppermute | solution.py:95
  10.9 1.5 %collective-permute-start.3 = (bf16[192,256]{1,0:T(8,128)(2,1)S(1)}, bf16[192,256]{1,0:T(8,128)(2,1)S(1)}, u32[]{:S(2)}, u32[]{:S(2)}) collective-permute-start(bf16[192,256]{1,0:T(8,128)(2,1)S(1)} %get-tuple-element.56), channel_id=1, source_target_pairs={{0,16},{8,24},{16,0},{24,8},{1,17},{9,25},{17,1},{25,9},{2,18},{10... | collective-permute-start | bytes 294920 | tf_op jit(solution)/shard_map/ppermute | solution.py:95
  12.4 1.1 collective-permute-done.2
  13.5 2.0 %collective-permute-done.3 = bf16[192,256]{1,0:T(8,128)(2,1)S(1)} collective-permute-done((bf16[192,256]{1,0:T(8,128)(2,1)S(1)}, bf16[192,256]{1,0:T(8,128)(2,1)S(1)}, u32[]{:S(2)}, u32[]{:S(2)}) %collective-permute-start.3) | collective-permute-done | bytes 98336 | tf_op jit(solution)/shard_map/ppermute | solution.py:95
  15.5 2.5 %collective-permute-done.4 = bf16[192,256]{1,0:T(8,128)(2,1)S(1)} collective-permute-done((bf16[192,256]{1,0:T(8,128)(2,1)S(1)}, bf16[192,256]{1,0:T(8,128)(2,1)S(1)}, u32[]{:S(2)}, u32[]{:S(2)}) %collective-permute-start.4) | collective-permute-done | bytes 98336 | tf_op jit(solution)/shard_map/ppermute | solution.py:95
  18.9 2.2 %collective-permute-start.6 = (bf16[192,256]{1,0:T(8,128)(2,1)S(1)}, bf16[192,256]{1,0:T(8,128)(2,1)S(1)}, u32[]{:S(2)}, u32[]{:S(2)}) collective-permute-start(bf16[192,256]{1,0:T(8,128)(2,1)S(1)} %get-tuple-element.63.refs_0_), channel_id=1, source_target_pairs={{0,16},{8,24},{16,0},{24,8},{1,17},{9,25},{17,1},{25,9},{2,18},{10... | collective-permute-start | bytes 294920 | tf_op jit(solution)/shard_map/ppermute | solution.py:95
  21.6 1.5 %collective-permute-start.8 = (bf16[192,256]{1,0:T(8,128)(2,1)S(1)}, bf16[192,256]{1,0:T(8,128)(2,1)S(1)}, u32[]{:S(2)}, u32[]{:S(2)}) collective-permute-start(bf16[192,256]{1,0:T(8,128)(2,1)S(1)} %get-tuple-element.60), channel_id=1, source_target_pairs={{0,8},{8,0},{16,24},{24,16},{1,9},{9,1},{17,25},{25,17},{2,10},{10... | collective-permute-start | bytes 294920 | tf_op jit(solution)/shard_map/ppermute | solution.py:95
  23.1 1.6 %collective-permute-done.7.refs_3_ = bf16[192,256]{1,0:T(8,128)(2,1)S(1)} collective-permute-done((bf16[192,256]{1,0:T(8,128)(2,1)S(1)}, bf16[192,256]{1,0:T(8,128)(2,1)S(1)}, u32[]{:S(2)}, u32[]{:S(2)}) %collective-permute-start.7) | collective-permute-done | bytes 98336 | tf_op jit(solution)/shard_map/ppermute | solution.py:95
  25.2 1.6 %collective-permute-done.6.refs_2_ = bf16[192,256]{1,0:T(8,128)(2,1)S(1)} collective-permute-done((bf16[192,256]{1,0:T(8,128)(2,1)S(1)}, bf16[192,256]{1,0:T(8,128)(2,1)S(1)}, u32[]{:S(2)}, u32[]{:S(2)}) %collective-permute-start.6) | collective-permute-done | bytes 98336 | tf_op jit(solution)/shard_map/ppermute | solution.py:95
  27.3 1.2 %collective-permute-done.14 = f32[64,256]{1,0:T(8,128)S(1)} collective-permute-done((f32[64,256]{1,0:T(8,128)S(1)}, f32[64,256]{1,0:T(8,128)S(1)}, u32[]{:S(2)}, u32[]{:S(2)}) %collective-permute-start.14) | collective-permute-done | bytes 65568 | tf_op jit(solution)/shard_map/ppermute | solution.py:100
  28.5 4.4 %collective-permute-start.17 = (f32[64,256]{1,0:T(8,128)S(1)}, f32[64,256]{1,0:T(8,128)S(1)}, u32[]{:S(2)}, u32[]{:S(2)}) collective-permute-start(f32[64,256]{1,0:T(8,128)S(1)} %add.81), channel_id=1, source_target_pairs={{0,6},{1,7},{2,4},{3,5},{4,2},{5,3},{6,0},{7,1},{8,14},{9,15},{10,... | collective-permute-start | bytes 196616 | tf_op jit(solution)/shard_map/ppermute | solution.py:126
  34.0 2.0 %collective-permute-start.13 = (bf16[192,256]{1,0:T(8,128)(2,1)S(1)}, bf16[192,256]{1,0:T(8,128)(2,1)S(1)}, u32[]{:S(2)}, u32[]{:S(2)}) collective-permute-start(bf16[192,256]{1,0:T(8,128)(2,1)S(1)} %subtract_convert_fusion.1.refs_0_), channel_id=1, source_target_pairs={{0,24},{8,16},{16,8},{24,0},{1,25},{9,17},{17,9},{25,1},{2,26},{10... | collective-permute-start | bytes 294920 | tf_op jit(solution)/shard_map/ppermute | solution.py:95
  36.5 1.1 collective-permute-start.11
  37.6 2.0 %collective-permute-done.16 = f32[64,256]{1,0:T(8,128)S(1)} collective-permute-done((f32[64,256]{1,0:T(8,128)S(1)}, f32[64,256]{1,0:T(8,128)S(1)}, u32[]{:S(2)}, u32[]{:S(2)}) %collective-permute-start.16) | collective-permute-done | bytes 65568 | tf_op jit(solution)/shard_map/ppermute | solution.py:126
  39.5 2.1 %collective-permute-start.20 = (f32[64,256]{1,0:T(8,128)S(1)}, f32[64,256]{1,0:T(8,128)S(1)}, u32[]{:S(2)}, u32[]{:S(2)}) collective-permute-start(f32[64,256]{1,0:T(8,128)S(1)} %add_add_fusion.5.refs_0_), channel_id=1, source_target_pairs={{0,24},{8,16},{16,8},{24,0},{1,25},{9,17},{17,9},{25,1},{2,26},{10... | collective-permute-start | bytes 196616 | tf_op jit(solution)/shard_map/ppermute | solution.py:95
  46.7 3.9 %shard_map.73 = (f32[128,128]{1,0:T(8,128)S(1)}, f32[128,128]{1,0:T(8,128)S(1)}, f32[128,128]{1,0:T(8,128)S(1)}, f32[1,256]{1,0:T(1,128)S(1)}) custom-call(f32[64,256]{1,0:T(8,128)S(1)} %add_add_fusion.5.refs_0_, f32[64,256]{1,0:T(8,128)S(1)} %collective-permute-done.18.refs_1_, f32[64,256]{1,0:T(8,128)S(1)} %collective-permute-done.19.refs_2_, ...), custom_call_target="tpu_custom_call" | custom-call | flops 6000000000 | bytes 262144 | tf_op jit(solution)/shard_map/pallas_call | solution.py:82
  50.5 3.4 %shard_map.74.factor.refs_4_ = f32[256,256]{1,0:T(8,128)S(1)} custom-call(f32[128,128]{1,0:T(8,128)S(1)} %get-tuple-element.65.top, f32[128,128]{1,0:T(8,128)S(1)} %get-tuple-element.66.corner, f32[128,128]{1,0:T(8,128)S(1)} %get-tuple-element.67.rest, f32[1,256]{1,0:T(1,128)S(1)} %get-tuple-element.68.across), custom_call_target="tpu_custom_call" | custom-call | flops 6000000000 | bytes 197632 | tf_op jit(solution)/shard_map/pallas_call | solution.py:82
  54.0 2.8 %shard_map.76 = (f32[192,256]{1,0:T(8,128)S(1)}, bf16[192,256]{1,0:T(8,128)(2,1)S(1)}, bf16[192,256]{1,0:T(8,128)(2,1)S(1)}, bf16[192,256]{1,0:T(8,128)(2,1)S(1)}) custom-call(f32[1,2]{1,0:T(1,128)S(1)} %get-tuple-element.50.weights, bf16[768,256]{1,0:T(8,128)(2,1)S(1)} %get-tuple-element.58.field, bf16[768,256]{1,0:T(8,128)(2,1)S(1)} %shard_map.72.low, ...), custom_call_target="tpu_custom_call" | custom-call | flops 100000000 | bytes 3997704 | tf_op jit(solution)/shard_map/pallas_call | solution.py:82
  57.6 1.2 %collective-permute-start.24 = (bf16[192,256]{1,0:T(8,128)(2,1)S(1)}, bf16[192,256]{1,0:T(8,128)(2,1)S(1)}, u32[]{:S(2)}, u32[]{:S(2)}) collective-permute-start(bf16[192,256]{1,0:T(8,128)(2,1)S(1)} %get-tuple-element.73), channel_id=1, source_target_pairs={{0,16},{8,24},{16,0},{24,8},{1,17},{9,25},{17,1},{25,9},{2,18},{10... | collective-permute-start | bytes 294920 | tf_op jit(solution)/shard_map/ppermute | solution.py:95
  58.8 1.6 %collective-permute-start.25 = (bf16[192,256]{1,0:T(8,128)(2,1)S(1)}, bf16[192,256]{1,0:T(8,128)(2,1)S(1)}, u32[]{:S(2)}, u32[]{:S(2)}) collective-permute-start(bf16[192,256]{1,0:T(8,128)(2,1)S(1)} %get-tuple-element.74), channel_id=1, source_target_pairs={{0,24},{8,16},{16,8},{24,0},{1,25},{9,17},{17,9},{25,1},{2,26},{10... | collective-permute-start | bytes 294920 | tf_op jit(solution)/shard_map/ppermute | solution.py:95
  60.4 1.3 %collective-permute-start.39 = (bf16[128,256]{1,0:T(8,128)(2,1)S(1)}, bf16[128,256]{1,0:T(8,128)(2,1)S(1)}, u32[]{:S(2)}, u32[]{:S(2)}) collective-permute-start(bf16[128,256]{1,0:T(8,128)(2,1)S(1)} %get-tuple-element.84), channel_id=1, source_target_pairs={{1,0},{2,1},{3,2},{4,3},{5,4},{6,5},{7,6},{9,8},{10,9},{11,10},{12... | collective-permute-start | bytes 196616 | tf_op jit(solution)/shard_map/ppermute | solution.py:522
  63.2 1.9 %collective-permute-done.25 = bf16[192,256]{1,0:T(8,128)(2,1)S(1)} collective-permute-done((bf16[192,256]{1,0:T(8,128)(2,1)S(1)}, bf16[192,256]{1,0:T(8,128)(2,1)S(1)}, u32[]{:S(2)}, u32[]{:S(2)}) %collective-permute-start.25) | collective-permute-done | bytes 98336 | tf_op jit(solution)/shard_map/ppermute | solution.py:95
  65.2 1.9 %collective-permute-start.28 = (bf16[192,256]{1,0:T(8,128)(2,1)S(1)}, bf16[192,256]{1,0:T(8,128)(2,1)S(1)}, u32[]{:S(2)}, u32[]{:S(2)}) collective-permute-start(bf16[192,256]{1,0:T(8,128)(2,1)S(1)} %get-tuple-element.77.refs_0_), channel_id=1, source_target_pairs={{0,24},{8,16},{16,8},{24,0},{1,25},{9,17},{17,9},{25,1},{2,26},{10... | collective-permute-start | bytes 294920 | tf_op jit(solution)/shard_map/ppermute | solution.py:95
  68.7 1.9 %collective-permute-start.31 = (bf16[192,256]{1,0:T(8,128)(2,1)S(1)}, bf16[192,256]{1,0:T(8,128)(2,1)S(1)}, u32[]{:S(2)}, u32[]{:S(2)}) collective-permute-start(bf16[192,256]{1,0:T(8,128)(2,1)S(1)} %subtract_convert_fusion.refs_0_), channel_id=1, source_target_pairs={{0,24},{8,16},{16,8},{24,0},{1,25},{9,17},{17,9},{25,1},{2,26},{10... | collective-permute-start | bytes 294920 | tf_op jit(solution)/shard_map/ppermute | solution.py:95
  71.6 2.5 %collective-permute-done.27.refs_2_ = bf16[192,256]{1,0:T(8,128)(2,1)S(1)} collective-permute-done((bf16[192,256]{1,0:T(8,128)(2,1)S(1)}, bf16[192,256]{1,0:T(8,128)(2,1)S(1)}, u32[]{:S(2)}, u32[]{:S(2)}) %collective-permute-start.27) | collective-permute-done | bytes 98336 | tf_op jit(solution)/shard_map/ppermute | solution.py:95
  74.6 1.2 %shard_map.82 = f32[64,256]{1,0:T(8,128)S(1)} custom-call(bf16[768,256]{1,0:T(8,128)(2,1)S(1)} %get-tuple-element.58.field, bf16[768,256]{1,0:T(8,128)(2,1)S(1)} %shard_map.72.low, bf16[128,256]{1,0:T(8,128)(2,1)S(1)} %collective-permute-done.39.after, f32[768,128]{1,0:T(8,128)S(1)} %copy-done.1, f32[768,128]{1,0:T(8,128)S(1)} %copy-done), custom_call_target="tpu_custom_call" | custom-call | flops 100000000 | bytes 1638400 | tf_op jit(solution)/shard_map/pallas_call | solution.py:82
  77.9 2.8 %collective-permute-start.35 = (f32[64,256]{1,0:T(8,128)S(1)}, f32[64,256]{1,0:T(8,128)S(1)}, u32[]{:S(2)}, u32[]{:S(2)}) collective-permute-start(f32[64,256]{1,0:T(8,128)S(1)} %add.88), channel_id=1, source_target_pairs={{0,6},{1,7},{2,4},{3,5},{4,2},{5,3},{6,0},{7,1},{8,14},{9,15},{10,... | collective-permute-start | bytes 196616 | tf_op jit(solution)/shard_map/ppermute | solution.py:126
  80.7 1.4 %collective-permute-start.34 = (f32[64,256]{1,0:T(8,128)S(1)}, f32[64,256]{1,0:T(8,128)S(1)}, u32[]{:S(2)}, u32[]{:S(2)}) collective-permute-start(f32[64,256]{1,0:T(8,128)S(1)} %add.88), channel_id=1, source_target_pairs={{0,4},{1,5},{2,6},{3,7},{4,0},{5,1},{6,2},{7,3},{8,12},{9,13},{10,... | collective-permute-start | bytes 196616 | tf_op jit(solution)/shard_map/ppermute | solution.py:126
  82.4 2.8 %collective-permute-start.43 = (f32[64,256]{1,0:T(8,128)S(1)}, f32[64,256]{1,0:T(8,128)S(1)}, u32[]{:S(2)}, u32[]{:S(2)}) collective-permute-start(f32[64,256]{1,0:T(8,128)S(1)} %add.92), channel_id=1, source_target_pairs={{0,6},{1,7},{2,4},{3,5},{4,2},{5,3},{6,0},{7,1},{8,14},{9,15},{10,... | collective-permute-start | bytes 196616 | tf_op jit(solution)/shard_map/ppermute | solution.py:126
  85.7 3.2 %collective-permute-start.41 = (f32[64,256]{1,0:T(8,128)S(1)}, f32[64,256]{1,0:T(8,128)S(1)}, u32[]{:S(2)}, u32[]{:S(2)}) collective-permute-start(f32[64,256]{1,0:T(8,128)S(1)} %add.92), channel_id=1, source_target_pairs={{0,2},{1,3},{2,0},{3,1},{4,6},{5,7},{6,4},{7,5},{8,10},{9,11},{10,... | collective-permute-start | bytes 196616 | tf_op jit(solution)/shard_map/ppermute | solution.py:126
  89.0 2.1 %collective-permute-done.34 = f32[64,256]{1,0:T(8,128)S(1)} collective-permute-done((f32[64,256]{1,0:T(8,128)S(1)}, f32[64,256]{1,0:T(8,128)S(1)}, u32[]{:S(2)}, u32[]{:S(2)}) %collective-permute-start.34) | collective-permute-done | bytes 65568 | tf_op jit(solution)/shard_map/ppermute | solution.py:126
  91.1 1.5 %collective-permute-start.44 = (bf16[128,256]{1,0:T(8,128)(2,1)S(1)}, bf16[128,256]{1,0:T(8,128)(2,1)S(1)}, u32[]{:S(2)}, u32[]{:S(2)}) collective-permute-start(bf16[128,256]{1,0:T(8,128)(2,1)S(1)} %get-tuple-element.88), channel_id=1, source_target_pairs={{1,0},{2,1},{3,2},{4,3},{5,4},{6,5},{7,6},{9,8},{10,9},{11,10},{12... | collective-permute-start | bytes 196616 | tf_op jit(solution)/shard_map/ppermute | solution.py:522
  92.7 1.3 %collective-permute-start.38 = (f32[64,256]{1,0:T(8,128)S(1)}, f32[64,256]{1,0:T(8,128)S(1)}, u32[]{:S(2)}, u32[]{:S(2)}) collective-permute-start(f32[64,256]{1,0:T(8,128)S(1)} %add_add_fusion.4.refs_0_), channel_id=1, source_target_pairs={{0,24},{8,16},{16,8},{24,0},{1,25},{9,17},{17,9},{25,1},{2,26},{10... | collective-permute-start | bytes 196616 | tf_op jit(solution)/shard_map/ppermute | solution.py:95
  94.9 1.2 %shard_map.83 = f32[64,256]{1,0:T(8,128)S(1)} custom-call(bf16[768,256]{1,0:T(8,128)(2,1)S(1)} %get-tuple-element.75.field, bf16[768,256]{1,0:T(8,128)(2,1)S(1)} %shard_map.78.low, bf16[128,256]{1,0:T(8,128)(2,1)S(1)} %collective-permute-done.44.after, f32[768,128]{1,0:T(8,128)S(1)} %copy-done.1, f32[768,128]{1,0:T(8,128)S(1)} %copy-done), custom_call_target="tpu_custom_call" | custom-call | flops 100000000 | bytes 1638400 | tf_op jit(solution)/shard_map/pallas_call | solution.py:82
  96.2 1.4 %collective-permute-start.36 = (f32[64,256]{1,0:T(8,128)S(1)}, f32[64,256]{1,0:T(8,128)S(1)}, u32[]{:S(2)}, u32[]{:S(2)}) collective-permute-start(f32[64,256]{1,0:T(8,128)S(1)} %add_add_fusion.4.refs_0_), channel_id=1, source_target_pairs={{0,8},{8,0},{16,24},{24,16},{1,9},{9,1},{17,25},{25,17},{2,10},{10... | collective-permute-start | bytes 196616 | tf_op jit(solution)/shard_map/ppermute | solution.py:95
  98.8 1.2 collective-permute-done.37.refs_2_
  100.0 1.0 collective-permute-done.36.refs_1_
  101.0 2.2 %collective-permute-start.48 = (f32[64,256]{1,0:T(8,128)S(1)}, f32[64,256]{1,0:T(8,128)S(1)}, u32[]{:S(2)}, u32[]{:S(2)}) collective-permute-start(f32[64,256]{1,0:T(8,128)S(1)} %add.96), channel_id=1, source_target_pairs={{0,6},{1,7},{2,4},{3,5},{4,2},{5,3},{6,0},{7,1},{8,14},{9,15},{10,... | collective-permute-start | bytes 196616 | tf_op jit(solution)/shard_map/ppermute | solution.py:126
  103.2 2.2 %collective-permute-start.46 = (f32[64,256]{1,0:T(8,128)S(1)}, f32[64,256]{1,0:T(8,128)S(1)}, u32[]{:S(2)}, u32[]{:S(2)}) collective-permute-start(f32[64,256]{1,0:T(8,128)S(1)} %add.96), channel_id=1, source_target_pairs={{0,2},{1,3},{2,0},{3,1},{4,6},{5,7},{6,4},{7,5},{8,10},{9,11},{10,... | collective-permute-start | bytes 196616 | tf_op jit(solution)/shard_map/ppermute | solution.py:126
  105.4 3.9 %shard_map.79 = (f32[128,128]{1,0:T(8,128)S(1)}, f32[128,128]{1,0:T(8,128)S(1)}, f32[128,128]{1,0:T(8,128)S(1)}, f32[1,256]{1,0:T(1,128)S(1)}) custom-call(f32[64,256]{1,0:T(8,128)S(1)} %add_add_fusion.4.refs_0_, f32[64,256]{1,0:T(8,128)S(1)} %collective-permute-done.36.refs_1_, f32[64,256]{1,0:T(8,128)S(1)} %collective-permute-done.37.refs_2_, ...), custom_call_target="tpu_custom_call" | custom-call | flops 6000000000 | bytes 262144 | tf_op jit(solution)/shard_map/pallas_call | solution.py:82
  109.6 1.3 %collective-permute-start.51 = (f32[128,256]{1,0:T(8,128)S(1)}, f32[128,256]{1,0:T(8,128)S(1)}, u32[]{:S(2)}, u32[]{:S(2)}) collective-permute-start(f32[128,256]{1,0:T(8,128)S(1)} %pad_maximum_fusion.refs_0_), channel_id=1, source_target_pairs={{0,24},{8,16},{16,8},{24,0},{1,25},{9,17},{17,9},{25,1},{2,26},{10... | collective-permute-start | bytes 393224 | tf_op jit(solution)/shard_map/ppermute | solution.py:95
  110.9 1.1 collective-permute-start.50
  112.0 1.2 collective-permute-start.49
  113.2 3.4 %shard_map.80.factor.refs_5_ = f32[256,256]{1,0:T(8,128)S(1)} custom-call(f32[128,128]{1,0:T(8,128)S(1)} %get-tuple-element.79.top, f32[128,128]{1,0:T(8,128)S(1)} %get-tuple-element.80.corner, f32[128,128]{1,0:T(8,128)S(1)} %get-tuple-element.81.rest, f32[1,256]{1,0:T(1,128)S(1)} %get-tuple-element.82.across), custom_call_target="tpu_custom_call" | custom-call | flops 6000000000 | bytes 197632 | tf_op jit(solution)/shard_map/pallas_call | solution.py:82
  117.1 1.2 %collective-permute-done.50.refs_2_ = f32[128,256]{1,0:T(8,128)S(1)} collective-permute-done((f32[128,256]{1,0:T(8,128)S(1)}, f32[128,256]{1,0:T(8,128)S(1)}, u32[]{:S(2)}, u32[]{:S(2)}) %collective-permute-start.50) | collective-permute-done | bytes 131104 | tf_op jit(solution)/shard_map/ppermute | solution.py:95
  118.3 1.7 %finish.1 = (f32[768,256]{1,0:T(8,128)}, f32[2,256,256]{2,1,0:T(8,128)}) custom-call(f32[768,256]{1,0:T(8,128)S(1)} %shard_map.81.vectors, f32[128,256]{1,0:T(8,128)S(1)} %pad_maximum_fusion.refs_0_, f32[128,256]{1,0:T(8,128)S(1)} %collective-permute-done.49.refs_1_, f32[128,256]{1,0:T(8,128)S(1)} %collective-permute-done.50.refs_2_, ...), custom_call_target="tpu_custom_call" | custom-call | flops 1000000000 | bytes 1000000 | tf_op jit(solution)/shard_map/finish/pallas_call | solution.py:595
  (90 shorter events, 22.8 us)
Async XLA Ops:
  3.4 3.7 %collective-permute-start.1 = (bf16[128,512]{1,0:T(8,128)(2,1)S(1)}, bf16[128,512]{1,0:T(8,128)(2,1)S(1)}, u32[]{:S(2)}, u32[]{:S(2)}) collective-permute-start(bf16[128,512]{1,0:T(8,128)(2,1)S(1)} %get-tuple-element.52), channel_id=1, source_target_pairs={{1,2},{3,4},{5,6},{2,1},{4,3},{6,5},{9,10},{11,12},{13,14},{10,9},... | collective-permute-start | bytes 393224 | tf_op jit(solution)/shard_map/ppermute | solution.py:106
  8.0 5.5 %collective-permute-start.2 = (bf16[192,256]{1,0:T(8,128)(2,1)S(1)}, bf16[192,256]{1,0:T(8,128)(2,1)S(1)}, u32[]{:S(2)}, u32[]{:S(2)}) collective-permute-start(bf16[192,256]{1,0:T(8,128)(2,1)S(1)} %get-tuple-element.55), channel_id=1, source_target_pairs={{0,8},{8,0},{16,24},{24,16},{1,9},{9,1},{17,25},{25,17},{2,10},{10... | collective-permute-start | bytes 294920 | tf_op jit(solution)/shard_map/ppermute | solution.py:95
  10.9 4.6 %collective-permute-start.3 = (bf16[192,256]{1,0:T(8,128)(2,1)S(1)}, bf16[192,256]{1,0:T(8,128)(2,1)S(1)}, u32[]{:S(2)}, u32[]{:S(2)}) collective-permute-start(bf16[192,256]{1,0:T(8,128)(2,1)S(1)} %get-tuple-element.56), channel_id=1, source_target_pairs={{0,16},{8,24},{16,0},{24,8},{1,17},{9,25},{17,1},{25,9},{2,18},{10... | collective-permute-start | bytes 294920 | tf_op jit(solution)/shard_map/ppermute | solution.py:95
  12.4 5.6 %collective-permute-start.4 = (bf16[192,256]{1,0:T(8,128)(2,1)S(1)}, bf16[192,256]{1,0:T(8,128)(2,1)S(1)}, u32[]{:S(2)}, u32[]{:S(2)}) collective-permute-start(bf16[192,256]{1,0:T(8,128)(2,1)S(1)} %get-tuple-element.57), channel_id=1, source_target_pairs={{0,24},{8,16},{16,8},{24,0},{1,25},{9,17},{17,9},{25,1},{2,26},{10... | collective-permute-start | bytes 294920 | tf_op jit(solution)/shard_map/ppermute | solution.py:95
  18.1 6.7 %collective-permute-start.7 = (bf16[192,256]{1,0:T(8,128)(2,1)S(1)}, bf16[192,256]{1,0:T(8,128)(2,1)S(1)}, u32[]{:S(2)}, u32[]{:S(2)}) collective-permute-start(bf16[192,256]{1,0:T(8,128)(2,1)S(1)} %get-tuple-element.63.refs_0_), channel_id=1, source_target_pairs={{0,24},{8,16},{16,8},{24,0},{1,25},{9,17},{17,9},{25,1},{2,26},{10... | collective-permute-start | bytes 294920 | tf_op jit(solution)/shard_map/ppermute | solution.py:95
  18.9 7.9 %collective-permute-start.6 = (bf16[192,256]{1,0:T(8,128)(2,1)S(1)}, bf16[192,256]{1,0:T(8,128)(2,1)S(1)}, u32[]{:S(2)}, u32[]{:S(2)}) collective-permute-start(bf16[192,256]{1,0:T(8,128)(2,1)S(1)} %get-tuple-element.63.refs_0_), channel_id=1, source_target_pairs={{0,16},{8,24},{16,0},{24,8},{1,17},{9,25},{17,1},{25,9},{2,18},{10... | collective-permute-start | bytes 294920 | tf_op jit(solution)/shard_map/ppermute | solution.py:95
  21.1 5.7 %collective-permute-start.5 = (bf16[192,256]{1,0:T(8,128)(2,1)S(1)}, bf16[192,256]{1,0:T(8,128)(2,1)S(1)}, u32[]{:S(2)}, u32[]{:S(2)}) collective-permute-start(bf16[192,256]{1,0:T(8,128)(2,1)S(1)} %get-tuple-element.63.refs_0_), channel_id=1, source_target_pairs={{0,8},{8,0},{16,24},{24,16},{1,9},{9,1},{17,25},{25,17},{2,10},{10... | collective-permute-start | bytes 294920 | tf_op jit(solution)/shard_map/ppermute | solution.py:95
  21.6 12.2 %collective-permute-start.8 = (bf16[192,256]{1,0:T(8,128)(2,1)S(1)}, bf16[192,256]{1,0:T(8,128)(2,1)S(1)}, u32[]{:S(2)}, u32[]{:S(2)}) collective-permute-start(bf16[192,256]{1,0:T(8,128)(2,1)S(1)} %get-tuple-element.60), channel_id=1, source_target_pairs={{0,8},{8,0},{16,24},{24,16},{1,9},{9,1},{17,25},{25,17},{2,10},{10... | collective-permute-start | bytes 294920 | tf_op jit(solution)/shard_map/ppermute | solution.py:95
  23.1 10.8 %collective-permute-start.9 = (bf16[192,256]{1,0:T(8,128)(2,1)S(1)}, bf16[192,256]{1,0:T(8,128)(2,1)S(1)}, u32[]{:S(2)}, u32[]{:S(2)}) collective-permute-start(bf16[192,256]{1,0:T(8,128)(2,1)S(1)} %get-tuple-element.61), channel_id=1, source_target_pairs={{0,16},{8,24},{16,0},{24,8},{1,17},{9,25},{17,1},{25,9},{2,18},{10... | collective-permute-start | bytes 294920 | tf_op jit(solution)/shard_map/ppermute | solution.py:95
  24.8 9.2 %collective-permute-start.10 = (bf16[192,256]{1,0:T(8,128)(2,1)S(1)}, bf16[192,256]{1,0:T(8,128)(2,1)S(1)}, u32[]{:S(2)}, u32[]{:S(2)}) collective-permute-start(bf16[192,256]{1,0:T(8,128)(2,1)S(1)} %get-tuple-element.62), channel_id=1, source_target_pairs={{0,24},{8,16},{16,8},{24,0},{1,25},{9,17},{17,9},{25,1},{2,26},{10... | collective-permute-start | bytes 294920 | tf_op jit(solution)/shard_map/ppermute | solution.py:95
  28.5 8.0 %collective-permute-start.17 = (f32[64,256]{1,0:T(8,128)S(1)}, f32[64,256]{1,0:T(8,128)S(1)}, u32[]{:S(2)}, u32[]{:S(2)}) collective-permute-start(f32[64,256]{1,0:T(8,128)S(1)} %add.81), channel_id=1, source_target_pairs={{0,6},{1,7},{2,4},{3,5},{4,2},{5,3},{6,0},{7,1},{8,14},{9,15},{10,... | collective-permute-start | bytes 196616 | tf_op jit(solution)/shard_map/ppermute | solution.py:126
  32.9 6.6 %collective-permute-start.16 = (f32[64,256]{1,0:T(8,128)S(1)}, f32[64,256]{1,0:T(8,128)S(1)}, u32[]{:S(2)}, u32[]{:S(2)}) collective-permute-start(f32[64,256]{1,0:T(8,128)S(1)} %add.81), channel_id=1, source_target_pairs={{0,4},{1,5},{2,6},{3,7},{4,0},{5,1},{6,2},{7,3},{8,12},{9,13},{10,... | collective-permute-start | bytes 196616 | tf_op jit(solution)/shard_map/ppermute | solution.py:126
  33.8 5.7 %collective-permute-start.15 = (f32[64,256]{1,0:T(8,128)S(1)}, f32[64,256]{1,0:T(8,128)S(1)}, u32[]{:S(2)}, u32[]{:S(2)}) collective-permute-start(f32[64,256]{1,0:T(8,128)S(1)} %add.81), channel_id=1, source_target_pairs={{0,2},{1,3},{2,0},{3,1},{4,6},{5,7},{6,4},{7,5},{8,10},{9,11},{10,... | collective-permute-start | bytes 196616 | tf_op jit(solution)/shard_map/ppermute | solution.py:126
  34.0 8.4 %collective-permute-start.13 = (bf16[192,256]{1,0:T(8,128)(2,1)S(1)}, bf16[192,256]{1,0:T(8,128)(2,1)S(1)}, u32[]{:S(2)}, u32[]{:S(2)}) collective-permute-start(bf16[192,256]{1,0:T(8,128)(2,1)S(1)} %subtract_convert_fusion.1.refs_0_), channel_id=1, source_target_pairs={{0,24},{8,16},{16,8},{24,0},{1,25},{9,17},{17,9},{25,1},{2,26},{10... | collective-permute-start | bytes 294920 | tf_op jit(solution)/shard_map/ppermute | solution.py:95
  36.0 7.1 %collective-permute-start.12 = (bf16[192,256]{1,0:T(8,128)(2,1)S(1)}, bf16[192,256]{1,0:T(8,128)(2,1)S(1)}, u32[]{:S(2)}, u32[]{:S(2)}) collective-permute-start(bf16[192,256]{1,0:T(8,128)(2,1)S(1)} %subtract_convert_fusion.1.refs_0_), channel_id=1, source_target_pairs={{0,16},{8,24},{16,0},{24,8},{1,17},{9,25},{17,1},{25,9},{2,18},{10... | collective-permute-start | bytes 294920 | tf_op jit(solution)/shard_map/ppermute | solution.py:95
  36.5 6.6 %collective-permute-start.11 = (bf16[192,256]{1,0:T(8,128)(2,1)S(1)}, bf16[192,256]{1,0:T(8,128)(2,1)S(1)}, u32[]{:S(2)}, u32[]{:S(2)}) collective-permute-start(bf16[192,256]{1,0:T(8,128)(2,1)S(1)} %subtract_convert_fusion.1.refs_0_), channel_id=1, source_target_pairs={{0,8},{8,0},{16,24},{24,16},{1,9},{9,1},{17,25},{25,17},{2,10},{10... | collective-permute-start | bytes 294920 | tf_op jit(solution)/shard_map/ppermute | solution.py:95
  39.5 5.5 %collective-permute-start.20 = (f32[64,256]{1,0:T(8,128)S(1)}, f32[64,256]{1,0:T(8,128)S(1)}, u32[]{:S(2)}, u32[]{:S(2)}) collective-permute-start(f32[64,256]{1,0:T(8,128)S(1)} %add_add_fusion.5.refs_0_), channel_id=1, source_target_pairs={{0,24},{8,16},{16,8},{24,0},{1,25},{9,17},{17,9},{25,1},{2,26},{10... | collective-permute-start | bytes 196616 | tf_op jit(solution)/shard_map/ppermute | solution.py:95
  41.6 4.3 %collective-permute-start.19 = (f32[64,256]{1,0:T(8,128)S(1)}, f32[64,256]{1,0:T(8,128)S(1)}, u32[]{:S(2)}, u32[]{:S(2)}) collective-permute-start(f32[64,256]{1,0:T(8,128)S(1)} %add_add_fusion.5.refs_0_), channel_id=1, source_target_pairs={{0,16},{8,24},{16,0},{24,8},{1,17},{9,25},{17,1},{25,9},{2,18},{10... | collective-permute-start | bytes 196616 | tf_op jit(solution)/shard_map/ppermute | solution.py:95
  42.4 4.3 %collective-permute-start.18 = (f32[64,256]{1,0:T(8,128)S(1)}, f32[64,256]{1,0:T(8,128)S(1)}, u32[]{:S(2)}, u32[]{:S(2)}) collective-permute-start(f32[64,256]{1,0:T(8,128)S(1)} %add_add_fusion.5.refs_0_), channel_id=1, source_target_pairs={{0,8},{8,0},{16,24},{24,16},{1,9},{9,1},{17,25},{25,17},{2,10},{10... | collective-permute-start | bytes 196616 | tf_op jit(solution)/shard_map/ppermute | solution.py:95
  44.1 9.9 %collective-permute-start.21 = (f32[128,512]{1,0:T(8,128)S(1)}, f32[128,512]{1,0:T(8,128)S(1)}, u32[]{:S(2)}, u32[]{:S(2)}) collective-permute-start(f32[128,512]{1,0:T(8,128)S(1)} %get-tuple-element.69), channel_id=1, source_target_pairs={{0,1},{1,0},{2,3},{3,2},{4,5},{5,4},{6,7},{7,6},{8,9},{9,8},{10,11... | collective-permute-start | bytes 786440 | tf_op jit(solution)/shard_map/ppermute | solution.py:100
  44.2 9.9 %collective-permute-start.22 = (f32[128,512]{1,0:T(8,128)S(1)}, f32[128,512]{1,0:T(8,128)S(1)}, u32[]{:S(2)}, u32[]{:S(2)}) collective-permute-start(f32[128,512]{1,0:T(8,128)S(1)} %get-tuple-element.70), channel_id=1, source_target_pairs={{1,2},{3,4},{5,6},{2,1},{4,3},{6,5},{9,10},{11,12},{13,14},{10,9},... | collective-permute-start | bytes 786440 | tf_op jit(solution)/shard_map/ppermute | solution.py:106
  56.9 5.5 %collective-permute-start.23 = (bf16[192,256]{1,0:T(8,128)(2,1)S(1)}, bf16[192,256]{1,0:T(8,128)(2,1)S(1)}, u32[]{:S(2)}, u32[]{:S(2)}) collective-permute-start(bf16[192,256]{1,0:T(8,128)(2,1)S(1)} %get-tuple-element.72), channel_id=1, source_target_pairs={{0,8},{8,0},{16,24},{24,16},{1,9},{9,1},{17,25},{25,17},{2,10},{10... | collective-permute-start | bytes 294920 | tf_op jit(solution)/shard_map/ppermute | solution.py:95
  57.6 5.6 %collective-permute-start.24 = (bf16[192,256]{1,0:T(8,128)(2,1)S(1)}, bf16[192,256]{1,0:T(8,128)(2,1)S(1)}, u32[]{:S(2)}, u32[]{:S(2)}) collective-permute-start(bf16[192,256]{1,0:T(8,128)(2,1)S(1)} %get-tuple-element.73), channel_id=1, source_target_pairs={{0,16},{8,24},{16,0},{24,8},{1,17},{9,25},{17,1},{25,9},{2,18},{10... | collective-permute-start | bytes 294920 | tf_op jit(solution)/shard_map/ppermute | solution.py:95
  58.8 6.3 %collective-permute-start.25 = (bf16[192,256]{1,0:T(8,128)(2,1)S(1)}, bf16[192,256]{1,0:T(8,128)(2,1)S(1)}, u32[]{:S(2)}, u32[]{:S(2)}) collective-permute-start(bf16[192,256]{1,0:T(8,128)(2,1)S(1)} %get-tuple-element.74), channel_id=1, source_target_pairs={{0,24},{8,16},{16,8},{24,0},{1,25},{9,17},{17,9},{25,1},{2,26},{10... | collective-permute-start | bytes 294920 | tf_op jit(solution)/shard_map/ppermute | solution.py:95
  60.4 10.3 %collective-permute-start.39 = (bf16[128,256]{1,0:T(8,128)(2,1)S(1)}, bf16[128,256]{1,0:T(8,128)(2,1)S(1)}, u32[]{:S(2)}, u32[]{:S(2)}) collective-permute-start(bf16[128,256]{1,0:T(8,128)(2,1)S(1)} %get-tuple-element.84), channel_id=1, source_target_pairs={{1,0},{2,1},{3,2},{4,3},{5,4},{6,5},{7,6},{9,8},{10,9},{11,10},{12... | collective-permute-start | bytes 196616 | tf_op jit(solution)/shard_map/ppermute | solution.py:522
  65.2 6.5 %collective-permute-start.28 = (bf16[192,256]{1,0:T(8,128)(2,1)S(1)}, bf16[192,256]{1,0:T(8,128)(2,1)S(1)}, u32[]{:S(2)}, u32[]{:S(2)}) collective-permute-start(bf16[192,256]{1,0:T(8,128)(2,1)S(1)} %get-tuple-element.77.refs_0_), channel_id=1, source_target_pairs={{0,24},{8,16},{16,8},{24,0},{1,25},{9,17},{17,9},{25,1},{2,26},{10... | collective-permute-start | bytes 294920 | tf_op jit(solution)/shard_map/ppermute | solution.py:95
  67.1 7.0 %collective-permute-start.27 = (bf16[192,256]{1,0:T(8,128)(2,1)S(1)}, bf16[192,256]{1,0:T(8,128)(2,1)S(1)}, u32[]{:S(2)}, u32[]{:S(2)}) collective-permute-start(bf16[192,256]{1,0:T(8,128)(2,1)S(1)} %get-tuple-element.77.refs_0_), channel_id=1, source_target_pairs={{0,16},{8,24},{16,0},{24,8},{1,17},{9,25},{17,1},{25,9},{2,18},{10... | collective-permute-start | bytes 294920 | tf_op jit(solution)/shard_map/ppermute | solution.py:95
  67.8 6.3 %collective-permute-start.26 = (bf16[192,256]{1,0:T(8,128)(2,1)S(1)}, bf16[192,256]{1,0:T(8,128)(2,1)S(1)}, u32[]{:S(2)}, u32[]{:S(2)}) collective-permute-start(bf16[192,256]{1,0:T(8,128)(2,1)S(1)} %get-tuple-element.77.refs_0_), channel_id=1, source_target_pairs={{0,8},{8,0},{16,24},{24,16},{1,9},{9,1},{17,25},{25,17},{2,10},{10... | collective-permute-start | bytes 294920 | tf_op jit(solution)/shard_map/ppermute | solution.py:95
  68.7 13.4 %collective-permute-start.31 = (bf16[192,256]{1,0:T(8,128)(2,1)S(1)}, bf16[192,256]{1,0:T(8,128)(2,1)S(1)}, u32[]{:S(2)}, u32[]{:S(2)}) collective-permute-start(bf16[192,256]{1,0:T(8,128)(2,1)S(1)} %subtract_convert_fusion.refs_0_), channel_id=1, source_target_pairs={{0,24},{8,16},{16,8},{24,0},{1,25},{9,17},{17,9},{25,1},{2,26},{10... | collective-permute-start | bytes 294920 | tf_op jit(solution)/shard_map/ppermute | solution.py:95
  74.5 3.4 %collective-permute-start.32 = (f32[64,256]{1,0:T(8,128)S(1)}, f32[64,256]{1,0:T(8,128)S(1)}, u32[]{:S(2)}, u32[]{:S(2)}) collective-permute-start(f32[64,256]{1,0:T(8,128)S(1)} %get-tuple-element.78), channel_id=1, source_target_pairs={{0,1},{1,0},{2,3},{3,2},{4,5},{5,4},{6,7},{7,6},{8,9},{9,8},{10,11... | collective-permute-start | bytes 196616 | tf_op jit(solution)/shard_map/ppermute | solution.py:100
  75.8 4.9 %collective-permute-start.40 = (f32[64,256]{1,0:T(8,128)S(1)}, f32[64,256]{1,0:T(8,128)S(1)}, u32[]{:S(2)}, u32[]{:S(2)}) collective-permute-start(f32[64,256]{1,0:T(8,128)S(1)} %shard_map.82), channel_id=1, source_target_pairs={{0,1},{1,0},{2,3},{3,2},{4,5},{5,4},{6,7},{7,6},{8,9},{9,8},{10,11... | collective-permute-start | bytes 196616 | tf_op jit(solution)/shard_map/ppermute | solution.py:100
  76.3 6.0 %collective-permute-start.30 = (bf16[192,256]{1,0:T(8,128)(2,1)S(1)}, bf16[192,256]{1,0:T(8,128)(2,1)S(1)}, u32[]{:S(2)}, u32[]{:S(2)}) collective-permute-start(bf16[192,256]{1,0:T(8,128)(2,1)S(1)} %subtract_convert_fusion.refs_0_), channel_id=1, source_target_pairs={{0,16},{8,24},{16,0},{24,8},{1,17},{9,25},{17,1},{25,9},{2,18},{10... | collective-permute-start | bytes 294920 | tf_op jit(solution)/shard_map/ppermute | solution.py:95
  76.9 8.2 %collective-permute-start.29 = (bf16[192,256]{1,0:T(8,128)(2,1)S(1)}, bf16[192,256]{1,0:T(8,128)(2,1)S(1)}, u32[]{:S(2)}, u32[]{:S(2)}) collective-permute-start(bf16[192,256]{1,0:T(8,128)(2,1)S(1)} %subtract_convert_fusion.refs_0_), channel_id=1, source_target_pairs={{0,8},{8,0},{16,24},{24,16},{1,9},{9,1},{17,25},{25,17},{2,10},{10... | collective-permute-start | bytes 294920 | tf_op jit(solution)/shard_map/ppermute | solution.py:95
  77.9 7.8 %collective-permute-start.35 = (f32[64,256]{1,0:T(8,128)S(1)}, f32[64,256]{1,0:T(8,128)S(1)}, u32[]{:S(2)}, u32[]{:S(2)}) collective-permute-start(f32[64,256]{1,0:T(8,128)S(1)} %add.88), channel_id=1, source_target_pairs={{0,6},{1,7},{2,4},{3,5},{4,2},{5,3},{6,0},{7,1},{8,14},{9,15},{10,... | collective-permute-start | bytes 196616 | tf_op jit(solution)/shard_map/ppermute | solution.py:126
  80.7 10.4 %collective-permute-start.34 = (f32[64,256]{1,0:T(8,128)S(1)}, f32[64,256]{1,0:T(8,128)S(1)}, u32[]{:S(2)}, u32[]{:S(2)}) collective-permute-start(f32[64,256]{1,0:T(8,128)S(1)} %add.88), channel_id=1, source_target_pairs={{0,4},{1,5},{2,6},{3,7},{4,0},{5,1},{6,2},{7,3},{8,12},{9,13},{10,... | collective-permute-start | bytes 196616 | tf_op jit(solution)/shard_map/ppermute | solution.py:126
  82.1 10.5 %collective-permute-start.33 = (f32[64,256]{1,0:T(8,128)S(1)}, f32[64,256]{1,0:T(8,128)S(1)}, u32[]{:S(2)}, u32[]{:S(2)}) collective-permute-start(f32[64,256]{1,0:T(8,128)S(1)} %add.88), channel_id=1, source_target_pairs={{0,2},{1,3},{2,0},{3,1},{4,6},{5,7},{6,4},{7,5},{8,10},{9,11},{10,... | collective-permute-start | bytes 196616 | tf_op jit(solution)/shard_map/ppermute | solution.py:126
  82.4 13.8 %collective-permute-start.43 = (f32[64,256]{1,0:T(8,128)S(1)}, f32[64,256]{1,0:T(8,128)S(1)}, u32[]{:S(2)}, u32[]{:S(2)}) collective-permute-start(f32[64,256]{1,0:T(8,128)S(1)} %add.92), channel_id=1, source_target_pairs={{0,6},{1,7},{2,4},{3,5},{4,2},{5,3},{6,0},{7,1},{8,14},{9,15},{10,... | collective-permute-start | bytes 196616 | tf_op jit(solution)/shard_map/ppermute | solution.py:126
  85.2 12.4 %collective-permute-start.42 = (f32[64,256]{1,0:T(8,128)S(1)}, f32[64,256]{1,0:T(8,128)S(1)}, u32[]{:S(2)}, u32[]{:S(2)}) collective-permute-start(f32[64,256]{1,0:T(8,128)S(1)} %add.92), channel_id=1, source_target_pairs={{0,4},{1,5},{2,6},{3,7},{4,0},{5,1},{6,2},{7,3},{8,12},{9,13},{10,... | collective-permute-start | bytes 196616 | tf_op jit(solution)/shard_map/ppermute | solution.py:126
  85.7 12.1 %collective-permute-start.41 = (f32[64,256]{1,0:T(8,128)S(1)}, f32[64,256]{1,0:T(8,128)S(1)}, u32[]{:S(2)}, u32[]{:S(2)}) collective-permute-start(f32[64,256]{1,0:T(8,128)S(1)} %add.92), channel_id=1, source_target_pairs={{0,2},{1,3},{2,0},{3,1},{4,6},{5,7},{6,4},{7,5},{8,10},{9,11},{10,... | collective-permute-start | bytes 196616 | tf_op jit(solution)/shard_map/ppermute | solution.py:126
  92.7 6.1 %collective-permute-start.38 = (f32[64,256]{1,0:T(8,128)S(1)}, f32[64,256]{1,0:T(8,128)S(1)}, u32[]{:S(2)}, u32[]{:S(2)}) collective-permute-start(f32[64,256]{1,0:T(8,128)S(1)} %add_add_fusion.4.refs_0_), channel_id=1, source_target_pairs={{0,24},{8,16},{16,8},{24,0},{1,25},{9,17},{17,9},{25,1},{2,26},{10... | collective-permute-start | bytes 196616 | tf_op jit(solution)/shard_map/ppermute | solution.py:95
  94.3 5.7 %collective-permute-start.37 = (f32[64,256]{1,0:T(8,128)S(1)}, f32[64,256]{1,0:T(8,128)S(1)}, u32[]{:S(2)}, u32[]{:S(2)}) collective-permute-start(f32[64,256]{1,0:T(8,128)S(1)} %add_add_fusion.4.refs_0_), channel_id=1, source_target_pairs={{0,16},{8,24},{16,0},{24,8},{1,17},{9,25},{17,1},{25,9},{2,18},{10... | collective-permute-start | bytes 196616 | tf_op jit(solution)/shard_map/ppermute | solution.py:95
  96.2 4.9 %collective-permute-start.36 = (f32[64,256]{1,0:T(8,128)S(1)}, f32[64,256]{1,0:T(8,128)S(1)}, u32[]{:S(2)}, u32[]{:S(2)}) collective-permute-start(f32[64,256]{1,0:T(8,128)S(1)} %add_add_fusion.4.refs_0_), channel_id=1, source_target_pairs={{0,8},{8,0},{16,24},{24,16},{1,9},{9,1},{17,25},{25,17},{2,10},{10... | collective-permute-start | bytes 196616 | tf_op jit(solution)/shard_map/ppermute | solution.py:95
  101.0 8.3 %collective-permute-start.48 = (f32[64,256]{1,0:T(8,128)S(1)}, f32[64,256]{1,0:T(8,128)S(1)}, u32[]{:S(2)}, u32[]{:S(2)}) collective-permute-start(f32[64,256]{1,0:T(8,128)S(1)} %add.96), channel_id=1, source_target_pairs={{0,6},{1,7},{2,4},{3,5},{4,2},{5,3},{6,0},{7,1},{8,14},{9,15},{10,... | collective-permute-start | bytes 196616 | tf_op jit(solution)/shard_map/ppermute | solution.py:126
  103.2 6.4 %collective-permute-start.47 = (f32[64,256]{1,0:T(8,128)S(1)}, f32[64,256]{1,0:T(8,128)S(1)}, u32[]{:S(2)}, u32[]{:S(2)}) collective-permute-start(f32[64,256]{1,0:T(8,128)S(1)} %add.96), channel_id=1, source_target_pairs={{0,4},{1,5},{2,6},{3,7},{4,0},{5,1},{6,2},{7,3},{8,12},{9,13},{10,... | collective-permute-start | bytes 196616 | tf_op jit(solution)/shard_map/ppermute | solution.py:126
  103.2 6.4 %collective-permute-start.46 = (f32[64,256]{1,0:T(8,128)S(1)}, f32[64,256]{1,0:T(8,128)S(1)}, u32[]{:S(2)}, u32[]{:S(2)}) collective-permute-start(f32[64,256]{1,0:T(8,128)S(1)} %add.96), channel_id=1, source_target_pairs={{0,2},{1,3},{2,0},{3,1},{4,6},{5,7},{6,4},{7,5},{8,10},{9,11},{10,... | collective-permute-start | bytes 196616 | tf_op jit(solution)/shard_map/ppermute | solution.py:126
  109.6 7.5 %collective-permute-start.51 = (f32[128,256]{1,0:T(8,128)S(1)}, f32[128,256]{1,0:T(8,128)S(1)}, u32[]{:S(2)}, u32[]{:S(2)}) collective-permute-start(f32[128,256]{1,0:T(8,128)S(1)} %pad_maximum_fusion.refs_0_), channel_id=1, source_target_pairs={{0,24},{8,16},{16,8},{24,0},{1,25},{9,17},{17,9},{25,1},{2,26},{10... | collective-permute-start | bytes 393224 | tf_op jit(solution)/shard_map/ppermute | solution.py:95
  110.9 7.4 %collective-permute-start.50 = (f32[128,256]{1,0:T(8,128)S(1)}, f32[128,256]{1,0:T(8,128)S(1)}, u32[]{:S(2)}, u32[]{:S(2)}) collective-permute-start(f32[128,256]{1,0:T(8,128)S(1)} %pad_maximum_fusion.refs_0_), channel_id=1, source_target_pairs={{0,16},{8,24},{16,0},{24,8},{1,17},{9,25},{17,1},{25,9},{2,18},{10... | collective-permute-start | bytes 393224 | tf_op jit(solution)/shard_map/ppermute | solution.py:95
  112.0 6.4 %collective-permute-start.49 = (f32[128,256]{1,0:T(8,128)S(1)}, f32[128,256]{1,0:T(8,128)S(1)}, u32[]{:S(2)}, u32[]{:S(2)}) collective-permute-start(f32[128,256]{1,0:T(8,128)S(1)} %pad_maximum_fusion.refs_0_), channel_id=1, source_target_pairs={{0,8},{8,0},{16,24},{24,16},{1,9},{9,1},{17,25},{25,17},{2,10},{10... | collective-permute-start | bytes 393224 | tf_op jit(solution)/shard_map/ppermute | solution.py:95
  (6 other events, 48.4 us)

commit v3 on v2

--- a/solution.py
+++ b/solution.py
@@ -526,14 +526,17 @@
     band = after.shape[0]
     tiles = field.shape[0] // band
 
-    def values(at):
-        return field[at].astype(F32) + low[at].astype(F32)
-
     for t in range(tiles):
         at = slice(t * band, (t + 1) * band)
-        following = slice((t + 1) * band, (t + 2) * band)
-        following = after[...].astype(F32) if t == tiles - 1 else values(following)
-        image[at] = 0.5 * dot_three(diag_tiles[at], values(at)) + dot_three(upper_tiles[at], following)
+        if t < tiles - 1:
+            both = slice(t * band, (t + 2) * band)
+            high, rest = field[both], low[both]
+        else:
+            high = jnp.concatenate([field[at], after[...]], 0)
+            rest = jnp.concatenate([low[at], jnp.zeros(after.shape, BF16)], 0)
+        left, remainder = halves_of(jnp.concatenate([0.5 * diag_tiles[at], upper_tiles[at]], 1))
+        times = lambda x, y: jnp.dot(x, y, preferred_element_type=F32)
+        image[at] = times(left, high) + (times(left, rest) + times(remainder, high))
     matrix[...] = dot_two(field[...], image[...], TN)
     matrix[...] += lax.dot_general(
         low[...], image[...].astype(BF16), TN, preferred_element_type=F32

time: 120 us -> 120 us (level)
  no operation moved by 1% of the time
where the time goes in v3:
time: 120 us
  starting transfers between devices  61.2 us (51%)
  Pallas kernels  28.9 us (24%)
  waiting for transfers between devices  28.1 us (23%)
    ppermute x30, starting transfers between devices, node_swap(): return lax.ppermute(block, 'node', [(i, i ^ step) for i in range(count)])  34.5 us
    pallas_call x14, Pallas kernels, whole(): pl.pallas_call(kernel, out_shape=out_shape, in_specs=[vmem for _ in opera...  22.4 us
    ppermute x30, waiting for transfers between devices, node_swap(): return lax.ppermute(block, 'node', [(i, i ^ step) for i in range(count)])  20.9 us
    ppermute x12, starting transfers between devices, chip_sum(): lax.ppermute(block, 'rows', route)  20.8 us
    pallas_call x2, Pallas kernels, from_hbm(): pl.pallas_call(kernel, in_specs=[pl.BlockSpec(memory_space=kind) for kind...  4.87 us
    ppermute x12, waiting for transfers between devices, chip_sum(): lax.ppermute(block, 'rows', route)  4.46 us
    ppermute x2, starting transfers between devices, next_head(): return lax.ppermute(head, 'rows', [(i + 1, i) for i in range(count - 1)])  2.78 us
    ppermute x6, waiting for transfers between devices, core_swap(): return lax.ppermute(block, 'rows', [(i, i ^ 1) for i in range(count)])  2.51 us
  transfers between devices with their start and end apart: 52, of which 22 were waited for; matrix products, arithmetic and copies ran while one was open for 0% of the time, Pallas kernels for 18%

profile of v3, /device:TPU:0, one launch (start us, length us, event | category | flops | bytes accessed | tf_op | source)
XLA Modules:
  0.0 119.8 jit_solution(1351323961629077011)
XLA Ops:
  0.6 2.2 %shard_map.68 = (bf16[128,512]{1,0:T(8,128)(2,1)S(1)}, bf16[128,512]{1,0:T(8,128)(2,1)S(1)}, f32[128,128]{1,0:T(8,128)S(1)}, bf16[768,256]{1,0:T(8,128)(2,1)S(1)}) custom-call(bf16[1,2,768,768]{3,2,1,0:T(8,128)(2,1)} %source.3, bf16[768,256]{1,0:T(8,128)(2,1)} %vectors_at.1, f32[768,128]{1,0:T(8,128)} %upper_tiles.3), custom_call_target="tpu_custom_call" | custom-call | flops 100000000 | bytes 1000000 | tf_op jit(solution)/shard_map/pallas_call | solution.py:174
  4.4 2.7 %shard_map.69 = (f32[768,256]{1,0:T(8,128)S(1)}, bf16[1,2,768,768]{3,2,1,0:T(8,128)(2,1)S(1)}, f32[1,2]{1,0:T(1,128)S(1)}) custom-call(f32[1,2]{1,0:T(1,128)} %weights_at.1, bf16[1,2,768,768]{3,2,1,0:T(8,128)(2,1)} %source.3, bf16[768,256]{1,0:T(8,128)(2,1)S(1)} %get-tuple-element.47.vectors, f32[128,128]{1,0:T(8,128)S(1)} %get-tuple-element.48.coupling, ...), custom_call_target="tpu_custom_call" | custom-call | flops 100000000 | bytes 1000000 | tf_op jit(solution)/shard_map/pallas_call | solution.py:174
  8.0 2.9 %collective-permute-start.2 = (bf16[192,256]{1,0:T(8,128)(2,1)S(1)}, bf16[192,256]{1,0:T(8,128)(2,1)S(1)}, u32[]{:S(2)}, u32[]{:S(2)}) collective-permute-start(bf16[192,256]{1,0:T(8,128)(2,1)S(1)} %get-tuple-element.55), channel_id=1, source_target_pairs={{0,8},{8,0},{16,24},{24,16},{1,9},{9,1},{17,25},{25,17},{2,10},{10... | collective-permute-start | bytes 294920 | tf_op jit(solution)/shard_map/ppermute | solution.py:95
  10.9 1.5 %collective-permute-start.3 = (bf16[192,256]{1,0:T(8,128)(2,1)S(1)}, bf16[192,256]{1,0:T(8,128)(2,1)S(1)}, u32[]{:S(2)}, u32[]{:S(2)}) collective-permute-start(bf16[192,256]{1,0:T(8,128)(2,1)S(1)} %get-tuple-element.56), channel_id=1, source_target_pairs={{0,16},{8,24},{16,0},{24,8},{1,17},{9,25},{17,1},{25,9},{2,18},{10... | collective-permute-start | bytes 294920 | tf_op jit(solution)/shard_map/ppermute | solution.py:95
  12.4 1.1 collective-permute-done.2
  13.5 2.0 %collective-permute-done.3 = bf16[192,256]{1,0:T(8,128)(2,1)S(1)} collective-permute-done((bf16[192,256]{1,0:T(8,128)(2,1)S(1)}, bf16[192,256]{1,0:T(8,128)(2,1)S(1)}, u32[]{:S(2)}, u32[]{:S(2)}) %collective-permute-start.3) | collective-permute-done | bytes 98336 | tf_op jit(solution)/shard_map/ppermute | solution.py:95
  15.5 2.5 %collective-permute-done.4 = bf16[192,256]{1,0:T(8,128)(2,1)S(1)} collective-permute-done((bf16[192,256]{1,0:T(8,128)(2,1)S(1)}, bf16[192,256]{1,0:T(8,128)(2,1)S(1)}, u32[]{:S(2)}, u32[]{:S(2)}) %collective-permute-start.4) | collective-permute-done | bytes 98336 | tf_op jit(solution)/shard_map/ppermute | solution.py:95
  18.9 2.2 %collective-permute-start.6 = (bf16[192,256]{1,0:T(8,128)(2,1)S(1)}, bf16[192,256]{1,0:T(8,128)(2,1)S(1)}, u32[]{:S(2)}, u32[]{:S(2)}) collective-permute-start(bf16[192,256]{1,0:T(8,128)(2,1)S(1)} %get-tuple-element.63.refs_0_), channel_id=1, source_target_pairs={{0,16},{8,24},{16,0},{24,8},{1,17},{9,25},{17,1},{25,9},{2,18},{10... | collective-permute-start | bytes 294920 | tf_op jit(solution)/shard_map/ppermute | solution.py:95
  21.6 1.5 %collective-permute-start.8 = (bf16[192,256]{1,0:T(8,128)(2,1)S(1)}, bf16[192,256]{1,0:T(8,128)(2,1)S(1)}, u32[]{:S(2)}, u32[]{:S(2)}) collective-permute-start(bf16[192,256]{1,0:T(8,128)(2,1)S(1)} %get-tuple-element.60), channel_id=1, source_target_pairs={{0,8},{8,0},{16,24},{24,16},{1,9},{9,1},{17,25},{25,17},{2,10},{10... | collective-permute-start | bytes 294920 | tf_op jit(solution)/shard_map/ppermute | solution.py:95
  23.1 1.6 %collective-permute-done.7.refs_3_ = bf16[192,256]{1,0:T(8,128)(2,1)S(1)} collective-permute-done((bf16[192,256]{1,0:T(8,128)(2,1)S(1)}, bf16[192,256]{1,0:T(8,128)(2,1)S(1)}, u32[]{:S(2)}, u32[]{:S(2)}) %collective-permute-start.7) | collective-permute-done | bytes 98336 | tf_op jit(solution)/shard_map/ppermute | solution.py:95
  25.2 1.6 %collective-permute-done.6.refs_2_ = bf16[192,256]{1,0:T(8,128)(2,1)S(1)} collective-permute-done((bf16[192,256]{1,0:T(8,128)(2,1)S(1)}, bf16[192,256]{1,0:T(8,128)(2,1)S(1)}, u32[]{:S(2)}, u32[]{:S(2)}) %collective-permute-start.6) | collective-permute-done | bytes 98336 | tf_op jit(solution)/shard_map/ppermute | solution.py:95
  27.3 1.2 %collective-permute-done.14 = f32[64,256]{1,0:T(8,128)S(1)} collective-permute-done((f32[64,256]{1,0:T(8,128)S(1)}, f32[64,256]{1,0:T(8,128)S(1)}, u32[]{:S(2)}, u32[]{:S(2)}) %collective-permute-start.14) | collective-permute-done | bytes 65568 | tf_op jit(solution)/shard_map/ppermute | solution.py:100
  28.5 4.4 %collective-permute-start.17 = (f32[64,256]{1,0:T(8,128)S(1)}, f32[64,256]{1,0:T(8,128)S(1)}, u32[]{:S(2)}, u32[]{:S(2)}) collective-permute-start(f32[64,256]{1,0:T(8,128)S(1)} %add.81), channel_id=1, source_target_pairs={{0,6},{1,7},{2,4},{3,5},{4,2},{5,3},{6,0},{7,1},{8,14},{9,15},{10,... | collective-permute-start | bytes 196616 | tf_op jit(solution)/shard_map/ppermute | solution.py:126
  34.0 2.0 %collective-permute-start.13 = (bf16[192,256]{1,0:T(8,128)(2,1)S(1)}, bf16[192,256]{1,0:T(8,128)(2,1)S(1)}, u32[]{:S(2)}, u32[]{:S(2)}) collective-permute-start(bf16[192,256]{1,0:T(8,128)(2,1)S(1)} %subtract_convert_fusion.1.refs_0_), channel_id=1, source_target_pairs={{0,24},{8,16},{16,8},{24,0},{1,25},{9,17},{17,9},{25,1},{2,26},{10... | collective-permute-start | bytes 294920 | tf_op jit(solution)/shard_map/ppermute | solution.py:95
  36.5 1.1 collective-permute-start.11
  37.6 2.0 %collective-permute-done.16 = f32[64,256]{1,0:T(8,128)S(1)} collective-permute-done((f32[64,256]{1,0:T(8,128)S(1)}, f32[64,256]{1,0:T(8,128)S(1)}, u32[]{:S(2)}, u32[]{:S(2)}) %collective-permute-start.16) | collective-permute-done | bytes 65568 | tf_op jit(solution)/shard_map/ppermute | solution.py:126
  39.5 2.1 %collective-permute-start.20 = (f32[64,256]{1,0:T(8,128)S(1)}, f32[64,256]{1,0:T(8,128)S(1)}, u32[]{:S(2)}, u32[]{:S(2)}) collective-permute-start(f32[64,256]{1,0:T(8,128)S(1)} %add_add_fusion.5.refs_0_), channel_id=1, source_target_pairs={{0,24},{8,16},{16,8},{24,0},{1,25},{9,17},{17,9},{25,1},{2,26},{10... | collective-permute-start | bytes 196616 | tf_op jit(solution)/shard_map/ppermute | solution.py:95
  46.7 3.9 %shard_map.73 = (f32[128,128]{1,0:T(8,128)S(1)}, f32[128,128]{1,0:T(8,128)S(1)}, f32[128,128]{1,0:T(8,128)S(1)}, f32[1,256]{1,0:T(1,128)S(1)}) custom-call(f32[64,256]{1,0:T(8,128)S(1)} %add_add_fusion.5.refs_0_, f32[64,256]{1,0:T(8,128)S(1)} %collective-permute-done.18.refs_1_, f32[64,256]{1,0:T(8,128)S(1)} %collective-permute-done.19.refs_2_, ...), custom_call_target="tpu_custom_call" | custom-call | flops 6000000000 | bytes 262144 | tf_op jit(solution)/shard_map/pallas_call | solution.py:82
  50.5 3.4 %shard_map.74.factor.refs_4_ = f32[256,256]{1,0:T(8,128)S(1)} custom-call(f32[128,128]{1,0:T(8,128)S(1)} %get-tuple-element.65.top, f32[128,128]{1,0:T(8,128)S(1)} %get-tuple-element.66.corner, f32[128,128]{1,0:T(8,128)S(1)} %get-tuple-element.67.rest, f32[1,256]{1,0:T(1,128)S(1)} %get-tuple-element.68.across), custom_call_target="tpu_custom_call" | custom-call | flops 6000000000 | bytes 197632 | tf_op jit(solution)/shard_map/pallas_call | solution.py:82
  54.0 2.8 %shard_map.76 = (f32[192,256]{1,0:T(8,128)S(1)}, bf16[192,256]{1,0:T(8,128)(2,1)S(1)}, bf16[192,256]{1,0:T(8,128)(2,1)S(1)}, bf16[192,256]{1,0:T(8,128)(2,1)S(1)}) custom-call(f32[1,2]{1,0:T(1,128)S(1)} %get-tuple-element.50.weights, bf16[768,256]{1,0:T(8,128)(2,1)S(1)} %get-tuple-element.58.field, bf16[768,256]{1,0:T(8,128)(2,1)S(1)} %shard_map.72.low, ...), custom_call_target="tpu_custom_call" | custom-call | flops 100000000 | bytes 3997704 | tf_op jit(solution)/shard_map/pallas_call | solution.py:82
  57.6 1.2 %collective-permute-start.24 = (bf16[192,256]{1,0:T(8,128)(2,1)S(1)}, bf16[192,256]{1,0:T(8,128)(2,1)S(1)}, u32[]{:S(2)}, u32[]{:S(2)}) collective-permute-start(bf16[192,256]{1,0:T(8,128)(2,1)S(1)} %get-tuple-element.73), channel_id=1, source_target_pairs={{0,16},{8,24},{16,0},{24,8},{1,17},{9,25},{17,1},{25,9},{2,18},{10... | collective-permute-start | bytes 294920 | tf_op jit(solution)/shard_map/ppermute | solution.py:95
  58.8 1.6 %collective-permute-start.25 = (bf16[192,256]{1,0:T(8,128)(2,1)S(1)}, bf16[192,256]{1,0:T(8,128)(2,1)S(1)}, u32[]{:S(2)}, u32[]{:S(2)}) collective-permute-start(bf16[192,256]{1,0:T(8,128)(2,1)S(1)} %get-tuple-element.74), channel_id=1, source_target_pairs={{0,24},{8,16},{16,8},{24,0},{1,25},{9,17},{17,9},{25,1},{2,26},{10... | collective-permute-start | bytes 294920 | tf_op jit(solution)/shard_map/ppermute | solution.py:95
  60.4 1.3 %collective-permute-start.39 = (bf16[128,256]{1,0:T(8,128)(2,1)S(1)}, bf16[128,256]{1,0:T(8,128)(2,1)S(1)}, u32[]{:S(2)}, u32[]{:S(2)}) collective-permute-start(bf16[128,256]{1,0:T(8,128)(2,1)S(1)} %get-tuple-element.84), channel_id=1, source_target_pairs={{1,0},{2,1},{3,2},{4,3},{5,4},{6,5},{7,6},{9,8},{10,9},{11,10},{12... | collective-permute-start | bytes 196616 | tf_op jit(solution)/shard_map/ppermute | solution.py:522
  63.2 1.9 %collective-permute-done.25 = bf16[192,256]{1,0:T(8,128)(2,1)S(1)} collective-permute-done((bf16[192,256]{1,0:T(8,128)(2,1)S(1)}, bf16[192,256]{1,0:T(8,128)(2,1)S(1)}, u32[]{:S(2)}, u32[]{:S(2)}) %collective-permute-start.25) | collective-permute-done | bytes 98336 | tf_op jit(solution)/shard_map/ppermute | solution.py:95
  65.2 1.9 %collective-permute-start.28 = (bf16[192,256]{1,0:T(8,128)(2,1)S(1)}, bf16[192,256]{1,0:T(8,128)(2,1)S(1)}, u32[]{:S(2)}, u32[]{:S(2)}) collective-permute-start(bf16[192,256]{1,0:T(8,128)(2,1)S(1)} %get-tuple-element.77.refs_0_), channel_id=1, source_target_pairs={{0,24},{8,16},{16,8},{24,0},{1,25},{9,17},{17,9},{25,1},{2,26},{10... | collective-permute-start | bytes 294920 | tf_op jit(solution)/shard_map/ppermute | solution.py:95
  68.7 1.9 %collective-permute-start.31 = (bf16[192,256]{1,0:T(8,128)(2,1)S(1)}, bf16[192,256]{1,0:T(8,128)(2,1)S(1)}, u32[]{:S(2)}, u32[]{:S(2)}) collective-permute-start(bf16[192,256]{1,0:T(8,128)(2,1)S(1)} %subtract_convert_fusion.refs_0_), channel_id=1, source_target_pairs={{0,24},{8,16},{16,8},{24,0},{1,25},{9,17},{17,9},{25,1},{2,26},{10... | collective-permute-start | bytes 294920 | tf_op jit(solution)/shard_map/ppermute | solution.py:95
  70.7 0.9 collective-permute-done.28.refs_3_
  71.6 2.5 %collective-permute-done.27.refs_2_ = bf16[192,256]{1,0:T(8,128)(2,1)S(1)} collective-permute-done((bf16[192,256]{1,0:T(8,128)(2,1)S(1)}, bf16[192,256]{1,0:T(8,128)(2,1)S(1)}, u32[]{:S(2)}, u32[]{:S(2)}) %collective-permute-start.27) | collective-permute-done | bytes 98336 | tf_op jit(solution)/shard_map/ppermute | solution.py:95
  76.6 1.0 collective-permute-start.29
  77.6 2.8 %collective-permute-start.35 = (f32[64,256]{1,0:T(8,128)S(1)}, f32[64,256]{1,0:T(8,128)S(1)}, u32[]{:S(2)}, u32[]{:S(2)}) collective-permute-start(f32[64,256]{1,0:T(8,128)S(1)} %add.88), channel_id=1, source_target_pairs={{0,6},{1,7},{2,4},{3,5},{4,2},{5,3},{6,0},{7,1},{8,14},{9,15},{10,... | collective-permute-start | bytes 196616 | tf_op jit(solution)/shard_map/ppermute | solution.py:126
  80.4 1.4 %collective-permute-start.34 = (f32[64,256]{1,0:T(8,128)S(1)}, f32[64,256]{1,0:T(8,128)S(1)}, u32[]{:S(2)}, u32[]{:S(2)}) collective-permute-start(f32[64,256]{1,0:T(8,128)S(1)} %add.88), channel_id=1, source_target_pairs={{0,4},{1,5},{2,6},{3,7},{4,0},{5,1},{6,2},{7,3},{8,12},{9,13},{10,... | collective-permute-start | bytes 196616 | tf_op jit(solution)/shard_map/ppermute | solution.py:126
  82.1 2.8 %collective-permute-start.43 = (f32[64,256]{1,0:T(8,128)S(1)}, f32[64,256]{1,0:T(8,128)S(1)}, u32[]{:S(2)}, u32[]{:S(2)}) collective-permute-start(f32[64,256]{1,0:T(8,128)S(1)} %add.92), channel_id=1, source_target_pairs={{0,6},{1,7},{2,4},{3,5},{4,2},{5,3},{6,0},{7,1},{8,14},{9,15},{10,... | collective-permute-start | bytes 196616 | tf_op jit(solution)/shard_map/ppermute | solution.py:126
  85.4 3.2 %collective-permute-start.41 = (f32[64,256]{1,0:T(8,128)S(1)}, f32[64,256]{1,0:T(8,128)S(1)}, u32[]{:S(2)}, u32[]{:S(2)}) collective-permute-start(f32[64,256]{1,0:T(8,128)S(1)} %add.92), channel_id=1, source_target_pairs={{0,2},{1,3},{2,0},{3,1},{4,6},{5,7},{6,4},{7,5},{8,10},{9,11},{10,... | collective-permute-start | bytes 196616 | tf_op jit(solution)/shard_map/ppermute | solution.py:126
  88.7 2.2 %collective-permute-done.34 = f32[64,256]{1,0:T(8,128)S(1)} collective-permute-done((f32[64,256]{1,0:T(8,128)S(1)}, f32[64,256]{1,0:T(8,128)S(1)}, u32[]{:S(2)}, u32[]{:S(2)}) %collective-permute-start.34) | collective-permute-done | bytes 65568 | tf_op jit(solution)/shard_map/ppermute | solution.py:126
  90.8 1.5 %collective-permute-start.44 = (bf16[128,256]{1,0:T(8,128)(2,1)S(1)}, bf16[128,256]{1,0:T(8,128)(2,1)S(1)}, u32[]{:S(2)}, u32[]{:S(2)}) collective-permute-start(bf16[128,256]{1,0:T(8,128)(2,1)S(1)} %get-tuple-element.88), channel_id=1, source_target_pairs={{1,0},{2,1},{3,2},{4,3},{5,4},{6,5},{7,6},{9,8},{10,9},{11,10},{12... | collective-permute-start | bytes 196616 | tf_op jit(solution)/shard_map/ppermute | solution.py:522
  92.4 1.3 %collective-permute-start.38 = (f32[64,256]{1,0:T(8,128)S(1)}, f32[64,256]{1,0:T(8,128)S(1)}, u32[]{:S(2)}, u32[]{:S(2)}) collective-permute-start(f32[64,256]{1,0:T(8,128)S(1)} %add_add_fusion.4.refs_0_), channel_id=1, source_target_pairs={{0,24},{8,16},{16,8},{24,0},{1,25},{9,17},{17,9},{25,1},{2,26},{10... | collective-permute-start | bytes 196616 | tf_op jit(solution)/shard_map/ppermute | solution.py:95
  95.6 1.4 %collective-permute-start.36 = (f32[64,256]{1,0:T(8,128)S(1)}, f32[64,256]{1,0:T(8,128)S(1)}, u32[]{:S(2)}, u32[]{:S(2)}) collective-permute-start(f32[64,256]{1,0:T(8,128)S(1)} %add_add_fusion.4.refs_0_), channel_id=1, source_target_pairs={{0,8},{8,0},{16,24},{24,16},{1,9},{9,1},{17,25},{25,17},{2,10},{10... | collective-permute-start | bytes 196616 | tf_op jit(solution)/shard_map/ppermute | solution.py:95
  97.3 0.9 collective-permute-done.45
  98.2 1.5 %collective-permute-done.37.refs_2_ = f32[64,256]{1,0:T(8,128)S(1)} collective-permute-done((f32[64,256]{1,0:T(8,128)S(1)}, f32[64,256]{1,0:T(8,128)S(1)}, u32[]{:S(2)}, u32[]{:S(2)}) %collective-permute-start.37) | collective-permute-done | bytes 65568 | tf_op jit(solution)/shard_map/ppermute | solution.py:95
  100.5 2.1 %collective-permute-start.48 = (f32[64,256]{1,0:T(8,128)S(1)}, f32[64,256]{1,0:T(8,128)S(1)}, u32[]{:S(2)}, u32[]{:S(2)}) collective-permute-start(f32[64,256]{1,0:T(8,128)S(1)} %add.96), channel_id=1, source_target_pairs={{0,6},{1,7},{2,4},{3,5},{4,2},{5,3},{6,0},{7,1},{8,14},{9,15},{10,... | collective-permute-start | bytes 196616 | tf_op jit(solution)/shard_map/ppermute | solution.py:126
  102.6 2.2 %collective-permute-start.46 = (f32[64,256]{1,0:T(8,128)S(1)}, f32[64,256]{1,0:T(8,128)S(1)}, u32[]{:S(2)}, u32[]{:S(2)}) collective-permute-start(f32[64,256]{1,0:T(8,128)S(1)} %add.96), channel_id=1, source_target_pairs={{0,2},{1,3},{2,0},{3,1},{4,6},{5,7},{6,4},{7,5},{8,10},{9,11},{10,... | collective-permute-start | bytes 196616 | tf_op jit(solution)/shard_map/ppermute | solution.py:126
  104.9 3.9 %shard_map.79 = (f32[128,128]{1,0:T(8,128)S(1)}, f32[128,128]{1,0:T(8,128)S(1)}, f32[128,128]{1,0:T(8,128)S(1)}, f32[1,256]{1,0:T(1,128)S(1)}) custom-call(f32[64,256]{1,0:T(8,128)S(1)} %add_add_fusion.4.refs_0_, f32[64,256]{1,0:T(8,128)S(1)} %collective-permute-done.36.refs_1_, f32[64,256]{1,0:T(8,128)S(1)} %collective-permute-done.37.refs_2_, ...), custom_call_target="tpu_custom_call" | custom-call | flops 6000000000 | bytes 262144 | tf_op jit(solution)/shard_map/pallas_call | solution.py:82
  109.1 1.2 %collective-permute-start.51 = (f32[128,256]{1,0:T(8,128)S(1)}, f32[128,256]{1,0:T(8,128)S(1)}, u32[]{:S(2)}, u32[]{:S(2)}) collective-permute-start(f32[128,256]{1,0:T(8,128)S(1)} %pad_maximum_fusion.refs_0_), channel_id=1, source_target_pairs={{0,24},{8,16},{16,8},{24,0},{1,25},{9,17},{17,9},{25,1},{2,26},{10... | collective-permute-start | bytes 393224 | tf_op jit(solution)/shard_map/ppermute | solution.py:95
  110.3 1.1 collective-permute-start.50
  111.4 1.2 %collective-permute-start.49 = (f32[128,256]{1,0:T(8,128)S(1)}, f32[128,256]{1,0:T(8,128)S(1)}, u32[]{:S(2)}, u32[]{:S(2)}) collective-permute-start(f32[128,256]{1,0:T(8,128)S(1)} %pad_maximum_fusion.refs_0_), channel_id=1, source_target_pairs={{0,8},{8,0},{16,24},{24,16},{1,9},{9,1},{17,25},{25,17},{2,10},{10... | collective-permute-start | bytes 393224 | tf_op jit(solution)/shard_map/ppermute | solution.py:95
  112.6 3.4 %shard_map.80.factor.refs_5_ = f32[256,256]{1,0:T(8,128)S(1)} custom-call(f32[128,128]{1,0:T(8,128)S(1)} %get-tuple-element.79.top, f32[128,128]{1,0:T(8,128)S(1)} %get-tuple-element.80.corner, f32[128,128]{1,0:T(8,128)S(1)} %get-tuple-element.81.rest, f32[1,256]{1,0:T(1,128)S(1)} %get-tuple-element.82.across), custom_call_target="tpu_custom_call" | custom-call | flops 6000000000 | bytes 197632 | tf_op jit(solution)/shard_map/pallas_call | solution.py:82
  116.6 1.3 %collective-permute-done.50.refs_2_ = f32[128,256]{1,0:T(8,128)S(1)} collective-permute-done((f32[128,256]{1,0:T(8,128)S(1)}, f32[128,256]{1,0:T(8,128)S(1)}, u32[]{:S(2)}, u32[]{:S(2)}) %collective-permute-start.50) | collective-permute-done | bytes 131104 | tf_op jit(solution)/shard_map/ppermute | solution.py:95
  117.9 1.7 %finish.1 = (f32[768,256]{1,0:T(8,128)}, f32[2,256,256]{2,1,0:T(8,128)}) custom-call(f32[768,256]{1,0:T(8,128)S(1)} %shard_map.81.vectors, f32[128,256]{1,0:T(8,128)S(1)} %pad_maximum_fusion.refs_0_, f32[128,256]{1,0:T(8,128)S(1)} %collective-permute-done.49.refs_1_, f32[128,256]{1,0:T(8,128)S(1)} %collective-permute-done.50.refs_2_, ...), custom_call_target="tpu_custom_call" | custom-call | flops 1000000000 | bytes 1000000 | tf_op jit(solution)/shard_map/finish/pallas_call | solution.py:598
  (90 shorter events, 22.6 us)
Async XLA Ops:
  3.4 3.7 %collective-permute-start.1 = (bf16[128,512]{1,0:T(8,128)(2,1)S(1)}, bf16[128,512]{1,0:T(8,128)(2,1)S(1)}, u32[]{:S(2)}, u32[]{:S(2)}) collective-permute-start(bf16[128,512]{1,0:T(8,128)(2,1)S(1)} %get-tuple-element.52), channel_id=1, source_target_pairs={{1,2},{3,4},{5,6},{2,1},{4,3},{6,5},{9,10},{11,12},{13,14},{10,9},... | collective-permute-start | bytes 393224 | tf_op jit(solution)/shard_map/ppermute | solution.py:106
  8.0 5.5 %collective-permute-start.2 = (bf16[192,256]{1,0:T(8,128)(2,1)S(1)}, bf16[192,256]{1,0:T(8,128)(2,1)S(1)}, u32[]{:S(2)}, u32[]{:S(2)}) collective-permute-start(bf16[192,256]{1,0:T(8,128)(2,1)S(1)} %get-tuple-element.55), channel_id=1, source_target_pairs={{0,8},{8,0},{16,24},{24,16},{1,9},{9,1},{17,25},{25,17},{2,10},{10... | collective-permute-start | bytes 294920 | tf_op jit(solution)/shard_map/ppermute | solution.py:95
  10.9 4.6 %collective-permute-start.3 = (bf16[192,256]{1,0:T(8,128)(2,1)S(1)}, bf16[192,256]{1,0:T(8,128)(2,1)S(1)}, u32[]{:S(2)}, u32[]{:S(2)}) collective-permute-start(bf16[192,256]{1,0:T(8,128)(2,1)S(1)} %get-tuple-element.56), channel_id=1, source_target_pairs={{0,16},{8,24},{16,0},{24,8},{1,17},{9,25},{17,1},{25,9},{2,18},{10... | collective-permute-start | bytes 294920 | tf_op jit(solution)/shard_map/ppermute | solution.py:95
  12.4 5.6 %collective-permute-start.4 = (bf16[192,256]{1,0:T(8,128)(2,1)S(1)}, bf16[192,256]{1,0:T(8,128)(2,1)S(1)}, u32[]{:S(2)}, u32[]{:S(2)}) collective-permute-start(bf16[192,256]{1,0:T(8,128)(2,1)S(1)} %get-tuple-element.57), channel_id=1, source_target_pairs={{0,24},{8,16},{16,8},{24,0},{1,25},{9,17},{17,9},{25,1},{2,26},{10... | collective-permute-start | bytes 294920 | tf_op jit(solution)/shard_map/ppermute | solution.py:95
  18.1 6.7 %collective-permute-start.7 = (bf16[192,256]{1,0:T(8,128)(2,1)S(1)}, bf16[192,256]{1,0:T(8,128)(2,1)S(1)}, u32[]{:S(2)}, u32[]{:S(2)}) collective-permute-start(bf16[192,256]{1,0:T(8,128)(2,1)S(1)} %get-tuple-element.63.refs_0_), channel_id=1, source_target_pairs={{0,24},{8,16},{16,8},{24,0},{1,25},{9,17},{17,9},{25,1},{2,26},{10... | collective-permute-start | bytes 294920 | tf_op jit(solution)/shard_map/ppermute | solution.py:95
  18.9 7.9 %collective-permute-start.6 = (bf16[192,256]{1,0:T(8,128)(2,1)S(1)}, bf16[192,256]{1,0:T(8,128)(2,1)S(1)}, u32[]{:S(2)}, u32[]{:S(2)}) collective-permute-start(bf16[192,256]{1,0:T(8,128)(2,1)S(1)} %get-tuple-element.63.refs_0_), channel_id=1, source_target_pairs={{0,16},{8,24},{16,0},{24,8},{1,17},{9,25},{17,1},{25,9},{2,18},{10... | collective-permute-start | bytes 294920 | tf_op jit(solution)/shard_map/ppermute | solution.py:95
  21.1 5.7 %collective-permute-start.5 = (bf16[192,256]{1,0:T(8,128)(2,1)S(1)}, bf16[192,256]{1,0:T(8,128)(2,1)S(1)}, u32[]{:S(2)}, u32[]{:S(2)}) collective-permute-start(bf16[192,256]{1,0:T(8,128)(2,1)S(1)} %get-tuple-element.63.refs_0_), channel_id=1, source_target_pairs={{0,8},{8,0},{16,24},{24,16},{1,9},{9,1},{17,25},{25,17},{2,10},{10... | collective-permute-start | bytes 294920 | tf_op jit(solution)/shard_map/ppermute | solution.py:95
  21.6 12.2 %collective-permute-start.8 = (bf16[192,256]{1,0:T(8,128)(2,1)S(1)}, bf16[192,256]{1,0:T(8,128)(2,1)S(1)}, u32[]{:S(2)}, u32[]{:S(2)}) collective-permute-start(bf16[192,256]{1,0:T(8,128)(2,1)S(1)} %get-tuple-element.60), channel_id=1, source_target_pairs={{0,8},{8,0},{16,24},{24,16},{1,9},{9,1},{17,25},{25,17},{2,10},{10... | collective-permute-start | bytes 294920 | tf_op jit(solution)/shard_map/ppermute | solution.py:95
  23.1 10.8 %collective-permute-start.9 = (bf16[192,256]{1,0:T(8,128)(2,1)S(1)}, bf16[192,256]{1,0:T(8,128)(2,1)S(1)}, u32[]{:S(2)}, u32[]{:S(2)}) collective-permute-start(bf16[192,256]{1,0:T(8,128)(2,1)S(1)} %get-tuple-element.61), channel_id=1, source_target_pairs={{0,16},{8,24},{16,0},{24,8},{1,17},{9,25},{17,1},{25,9},{2,18},{10... | collective-permute-start | bytes 294920 | tf_op jit(solution)/shard_map/ppermute | solution.py:95
  24.8 9.2 %collective-permute-start.10 = (bf16[192,256]{1,0:T(8,128)(2,1)S(1)}, bf16[192,256]{1,0:T(8,128)(2,1)S(1)}, u32[]{:S(2)}, u32[]{:S(2)}) collective-permute-start(bf16[192,256]{1,0:T(8,128)(2,1)S(1)} %get-tuple-element.62), channel_id=1, source_target_pairs={{0,24},{8,16},{16,8},{24,0},{1,25},{9,17},{17,9},{25,1},{2,26},{10... | collective-permute-start | bytes 294920 | tf_op jit(solution)/shard_map/ppermute | solution.py:95
  28.5 8.0 %collective-permute-start.17 = (f32[64,256]{1,0:T(8,128)S(1)}, f32[64,256]{1,0:T(8,128)S(1)}, u32[]{:S(2)}, u32[]{:S(2)}) collective-permute-start(f32[64,256]{1,0:T(8,128)S(1)} %add.81), channel_id=1, source_target_pairs={{0,6},{1,7},{2,4},{3,5},{4,2},{5,3},{6,0},{7,1},{8,14},{9,15},{10,... | collective-permute-start | bytes 196616 | tf_op jit(solution)/shard_map/ppermute | solution.py:126
  32.9 6.6 %collective-permute-start.16 = (f32[64,256]{1,0:T(8,128)S(1)}, f32[64,256]{1,0:T(8,128)S(1)}, u32[]{:S(2)}, u32[]{:S(2)}) collective-permute-start(f32[64,256]{1,0:T(8,128)S(1)} %add.81), channel_id=1, source_target_pairs={{0,4},{1,5},{2,6},{3,7},{4,0},{5,1},{6,2},{7,3},{8,12},{9,13},{10,... | collective-permute-start | bytes 196616 | tf_op jit(solution)/shard_map/ppermute | solution.py:126
  33.8 5.7 %collective-permute-start.15 = (f32[64,256]{1,0:T(8,128)S(1)}, f32[64,256]{1,0:T(8,128)S(1)}, u32[]{:S(2)}, u32[]{:S(2)}) collective-permute-start(f32[64,256]{1,0:T(8,128)S(1)} %add.81), channel_id=1, source_target_pairs={{0,2},{1,3},{2,0},{3,1},{4,6},{5,7},{6,4},{7,5},{8,10},{9,11},{10,... | collective-permute-start | bytes 196616 | tf_op jit(solution)/shard_map/ppermute | solution.py:126
  34.0 8.4 %collective-permute-start.13 = (bf16[192,256]{1,0:T(8,128)(2,1)S(1)}, bf16[192,256]{1,0:T(8,128)(2,1)S(1)}, u32[]{:S(2)}, u32[]{:S(2)}) collective-permute-start(bf16[192,256]{1,0:T(8,128)(2,1)S(1)} %subtract_convert_fusion.1.refs_0_), channel_id=1, source_target_pairs={{0,24},{8,16},{16,8},{24,0},{1,25},{9,17},{17,9},{25,1},{2,26},{10... | collective-permute-start | bytes 294920 | tf_op jit(solution)/shard_map/ppermute | solution.py:95
  36.0 7.1 %collective-permute-start.12 = (bf16[192,256]{1,0:T(8,128)(2,1)S(1)}, bf16[192,256]{1,0:T(8,128)(2,1)S(1)}, u32[]{:S(2)}, u32[]{:S(2)}) collective-permute-start(bf16[192,256]{1,0:T(8,128)(2,1)S(1)} %subtract_convert_fusion.1.refs_0_), channel_id=1, source_target_pairs={{0,16},{8,24},{16,0},{24,8},{1,17},{9,25},{17,1},{25,9},{2,18},{10... | collective-permute-start | bytes 294920 | tf_op jit(solution)/shard_map/ppermute | solution.py:95
  36.5 6.6 %collective-permute-start.11 = (bf16[192,256]{1,0:T(8,128)(2,1)S(1)}, bf16[192,256]{1,0:T(8,128)(2,1)S(1)}, u32[]{:S(2)}, u32[]{:S(2)}) collective-permute-start(bf16[192,256]{1,0:T(8,128)(2,1)S(1)} %subtract_convert_fusion.1.refs_0_), channel_id=1, source_target_pairs={{0,8},{8,0},{16,24},{24,16},{1,9},{9,1},{17,25},{25,17},{2,10},{10... | collective-permute-start | bytes 294920 | tf_op jit(solution)/shard_map/ppermute | solution.py:95
  39.5 5.5 %collective-permute-start.20 = (f32[64,256]{1,0:T(8,128)S(1)}, f32[64,256]{1,0:T(8,128)S(1)}, u32[]{:S(2)}, u32[]{:S(2)}) collective-permute-start(f32[64,256]{1,0:T(8,128)S(1)} %add_add_fusion.5.refs_0_), channel_id=1, source_target_pairs={{0,24},{8,16},{16,8},{24,0},{1,25},{9,17},{17,9},{25,1},{2,26},{10... | collective-permute-start | bytes 196616 | tf_op jit(solution)/shard_map/ppermute | solution.py:95
  41.6 4.3 %collective-permute-start.19 = (f32[64,256]{1,0:T(8,128)S(1)}, f32[64,256]{1,0:T(8,128)S(1)}, u32[]{:S(2)}, u32[]{:S(2)}) collective-permute-start(f32[64,256]{1,0:T(8,128)S(1)} %add_add_fusion.5.refs_0_), channel_id=1, source_target_pairs={{0,16},{8,24},{16,0},{24,8},{1,17},{9,25},{17,1},{25,9},{2,18},{10... | collective-permute-start | bytes 196616 | tf_op jit(solution)/shard_map/ppermute | solution.py:95
  42.4 4.3 %collective-permute-start.18 = (f32[64,256]{1,0:T(8,128)S(1)}, f32[64,256]{1,0:T(8,128)S(1)}, u32[]{:S(2)}, u32[]{:S(2)}) collective-permute-start(f32[64,256]{1,0:T(8,128)S(1)} %add_add_fusion.5.refs_0_), channel_id=1, source_target_pairs={{0,8},{8,0},{16,24},{24,16},{1,9},{9,1},{17,25},{25,17},{2,10},{10... | collective-permute-start | bytes 196616 | tf_op jit(solution)/shard_map/ppermute | solution.py:95
  44.1 9.9 %collective-permute-start.21 = (f32[128,512]{1,0:T(8,128)S(1)}, f32[128,512]{1,0:T(8,128)S(1)}, u32[]{:S(2)}, u32[]{:S(2)}) collective-permute-start(f32[128,512]{1,0:T(8,128)S(1)} %get-tuple-element.69), channel_id=1, source_target_pairs={{0,1},{1,0},{2,3},{3,2},{4,5},{5,4},{6,7},{7,6},{8,9},{9,8},{10,11... | collective-permute-start | bytes 786440 | tf_op jit(solution)/shard_map/ppermute | solution.py:100
  44.2 9.9 %collective-permute-start.22 = (f32[128,512]{1,0:T(8,128)S(1)}, f32[128,512]{1,0:T(8,128)S(1)}, u32[]{:S(2)}, u32[]{:S(2)}) collective-permute-start(f32[128,512]{1,0:T(8,128)S(1)} %get-tuple-element.70), channel_id=1, source_target_pairs={{1,2},{3,4},{5,6},{2,1},{4,3},{6,5},{9,10},{11,12},{13,14},{10,9},... | collective-permute-start | bytes 786440 | tf_op jit(solution)/shard_map/ppermute | solution.py:106
  56.9 5.5 %collective-permute-start.23 = (bf16[192,256]{1,0:T(8,128)(2,1)S(1)}, bf16[192,256]{1,0:T(8,128)(2,1)S(1)}, u32[]{:S(2)}, u32[]{:S(2)}) collective-permute-start(bf16[192,256]{1,0:T(8,128)(2,1)S(1)} %get-tuple-element.72), channel_id=1, source_target_pairs={{0,8},{8,0},{16,24},{24,16},{1,9},{9,1},{17,25},{25,17},{2,10},{10... | collective-permute-start | bytes 294920 | tf_op jit(solution)/shard_map/ppermute | solution.py:95
  57.6 5.6 %collective-permute-start.24 = (bf16[192,256]{1,0:T(8,128)(2,1)S(1)}, bf16[192,256]{1,0:T(8,128)(2,1)S(1)}, u32[]{:S(2)}, u32[]{:S(2)}) collective-permute-start(bf16[192,256]{1,0:T(8,128)(2,1)S(1)} %get-tuple-element.73), channel_id=1, source_target_pairs={{0,16},{8,24},{16,0},{24,8},{1,17},{9,25},{17,1},{25,9},{2,18},{10... | collective-permute-start | bytes 294920 | tf_op jit(solution)/shard_map/ppermute | solution.py:95
  58.8 6.3 %collective-permute-start.25 = (bf16[192,256]{1,0:T(8,128)(2,1)S(1)}, bf16[192,256]{1,0:T(8,128)(2,1)S(1)}, u32[]{:S(2)}, u32[]{:S(2)}) collective-permute-start(bf16[192,256]{1,0:T(8,128)(2,1)S(1)} %get-tuple-element.74), channel_id=1, source_target_pairs={{0,24},{8,16},{16,8},{24,0},{1,25},{9,17},{17,9},{25,1},{2,26},{10... | collective-permute-start | bytes 294920 | tf_op jit(solution)/shard_map/ppermute | solution.py:95
  60.4 10.3 %collective-permute-start.39 = (bf16[128,256]{1,0:T(8,128)(2,1)S(1)}, bf16[128,256]{1,0:T(8,128)(2,1)S(1)}, u32[]{:S(2)}, u32[]{:S(2)}) collective-permute-start(bf16[128,256]{1,0:T(8,128)(2,1)S(1)} %get-tuple-element.84), channel_id=1, source_target_pairs={{1,0},{2,1},{3,2},{4,3},{5,4},{6,5},{7,6},{9,8},{10,9},{11,10},{12... | collective-permute-start | bytes 196616 | tf_op jit(solution)/shard_map/ppermute | solution.py:522
  65.2 6.5 %collective-permute-start.28 = (bf16[192,256]{1,0:T(8,128)(2,1)S(1)}, bf16[192,256]{1,0:T(8,128)(2,1)S(1)}, u32[]{:S(2)}, u32[]{:S(2)}) collective-permute-start(bf16[192,256]{1,0:T(8,128)(2,1)S(1)} %get-tuple-element.77.refs_0_), channel_id=1, source_target_pairs={{0,24},{8,16},{16,8},{24,0},{1,25},{9,17},{17,9},{25,1},{2,26},{10... | collective-permute-start | bytes 294920 | tf_op jit(solution)/shard_map/ppermute | solution.py:95
  67.1 7.0 %collective-permute-start.27 = (bf16[192,256]{1,0:T(8,128)(2,1)S(1)}, bf16[192,256]{1,0:T(8,128)(2,1)S(1)}, u32[]{:S(2)}, u32[]{:S(2)}) collective-permute-start(bf16[192,256]{1,0:T(8,128)(2,1)S(1)} %get-tuple-element.77.refs_0_), channel_id=1, source_target_pairs={{0,16},{8,24},{16,0},{24,8},{1,17},{9,25},{17,1},{25,9},{2,18},{10... | collective-permute-start | bytes 294920 | tf_op jit(solution)/shard_map/ppermute | solution.py:95
  67.8 6.3 %collective-permute-start.26 = (bf16[192,256]{1,0:T(8,128)(2,1)S(1)}, bf16[192,256]{1,0:T(8,128)(2,1)S(1)}, u32[]{:S(2)}, u32[]{:S(2)}) collective-permute-start(bf16[192,256]{1,0:T(8,128)(2,1)S(1)} %get-tuple-element.77.refs_0_), channel_id=1, source_target_pairs={{0,8},{8,0},{16,24},{24,16},{1,9},{9,1},{17,25},{25,17},{2,10},{10... | collective-permute-start | bytes 294920 | tf_op jit(solution)/shard_map/ppermute | solution.py:95
  68.7 13.1 %collective-permute-start.31 = (bf16[192,256]{1,0:T(8,128)(2,1)S(1)}, bf16[192,256]{1,0:T(8,128)(2,1)S(1)}, u32[]{:S(2)}, u32[]{:S(2)}) collective-permute-start(bf16[192,256]{1,0:T(8,128)(2,1)S(1)} %subtract_convert_fusion.refs_0_), channel_id=1, source_target_pairs={{0,24},{8,16},{16,8},{24,0},{1,25},{9,17},{17,9},{25,1},{2,26},{10... | collective-permute-start | bytes 294920 | tf_op jit(solution)/shard_map/ppermute | solution.py:95
  75.5 4.9 %collective-permute-start.40 = (f32[64,256]{1,0:T(8,128)S(1)}, f32[64,256]{1,0:T(8,128)S(1)}, u32[]{:S(2)}, u32[]{:S(2)}) collective-permute-start(f32[64,256]{1,0:T(8,128)S(1)} %shard_map.82), channel_id=1, source_target_pairs={{0,1},{1,0},{2,3},{3,2},{4,5},{5,4},{6,7},{7,6},{8,9},{9,8},{10,11... | collective-permute-start | bytes 196616 | tf_op jit(solution)/shard_map/ppermute | solution.py:100
  76.1 6.0 %collective-permute-start.30 = (bf16[192,256]{1,0:T(8,128)(2,1)S(1)}, bf16[192,256]{1,0:T(8,128)(2,1)S(1)}, u32[]{:S(2)}, u32[]{:S(2)}) collective-permute-start(bf16[192,256]{1,0:T(8,128)(2,1)S(1)} %subtract_convert_fusion.refs_0_), channel_id=1, source_target_pairs={{0,16},{8,24},{16,0},{24,8},{1,17},{9,25},{17,1},{25,9},{2,18},{10... | collective-permute-start | bytes 294920 | tf_op jit(solution)/shard_map/ppermute | solution.py:95
  76.6 8.2 %collective-permute-start.29 = (bf16[192,256]{1,0:T(8,128)(2,1)S(1)}, bf16[192,256]{1,0:T(8,128)(2,1)S(1)}, u32[]{:S(2)}, u32[]{:S(2)}) collective-permute-start(bf16[192,256]{1,0:T(8,128)(2,1)S(1)} %subtract_convert_fusion.refs_0_), channel_id=1, source_target_pairs={{0,8},{8,0},{16,24},{24,16},{1,9},{9,1},{17,25},{25,17},{2,10},{10... | collective-permute-start | bytes 294920 | tf_op jit(solution)/shard_map/ppermute | solution.py:95
  77.6 7.8 %collective-permute-start.35 = (f32[64,256]{1,0:T(8,128)S(1)}, f32[64,256]{1,0:T(8,128)S(1)}, u32[]{:S(2)}, u32[]{:S(2)}) collective-permute-start(f32[64,256]{1,0:T(8,128)S(1)} %add.88), channel_id=1, source_target_pairs={{0,6},{1,7},{2,4},{3,5},{4,2},{5,3},{6,0},{7,1},{8,14},{9,15},{10,... | collective-permute-start | bytes 196616 | tf_op jit(solution)/shard_map/ppermute | solution.py:126
  80.4 10.4 %collective-permute-start.34 = (f32[64,256]{1,0:T(8,128)S(1)}, f32[64,256]{1,0:T(8,128)S(1)}, u32[]{:S(2)}, u32[]{:S(2)}) collective-permute-start(f32[64,256]{1,0:T(8,128)S(1)} %add.88), channel_id=1, source_target_pairs={{0,4},{1,5},{2,6},{3,7},{4,0},{5,1},{6,2},{7,3},{8,12},{9,13},{10,... | collective-permute-start | bytes 196616 | tf_op jit(solution)/shard_map/ppermute | solution.py:126
  81.8 10.5 %collective-permute-start.33 = (f32[64,256]{1,0:T(8,128)S(1)}, f32[64,256]{1,0:T(8,128)S(1)}, u32[]{:S(2)}, u32[]{:S(2)}) collective-permute-start(f32[64,256]{1,0:T(8,128)S(1)} %add.88), channel_id=1, source_target_pairs={{0,2},{1,3},{2,0},{3,1},{4,6},{5,7},{6,4},{7,5},{8,10},{9,11},{10,... | collective-permute-start | bytes 196616 | tf_op jit(solution)/shard_map/ppermute | solution.py:126
  82.1 13.5 %collective-permute-start.43 = (f32[64,256]{1,0:T(8,128)S(1)}, f32[64,256]{1,0:T(8,128)S(1)}, u32[]{:S(2)}, u32[]{:S(2)}) collective-permute-start(f32[64,256]{1,0:T(8,128)S(1)} %add.92), channel_id=1, source_target_pairs={{0,6},{1,7},{2,4},{3,5},{4,2},{5,3},{6,0},{7,1},{8,14},{9,15},{10,... | collective-permute-start | bytes 196616 | tf_op jit(solution)/shard_map/ppermute | solution.py:126
  84.9 12.1 %collective-permute-start.42 = (f32[64,256]{1,0:T(8,128)S(1)}, f32[64,256]{1,0:T(8,128)S(1)}, u32[]{:S(2)}, u32[]{:S(2)}) collective-permute-start(f32[64,256]{1,0:T(8,128)S(1)} %add.92), channel_id=1, source_target_pairs={{0,4},{1,5},{2,6},{3,7},{4,0},{5,1},{6,2},{7,3},{8,12},{9,13},{10,... | collective-permute-start | bytes 196616 | tf_op jit(solution)/shard_map/ppermute | solution.py:126
  85.4 11.8 %collective-permute-start.41 = (f32[64,256]{1,0:T(8,128)S(1)}, f32[64,256]{1,0:T(8,128)S(1)}, u32[]{:S(2)}, u32[]{:S(2)}) collective-permute-start(f32[64,256]{1,0:T(8,128)S(1)} %add.92), channel_id=1, source_target_pairs={{0,2},{1,3},{2,0},{3,1},{4,6},{5,7},{6,4},{7,5},{8,10},{9,11},{10,... | collective-permute-start | bytes 196616 | tf_op jit(solution)/shard_map/ppermute | solution.py:126
  90.8 3.1 %collective-permute-start.44 = (bf16[128,256]{1,0:T(8,128)(2,1)S(1)}, bf16[128,256]{1,0:T(8,128)(2,1)S(1)}, u32[]{:S(2)}, u32[]{:S(2)}) collective-permute-start(bf16[128,256]{1,0:T(8,128)(2,1)S(1)} %get-tuple-element.88), channel_id=1, source_target_pairs={{1,0},{2,1},{3,2},{4,3},{5,4},{6,5},{7,6},{9,8},{10,9},{11,10},{12... | collective-permute-start | bytes 196616 | tf_op jit(solution)/shard_map/ppermute | solution.py:522
  92.4 5.9 %collective-permute-start.38 = (f32[64,256]{1,0:T(8,128)S(1)}, f32[64,256]{1,0:T(8,128)S(1)}, u32[]{:S(2)}, u32[]{:S(2)}) collective-permute-start(f32[64,256]{1,0:T(8,128)S(1)} %add_add_fusion.4.refs_0_), channel_id=1, source_target_pairs={{0,24},{8,16},{16,8},{24,0},{1,25},{9,17},{17,9},{25,1},{2,26},{10... | collective-permute-start | bytes 196616 | tf_op jit(solution)/shard_map/ppermute | solution.py:95
  94.0 5.7 %collective-permute-start.37 = (f32[64,256]{1,0:T(8,128)S(1)}, f32[64,256]{1,0:T(8,128)S(1)}, u32[]{:S(2)}, u32[]{:S(2)}) collective-permute-start(f32[64,256]{1,0:T(8,128)S(1)} %add_add_fusion.4.refs_0_), channel_id=1, source_target_pairs={{0,16},{8,24},{16,0},{24,8},{1,17},{9,25},{17,1},{25,9},{2,18},{10... | collective-permute-start | bytes 196616 | tf_op jit(solution)/shard_map/ppermute | solution.py:95
  95.6 4.9 %collective-permute-start.36 = (f32[64,256]{1,0:T(8,128)S(1)}, f32[64,256]{1,0:T(8,128)S(1)}, u32[]{:S(2)}, u32[]{:S(2)}) collective-permute-start(f32[64,256]{1,0:T(8,128)S(1)} %add_add_fusion.4.refs_0_), channel_id=1, source_target_pairs={{0,8},{8,0},{16,24},{24,16},{1,9},{9,1},{17,25},{25,17},{2,10},{10... | collective-permute-start | bytes 196616 | tf_op jit(solution)/shard_map/ppermute | solution.py:95
  100.5 8.3 %collective-permute-start.48 = (f32[64,256]{1,0:T(8,128)S(1)}, f32[64,256]{1,0:T(8,128)S(1)}, u32[]{:S(2)}, u32[]{:S(2)}) collective-permute-start(f32[64,256]{1,0:T(8,128)S(1)} %add.96), channel_id=1, source_target_pairs={{0,6},{1,7},{2,4},{3,5},{4,2},{5,3},{6,0},{7,1},{8,14},{9,15},{10,... | collective-permute-start | bytes 196616 | tf_op jit(solution)/shard_map/ppermute | solution.py:126
  102.6 6.4 %collective-permute-start.47 = (f32[64,256]{1,0:T(8,128)S(1)}, f32[64,256]{1,0:T(8,128)S(1)}, u32[]{:S(2)}, u32[]{:S(2)}) collective-permute-start(f32[64,256]{1,0:T(8,128)S(1)} %add.96), channel_id=1, source_target_pairs={{0,4},{1,5},{2,6},{3,7},{4,0},{5,1},{6,2},{7,3},{8,12},{9,13},{10,... | collective-permute-start | bytes 196616 | tf_op jit(solution)/shard_map/ppermute | solution.py:126
  102.6 6.4 %collective-permute-start.46 = (f32[64,256]{1,0:T(8,128)S(1)}, f32[64,256]{1,0:T(8,128)S(1)}, u32[]{:S(2)}, u32[]{:S(2)}) collective-permute-start(f32[64,256]{1,0:T(8,128)S(1)} %add.96), channel_id=1, source_target_pairs={{0,2},{1,3},{2,0},{3,1},{4,6},{5,7},{6,4},{7,5},{8,10},{9,11},{10,... | collective-permute-start | bytes 196616 | tf_op jit(solution)/shard_map/ppermute | solution.py:126
  109.1 7.5 %collective-permute-start.51 = (f32[128,256]{1,0:T(8,128)S(1)}, f32[128,256]{1,0:T(8,128)S(1)}, u32[]{:S(2)}, u32[]{:S(2)}) collective-permute-start(f32[128,256]{1,0:T(8,128)S(1)} %pad_maximum_fusion.refs_0_), channel_id=1, source_target_pairs={{0,24},{8,16},{16,8},{24,0},{1,25},{9,17},{17,9},{25,1},{2,26},{10... | collective-permute-start | bytes 393224 | tf_op jit(solution)/shard_map/ppermute | solution.py:95
  110.3 7.6 %collective-permute-start.50 = (f32[128,256]{1,0:T(8,128)S(1)}, f32[128,256]{1,0:T(8,128)S(1)}, u32[]{:S(2)}, u32[]{:S(2)}) collective-permute-start(f32[128,256]{1,0:T(8,128)S(1)} %pad_maximum_fusion.refs_0_), channel_id=1, source_target_pairs={{0,16},{8,24},{16,0},{24,8},{1,17},{9,25},{17,1},{25,9},{2,18},{10... | collective-permute-start | bytes 393224 | tf_op jit(solution)/shard_map/ppermute | solution.py:95
  111.4 6.5 %collective-permute-start.49 = (f32[128,256]{1,0:T(8,128)S(1)}, f32[128,256]{1,0:T(8,128)S(1)}, u32[]{:S(2)}, u32[]{:S(2)}) collective-permute-start(f32[128,256]{1,0:T(8,128)S(1)} %pad_maximum_fusion.refs_0_), channel_id=1, source_target_pairs={{0,8},{8,0},{16,24},{24,16},{1,9},{9,1},{17,25},{25,17},{2,10},{10... | collective-permute-start | bytes 393224 | tf_op jit(solution)/shard_map/ppermute | solution.py:95
  (6 other events, 48.4 us)
